TPU v7x, 512 devices: a whole 4x8x8 slice. The times are simulated.
512 devices in a mesh: dp: 8 (over x, core), expert: 64 (over z, y).
Axes of the slice: x: 4, y: 8, z: 8, core: 2. Of those that a mesh axis runs over, the one named last changes fastest.
Arguments:
- query_reps: bfloat16 [4096, 2048], P('dp'), as said below
- code_reps: bfloat16 [4096, 2048], P('expert'), as said below
- positives: int32 [4096], P('dp'), may hold values from 0 to 4095, as said below
- file_lengths: int32 [64, 8, 8], P('expert', 'dp'), may hold values from 1 to 64, 128 in all within a row
- residual: bfloat16 [64, 1024, 2048], P('expert', 'dp'), may hold values from -6 to 6
- norm_gain: bfloat16 [2048], replicated, may hold values from 0.25 to 1.75
- expert_ids: int32 [64, 1024, 2], P('expert', 'dp'), may hold values from 0 to 63, as said below
- gate_units: int32 [64, 1024, 2], P('expert', 'dp'), may hold values from 16 to 191
- w_gate: bfloat16 [64, 2048, 768], P('expert', 'dp'), may hold values from -0.125 to 0.125
- w_up: bfloat16 [64, 2048, 768], P('expert', 'dp'), may hold values from -0.125 to 0.125
- w_down: bfloat16 [64, 2048, 768], P('expert', 'dp'), may hold values from -0.21875 to 0.21875
Outputs:
- token_grad: bfloat16 [64, 1024, 2048], P('expert', 'dp')
Inputs may be any that keep to these rules, and one draw needn't show every extreme that they name: `positives`: each code is the positive of exactly one query. `query_reps`: entries have magnitude at most 4 / sqrt(2048). `code_reps`: entries have magnitude at most 4 / sqrt(2048). `file_lengths`: the 8 lengths of one shard add up to 128. `expert_ids`: each token names 2 different experts; the tokens of one shard name each expert at most 6 times, and for each index of dp some expert is named exactly 6 times by the tokens of every shard with that index.
All inputs are finite; a program needn't handle non-finite values.
Results may differ from a plain program's by a relative error of at most 0.009.
Values may be sent and summed in bfloat16 or wider, within the bound.
No kernel may reach another device: no remote copies, remote signals or barrier semaphores. Data moves between devices by JAX's collectives and lax.ppermute only.
A program may use at most 64 MiB of HBM per device.

v0:
```python
import jax
import jax.numpy as jnp
from jax import lax
from jax.sharding import PartitionSpec as P

SCORE_SCALE = 20.0
GRAD_SCALE = 2560.0
EPSILON = 1e-06


def joined(value, axis, join):
    pieces = jax.tree.map(lambda part: lax.all_gather(part, axis), value)
    head = jax.tree.map(lambda part: part[0], pieces)
    tail = jax.tree.map(lambda part: part[1:], pieces)
    subtotal, _ = lax.scan(lambda subtotal, slab: (join(subtotal, slab), None), head, tail)
    return subtotal


def softmax_pair(first, second):
    row_top = jnp.maximum(first[0], second[0])
    return (
        row_top,
        first[1] * jnp.exp(first[0] - row_top) + second[1] * jnp.exp(second[0] - row_top),
    )


def expert_backward(normed_rows, cot_rows, gate_rows, weight_gate, weight_up, weight_down):
    gate_pre = jnp.dot(normed_rows, weight_gate, preferred_element_type=jnp.float32)
    up_pre = jnp.dot(normed_rows, weight_up, preferred_element_type=jnp.float32)
    back_hidden = gate_rows[:, None] * jnp.dot(
        cot_rows, weight_down, preferred_element_type=jnp.float32
    )
    sigmoid_gate = jax.nn.sigmoid(gate_pre)
    grad_gate = (
        back_hidden * up_pre * sigmoid_gate * (1.0 + gate_pre * (1.0 - sigmoid_gate))
    ).astype(jnp.bfloat16)
    grad_up = (back_hidden * gate_pre * sigmoid_gate).astype(jnp.bfloat16)
    contract = (((1,), (1,)), ((), ()))
    input_grad = lax.dot_general(
        grad_gate, weight_gate, contract, preferred_element_type=jnp.float32
    )
    input_grad = input_grad + lax.dot_general(
        grad_up, weight_up, contract, preferred_element_type=jnp.float32
    )
    return input_grad.astype(jnp.bfloat16)


def per_device(
    query_reps,
    code_reps,
    positives,
    file_lengths,
    residual,
    norm_gain,
    expert_ids,
    gate_units,
    w_gate,
    w_up,
    w_down,
):
    owners = lax.axis_size("expert")
    columns = code_reps.shape[0]
    file_count = file_lengths.shape[2]
    tokens = residual.shape[1]
    model_width = residual.shape[2]
    pick_count = expert_ids.shape[2]
    capacity = 3 * tokens * pick_count // (2 * owners)
    scores = jnp.dot(query_reps, code_reps.T, preferred_element_type=jnp.float32) * SCORE_SCALE
    local_top = jnp.max(scores, axis=1)
    local_total = jnp.sum(jnp.exp(scores - local_top[:, None]), axis=1)
    row_top, row_total = joined((local_top, local_total), "expert", softmax_pair)
    probabilities = jnp.exp(scores - row_top[:, None]) / row_total[:, None]
    column_ids = lax.axis_index("expert") * columns + jnp.arange(columns, dtype=jnp.int32)
    onehot = (positives[:, None] == column_ids[None, :]).astype(jnp.float32)
    weights = (GRAD_SCALE * (probabilities - onehot)).astype(jnp.bfloat16)
    code_grad = lax.psum_scatter(
        lax.dot_general(
            weights, query_reps, (((0,), (0,)), ((), ())), preferred_element_type=jnp.float32
        ),
        "dp",
        scatter_dimension=0,
        tiled=True,
    )
    lengths = file_lengths[0, 0]
    file_cot = (code_grad / lengths[:, None].astype(jnp.float32)).astype(jnp.bfloat16)
    file_ends = jnp.cumsum(lengths)
    position = jnp.arange(tokens, dtype=jnp.int32)
    segment = jnp.sum((position[:, None] >= file_ends[None, :]).astype(jnp.int32), axis=1)
    member = (segment[:, None] == jnp.arange(file_count, dtype=jnp.int32)[None, :]).astype(
        jnp.bfloat16
    )
    token_cot = jnp.dot(member, file_cot, preferred_element_type=jnp.float32).astype(jnp.bfloat16)
    stream = residual[0].astype(jnp.float32)
    root_inverse = lax.rsqrt(jnp.mean(stream * stream, axis=-1, keepdims=True) + EPSILON)
    norm_scale = norm_gain.astype(jnp.float32)
    normed = (stream * root_inverse * norm_scale).astype(jnp.bfloat16)
    chosen = expert_ids[0].reshape(-1)
    gate_values = gate_units[0].reshape(-1)
    assign_count = chosen.shape[0]
    expert_table = (chosen[:, None] == jnp.arange(owners, dtype=jnp.int32)[None, :]).astype(
        jnp.int32
    )
    earlier = jnp.cumsum(expert_table, axis=0) - expert_table
    slot_rank = jnp.sum(earlier * expert_table, axis=1)
    slot_index = chosen * capacity + slot_rank
    source = (
        jnp.full((owners * capacity,), assign_count, jnp.int32)
        .at[slot_index]
        .set(jnp.arange(assign_count, dtype=jnp.int32))
    )
    filled = source < assign_count
    token_of = jnp.where(filled, source // pick_count, tokens)
    gate_pad = jnp.concatenate(
        [gate_values.astype(jnp.float32) / 256.0, jnp.zeros((1,), jnp.float32)]
    )
    send_gate = gate_pad[source].astype(jnp.bfloat16).reshape(owners, capacity)
    normed_pad = jnp.concatenate([normed, jnp.zeros((1, model_width), jnp.bfloat16)])
    send_rows = normed_pad[token_of].reshape(owners, capacity, model_width)
    gathered = (
        lax.all_gather(w_gate, "dp", axis=1, tiled=True),
        lax.all_gather(w_up, "dp", axis=1, tiled=True),
        lax.all_gather(w_down, "dp", axis=1, tiled=True),
    )
    weight_gate = gathered[0][0]
    weight_up = gathered[1][0]
    weight_down = gathered[2][0]
    cot_pad = jnp.concatenate([token_cot, jnp.zeros((1, model_width), jnp.bfloat16)])
    send_cot = cot_pad[token_of].reshape(owners, capacity, model_width)
    row_block = lax.all_to_all(send_rows, "expert", split_axis=0, concat_axis=0, tiled=True)
    cot_block = lax.all_to_all(send_cot, "expert", split_axis=0, concat_axis=0, tiled=True)
    gate_rows = lax.all_to_all(send_gate, "expert", split_axis=0, concat_axis=0, tiled=True)
    senders = gate_rows.shape[0]
    items = gate_rows.shape[1]
    input_grad = expert_backward(
        row_block.reshape(-1, model_width),
        cot_block.reshape(-1, model_width),
        gate_rows.reshape(-1).astype(jnp.float32),
        weight_gate,
        weight_up,
        weight_down,
    )
    result = input_grad.reshape(senders, items, model_width)
    returned = lax.all_to_all(result, "expert", split_axis=0, concat_axis=0, tiled=True)
    per_pick = returned.reshape(owners * capacity, model_width)[slot_index].astype(jnp.float32)
    normed_grad = jnp.sum(per_pick.reshape(tokens, pick_count, model_width), axis=1)
    scaled = norm_scale * normed_grad
    correction = jnp.mean(scaled * stream, axis=-1, keepdims=True)
    token_grad = (
        token_cot.astype(jnp.float32)
        + root_inverse * scaled
        - stream * root_inverse**3 * correction
    )
    return token_grad.astype(jnp.bfloat16)[None]


def solution(mesh):
    return jax.shard_map(
        per_device,
        mesh=mesh,
        in_specs=(
            P("dp", None),
            P("expert", None),
            P("dp"),
            P("expert", "dp", None),
            P("expert", "dp", None),
            P(),
            P("expert", "dp", None),
            P("expert", "dp", None),
            P("expert", "dp", None),
            P("expert", "dp", None),
            P("expert", "dp", None),
        ),
        out_specs=P("expert", "dp", None),
        check_vma=False,
    )
```

profile of v0, /device:TPU:6, one launch (start us, length us, event | category | flops | bytes accessed | tf_op | source)
XLA Modules:
  0.0 363.9 jit_solution(7015134038822854983)
XLA Ops:
  9.9 56.3 %all-gather.3 = f32[64,1,512]{2,1,0:T(1,128)S(1)} all-gather(f32[1,1,512]{2,1,0:T(1,128)S(1)} %bitcast.89), channel_id=3, replica_groups=mesh['dp'=8,'expert'=64] {'expert'}, dimensions={0}, use_global_device_ids=true | all-gather | bytes 133120 | tf_op jit(solution)/shard_map/all_gather | solution.py:12
  66.2 47.6 %all-gather.2 = f32[64,1,512]{2,1,0:T(1,128)S(1)} all-gather(f32[1,1,512]{2,1,0:T(1,128)S(1)} %bitcast.88), channel_id=2, replica_groups=mesh['dp'=8,'expert'=64] {'expert'}, dimensions={0}, use_global_device_ids=true | all-gather | bytes 133120 | tf_op jit(solution)/shard_map/all_gather | solution.py:12
  113.8 3.4 while.12
  127.1 7.3 %all-to-all-start = ((bf16[64,1,6]{2,1,0:T(2,128)(2,1)}), bf16[64,1,6]{2,1,0:T(2,128)(2,1)S(1)}, u32[]{:S(2)}, u32[]{:S(2)}) async-start(bf16[64,1,6]{2,1,0:T(2,128)(2,1)} %convert_element_type.124), calls=%async_computation.1 | async-start | bytes 65536 | tf_op jit(solution)/shard_map/all_to_all | solution.py:131
  138.0 3.7 %reshape.162 = bf16[64,6,2048]{2,1,0:T(8,128)(2,1)} reshape(bf16[384,2048]{1,0:T(8,128)(2,1)} %gather_fusion.2) | data formatting | bytes 3145728 | tf_op jit(solution)/shard_map/reshape | solution.py:118
  141.7 6.0 %all-to-all-done = bf16[64,1,6]{2,1,0:T(2,128)(2,1)S(1)} async-done(((bf16[64,1,6]{2,1,0:T(2,128)(2,1)}), bf16[64,1,6]{2,1,0:T(2,128)(2,1)S(1)}, u32[]{:S(2)}, u32[]{:S(2)}) %all-to-all-start) | async-done | bytes 800 | tf_op jit(solution)/shard_map/all_to_all | solution.py:131
  147.7 21.6 %all-to-all-start.2 = ((bf16[64,6,2048]{2,1,0:T(8,128)(2,1)}), bf16[64,6,2048]{2,1,0:T(8,128)(2,1)}, u32[]{:S(2)}, u32[]{:S(2)}) async-start(bf16[64,6,2048]{2,1,0:T(8,128)(2,1)} %reshape.162), calls=%async_computation.3 | async-start | bytes 4194304 | tf_op jit(solution)/shard_map/all_to_all | solution.py:129
  172.3 3.1 gather_fusion.1
  175.4 3.7 %reshape.160 = bf16[64,6,2048]{2,1,0:T(8,128)(2,1)} reshape(bf16[384,2048]{1,0:T(8,128)(2,1)} %gather_fusion.1) | data formatting | bytes 3145728 | tf_op jit(solution)/shard_map/reshape | solution.py:128
  179.1 45.1 %all-to-all-done.2 = bf16[64,6,2048]{2,1,0:T(8,128)(2,1)} async-done(((bf16[64,6,2048]{2,1,0:T(8,128)(2,1)}), bf16[64,6,2048]{2,1,0:T(8,128)(2,1)}, u32[]{:S(2)}, u32[]{:S(2)}) %all-to-all-start.2) | async-done | bytes 1572896 | tf_op jit(solution)/shard_map/all_to_all | solution.py:129
  224.2 9.9 %all-to-all-start.1 = ((bf16[64,6,2048]{2,1,0:T(8,128)(2,1)}), bf16[64,6,2048]{2,1,0:T(8,128)(2,1)}, u32[]{:S(2)}, u32[]{:S(2)}) async-start(bf16[64,6,2048]{2,1,0:T(8,128)(2,1)} %reshape.160), calls=%async_computation.2 | async-start | bytes 4194304 | tf_op jit(solution)/shard_map/all_to_all | solution.py:130
  234.3 3.7 %reshape.163 = bf16[384,2048]{1,0:T(8,128)(2,1)} reshape(bf16[64,6,2048]{2,1,0:T(8,128)(2,1)} %all-to-all-done.2) | data formatting | bytes 3145728 | tf_op jit(solution)/shard_map/reshape | solution.py:135
  238.0 27.1 %all-to-all-done.1 = bf16[64,6,2048]{2,1,0:T(8,128)(2,1)} async-done(((bf16[64,6,2048]{2,1,0:T(8,128)(2,1)}), bf16[64,6,2048]{2,1,0:T(8,128)(2,1)}, u32[]{:S(2)}, u32[]{:S(2)}) %all-to-all-start.1) | async-done | bytes 1572896 | tf_op jit(solution)/shard_map/all_to_all | solution.py:130
  265.1 3.7 %reshape.161 = bf16[384,2048]{1,0:T(8,128)(2,1)} reshape(bf16[64,6,2048]{2,1,0:T(8,128)(2,1)} %all-to-all-done.1) | data formatting | bytes 3145728 | tf_op jit(solution)/shard_map/reshape | solution.py:136
  268.9 4.8 %fusion.2 = f32[384,768]{1,0:T(8,128)} fusion(bf16[384,2048]{1,0:T(8,128)(2,1)} %reshape.163, bf16[1,2048,768]{2,1,0:T(8,128)(2,1)} %all-gather.12.cloned.1.call-done), kind=kOutput, calls=%fused_computation.10 | convolution fusion | flops 1207959552 | bytes 5898240 | tf_op jit(solution)/shard_map/dot_general | solution.py:28
  273.7 4.8 %fusion.12 = f32[384,768]{1,0:T(8,128)} fusion(bf16[384,2048]{1,0:T(8,128)(2,1)} %reshape.161, bf16[1,2048,768]{2,1,0:T(8,128)(2,1)} %all-gather.8.cloned.1.call-done, f32[384]{0:T(512)S(1)} %reshape.167), kind=kOutput, calls=%fused_computation.24 | convolution fusion | flops 1208254464 | bytes 5899776 | tf_op jit(solution)/shard_map/dot_general | solution.py:30
  278.4 8.8 %fusion = f32[384,2048]{1,0:T(8,128)} fusion(bf16[1,2048,768]{2,1,0:T(8,128)(2,1)} %all-gather.12.cloned.1.call-done, f32[384,768]{1,0:T(8,128)} %fusion.12, bf16[384,2048]{1,0:T(8,128)(2,1)} %reshape.163, bf16[1,2048,768]{2,1,0:T(8,128)(2,1)} %all-gather.10.cloned.1.call-done, f32[384,768]{1,0:T(8,128)} %fusion.2), kind=kOutput, calls=%fused_computation.8 | convolution fusion | flops 2418868224 | bytes 13369344 | tf_op jit(solution)/shard_map/dot_general | solution.py:39
  287.2 6.1 %add_convert_fusion = bf16[384,2048]{1,0:T(8,128)(2,1)} fusion(f32[384,2048]{1,0:T(8,128)} %fusion, bf16[1,2048,768]{2,1,0:T(8,128)(2,1)} %all-gather.10.cloned.1.call-done, f32[384,768]{1,0:T(8,128)} %fusion.12, f32[384,768]{1,0:T(8,128)} %fusion.2), kind=kOutput, calls=%fused_computation.18 | convolution fusion | flops 1211301888 | bytes 10223616 | tf_op jit(solution)/shard_map/dot_general | solution.py:42
  293.3 3.7 %reshape.164 = bf16[64,6,2048]{2,1,0:T(8,128)(2,1)} reshape(bf16[384,2048]{1,0:T(8,128)(2,1)} %add_convert_fusion) | data formatting | bytes 3145728 | tf_op jit(solution)/shard_map/reshape | solution.py:142
  297.0 8.3 %all-to-all-start.3 = ((bf16[64,6,2048]{2,1,0:T(8,128)(2,1)}), bf16[64,6,2048]{2,1,0:T(8,128)(2,1)}, u32[]{:S(2)}, u32[]{:S(2)}) async-start(bf16[64,6,2048]{2,1,0:T(8,128)(2,1)} %reshape.164), calls=%async_computation.4 | async-start | bytes 4194304 | tf_op jit(solution)/shard_map/all_to_all | solution.py:143
  305.4 35.1 %all-to-all-done.3 = bf16[64,6,2048]{2,1,0:T(8,128)(2,1)} async-done(((bf16[64,6,2048]{2,1,0:T(8,128)(2,1)}), bf16[64,6,2048]{2,1,0:T(8,128)(2,1)}, u32[]{:S(2)}, u32[]{:S(2)}) %all-to-all-start.3) | async-done | bytes 1572896 | tf_op jit(solution)/shard_map/all_to_all | solution.py:143
  340.5 3.7 %reshape.165 = bf16[384,2048]{1,0:T(8,128)(2,1)} reshape(bf16[64,6,2048]{2,1,0:T(8,128)(2,1)} %all-to-all-done.3) | data formatting | bytes 3145728 | tf_op jit(solution)/shard_map/reshape | solution.py:144
  344.2 4.0 %gather_fusion.3 = bf16[256,2048]{1,0:T(8,128)(2,1)S(1)} fusion(bf16[384,2048]{1,0:T(8,128)(2,1)} %reshape.165, s32[1024]{0:T(1024)S(1)} %pad_clamp_fusion), kind=kCustom, calls=%fused_computation.3 | custom fusion | bytes 2098176 | tf_op jit(solution)/shard_map/gather | solution.py:144
  350.6 4.1 %reduce_sum.61 = f32[128,2048]{1,0:T(8,128)S(1)} reduce(f32[128,2,2048]{2,1,0:T(2,128)} %reshape.168, f32[]{:T(128)} %constant.23.clone.1), dimensions={1}, to_apply=%region_12.13 | reduce | flops 262144 | bytes 3145732 | tf_op jit(solution)/shard_map/reduce_sum | solution.py:145
  (210 shorter events, 26.7 us)
Async XLA Ops:
  6.5 1.6 copy-start
  6.5 110.7 %copy-start.7 = (s32[512]{0:T(512)S(1)}, s32[512]{0:T(512)}, u32[]{:S(2)}) copy-start(s32[512]{0:T(512)} %param.15) | copy-start | bytes 6148
  6.5 163.7 %reduce-scatter.2.cloned.1.call-start = ((), (), s32[]{:S(2)}) async-start(), calls=%async_computation.5 | async-start | bytes 589824 | tf_op jit(solution)/shard_map/reduce_scatter | solution.py:76
  117.3 2.9 copy-start.5
  118.6 3.1 copy-start.8
  118.6 15.8 %copy-start.6 = (bf16[2048]{0:T(1024)(128)(2,1)S(1)}, bf16[2048]{0:T(1024)(128)(2,1)}, u32[]{:S(2)}) copy-start(bf16[2048]{0:T(1024)(128)(2,1)} %param.18) | copy-start | bytes 12292
  118.6 15.8 %copy-start.1 = (bf16[1,128,2048]{2,1,0:T(8,128)(2,1)S(1)}, bf16[1,128,2048]{2,1,0:T(8,128)(2,1)}, u32[]{:S(2)}) copy-start(bf16[1,128,2048]{2,1,0:T(8,128)(2,1)} %param.17) | copy-start | bytes 1572868
  118.6 150.3 %all-gather.12.cloned.1.call-start = ((), (), s32[]{:S(2)}) async-start(), calls=%async_computation.8 | async-start | bytes 3538944 | tf_op jit(solution)/shard_map/all_gather | solution.py:120
  119.4 154.3 %all-gather.8.cloned.1.call-start = ((), (), s32[]{:S(2)}) async-start(), calls=%async_computation.6 | async-start | bytes 3538944 | tf_op jit(solution)/shard_map/all_gather | solution.py:122
  127.1 20.6 %all-to-all-start = ((bf16[64,1,6]{2,1,0:T(2,128)(2,1)}), bf16[64,1,6]{2,1,0:T(2,128)(2,1)S(1)}, u32[]{:S(2)}, u32[]{:S(2)}) async-start(bf16[64,1,6]{2,1,0:T(2,128)(2,1)} %convert_element_type.124), calls=%async_computation.1 | async-start | bytes 65536 | tf_op jit(solution)/shard_map/all_to_all | solution.py:131
  141.7 28.2 %copy-start.9 = (s32[1,1,8]{2,1,0:T(1,128)S(1)}, s32[1,1,8]{2,1,0:T(1,128)}, u32[]{:S(2)}) copy-start(s32[1,1,8]{2,1,0:T(1,128)} %param.16) | copy-start | bytes 100
  147.7 76.5 %all-to-all-start.2 = ((bf16[64,6,2048]{2,1,0:T(8,128)(2,1)}), bf16[64,6,2048]{2,1,0:T(8,128)(2,1)}, u32[]{:S(2)}, u32[]{:S(2)}) async-start(bf16[64,6,2048]{2,1,0:T(8,128)(2,1)} %reshape.162), calls=%async_computation.3 | async-start | bytes 4194304 | tf_op jit(solution)/shard_map/all_to_all | solution.py:129
  169.4 109.1 %all-gather.10.cloned.1.call-start = ((), (), s32[]{:S(2)}) async-start(), calls=%async_computation.7 | async-start | bytes 3538944 | tf_op jit(solution)/shard_map/all_gather | solution.py:121
  171.5 0.8 copy-start.3
  224.2 40.9 %all-to-all-start.1 = ((bf16[64,6,2048]{2,1,0:T(8,128)(2,1)}), bf16[64,6,2048]{2,1,0:T(8,128)(2,1)}, u32[]{:S(2)}, u32[]{:S(2)}) async-start(bf16[64,6,2048]{2,1,0:T(8,128)(2,1)} %reshape.160), calls=%async_computation.2 | async-start | bytes 4194304 | tf_op jit(solution)/shard_map/all_to_all | solution.py:130
  297.0 43.5 %all-to-all-start.3 = ((bf16[64,6,2048]{2,1,0:T(8,128)(2,1)}), bf16[64,6,2048]{2,1,0:T(8,128)(2,1)}, u32[]{:S(2)}, u32[]{:S(2)}) async-start(bf16[64,6,2048]{2,1,0:T(8,128)(2,1)} %reshape.164), calls=%async_computation.4 | async-start | bytes 4194304 | tf_op jit(solution)/shard_map/all_to_all | solution.py:143
  354.7 1.4 copy-start.2
  354.7 1.4 copy-start.4
Sparse Core Ops, SparseCore 0:
  118.7 28.8 reduce-scatter.1
  150.0 33.8 all-gather.11
  186.2 33.1 all-gather.7
  221.6 33.1 all-gather.9
where the time goes:
time: 367 us; the launch traced here: 364 us
  waiting for transfers between devices  115 us (31%)
  blocking collectives  104 us (28%)
  starting transfers between devices  47.3 us (13%)
  local copies, waits for them, and re-layouts  44.3 us (12%)
  matrix products  28.7 us (8%)
  between operations  13.5 us (4%)
  other arithmetic  9.64 us (3%)
    all_gather x2, blocking collectives, joined(): pieces = jax.tree.map(lambda part: lax.all_gather(part, axis), value)  104 us
    all_to_all x1, waiting for transfers between devices, per_device(): lax.all_to_all(send_rows, 'expert', split_axis=0, concat_axis=0, tiled=True)  45.1 us
    all_to_all x1, waiting for transfers between devices, per_device(): lax.all_to_all(result, 'expert', split_axis=0, concat_axis=0, tiled=True)  35.1 us
    all_to_all x1, waiting for transfers between devices, per_device(): lax.all_to_all(send_cot, 'expert', split_axis=0, concat_axis=0, tiled=True)  27.1 us
    all_to_all x1, starting transfers between devices, per_device(): lax.all_to_all(send_rows, 'expert', split_axis=0, concat_axis=0, tiled=True)  21.6 us
    all_to_all x1, starting transfers between devices, per_device(): lax.all_to_all(send_cot, 'expert', split_axis=0, concat_axis=0, tiled=True)  9.86 us
    dot_general x1, matrix products, expert_backward(): lax.dot_general(grad_gate, weight_gate, contract, preferred_element_type=...  8.76 us
    all_to_all x1, starting transfers between devices, per_device(): lax.all_to_all(result, 'expert', split_axis=0, concat_axis=0, tiled=True)  8.34 us
  transfers between devices with their start and end apart: 8, of which 4 were waited for; matrix products, arithmetic and copies ran while one was open for 11% of the time, Pallas kernels for 0%

commit v1 on v0

v1 whole, which is shorter than its diff:
```python
import functools
import jax
import jax.numpy as jnp
from jax import lax
from jax.experimental import pallas as pl
from jax.experimental.pallas import tpu as pltpu
from jax.sharding import PartitionSpec as P

SCORE_SCALE = 20.0
GRAD_SCALE = 2560.0
EPSILON = 1e-06
BF = jnp.bfloat16
F32 = jnp.float32

SLOTS = 6
BLOCK = 8
SECTION = 512
SECTIONS = 3


def iota(shape, dim):
    return lax.broadcasted_iota(jnp.int32, shape, dim)


def dot(a, b):
    return jnp.dot(a, b, preferred_element_type=F32)


def dot_first(a, b):
    return lax.dot_general(a, b, (((0,), (0,)), ((), ())), preferred_element_type=F32)


def dot_last(a, b):
    return lax.dot_general(a, b, (((1,), (1,)), ((), ())), preferred_element_type=F32)


def section(k):
    return slice(k * SECTION, (k + 1) * SECTION)


def tail_row(q, k):
    rank = jnp.bitwise_and(q, BLOCK - 1)
    high = (rank >= 3).astype(jnp.int32)
    return jnp.where(rank - 3 * high == k, q - rank + SLOTS + high, -1)


def picks(rows, q, first, second):
    r = iota((rows, q.shape[1]), 0)
    zero = jnp.zeros((), F32)
    return (jnp.where(r == q[0:1], first, zero) + jnp.where(r == q[1:2], second, zero)).astype(BF)


def pack_rows(rows_ref, q, out_ref):
    total = out_ref.shape[0]
    main = picks(total, q, 1.0, 1.0)
    tail = rows_ref[:, section(SECTIONS)]
    for k in range(SECTIONS):
        left = jnp.concatenate([main, picks(total, tail_row(q, k), 1.0, 1.0)], axis=1)
        right = jnp.concatenate([rows_ref[:, section(k)], tail], axis=0)
        out_ref[:, section(k)] = dot(left, right).astype(BF)


def inverse_rms(stream):
    return lax.rsqrt(jnp.mean(stream * stream, axis=-1, keepdims=True) + EPSILON)


def dispatch_kernel(residual_ref, gain_ref, ids_ref, out_ref, q_ref, normed_ref, *, experts):
    stream = residual_ref[...].astype(F32)
    normed_ref[...] = (stream * inverse_rms(stream) * gain_ref[...].astype(F32)).astype(BF)
    ids = jnp.concatenate([ids_ref[0:1, :], ids_ref[1:2, :]], axis=1)
    count = ids.shape[1]
    table = (iota((experts, count), 0) == ids).astype(F32)
    earlier = dot(
        table.astype(BF), (iota((count, count), 0) < iota((count, count), 1)).astype(F32).astype(BF)
    )
    rank = jnp.sum(table * earlier, axis=0, keepdims=True).astype(jnp.int32)
    q_flat = ids * BLOCK + rank
    half = count // 2
    q = jnp.concatenate([q_flat[:, :half], q_flat[:, half:]], axis=0)
    q_ref[...] = q
    pack_rows(normed_ref, q, out_ref)


def file_cotangent(code_grad_ref, lengths_ref):
    files = code_grad_ref.shape[0]
    length = jnp.zeros((files, 1), jnp.int32)
    row = iota((files, 1), 0)
    for f in range(files):
        length = jnp.where(row == f, lengths_ref[0, f], length)
    return (code_grad_ref[...] / length.astype(F32)).astype(BF)


def token_cotangent(code_grad_ref, lengths_ref, tokens):
    files = code_grad_ref.shape[0]
    position = iota((1, tokens), 1)
    segment = jnp.zeros((1, tokens), jnp.int32)
    end = jnp.int32(0)
    for f in range(files):
        end = end + lengths_ref[0, f]
        segment = segment + (position >= end).astype(jnp.int32)
    member = (iota((files, tokens), 0) == segment).astype(F32).astype(BF)
    return dot_first(member, file_cotangent(code_grad_ref, lengths_ref))


def cotangent_kernel(code_grad_ref, lengths_ref, q_ref, out_ref, token_ref):
    token_ref[...] = token_cotangent(code_grad_ref, lengths_ref, token_ref.shape[0]).astype(BF)
    pack_rows(token_ref, q_ref[...], out_ref)


def halves(total):
    return 2 if total % 512 == 0 else 1


def unpack_blocks(block_ref, rows_ref):
    parts = halves(block_ref.shape[0])
    height = block_ref.shape[0] // parts
    wide = height // BLOCK * SLOTS
    i, r = iota((wide, height), 0), iota((wide, height), 1)
    peer, j = r >> 3, r & (BLOCK - 1)
    main = ((i == peer * SLOTS + j) & (j < SLOTS)).astype(F32).astype(BF)
    for g in range(parts):
        rows = slice(g * wide, (g + 1) * wide)
        tail = jnp.zeros((wide, SECTION), F32)
        for k in range(SECTIONS):
            last = ((i == peer * SLOTS + (j - SLOTS) * 3 + k) & (j >= SLOTS)).astype(F32).astype(BF)
            both = dot(
                jnp.concatenate([main, last], axis=0),
                block_ref[g * height : (g + 1) * height, section(k)],
            )
            rows_ref[rows, section(k)] = both[:wide].astype(BF)
            tail = tail + both[wide:]
        rows_ref[rows, section(SECTIONS)] = tail.astype(BF)


def pack_blocks(rows_ref, block_ref):
    parts = halves(block_ref.shape[0])
    height = block_ref.shape[0] // parts
    wide = height // BLOCK * SLOTS
    r, i = iota((height, wide), 0), iota((height, wide), 1)
    peer, j = r >> 3, r & (BLOCK - 1)
    main = ((i == peer * SLOTS + j) & (j < SLOTS)).astype(F32).astype(BF)
    for g in range(parts):
        rows = slice(g * wide, (g + 1) * wide)
        tail = rows_ref[rows, section(SECTIONS)].astype(BF)
        for k in range(SECTIONS):
            last = ((i == peer * SLOTS + (j - SLOTS) * 3 + k) & (j >= SLOTS)).astype(F32).astype(BF)
            block_ref[g * height : (g + 1) * height, section(k)] = (
                dot(main, rows_ref[rows, section(k)].astype(BF)) + dot(last, tail)
            ).astype(BF)


def forward_kernel(block_ref, gate_ref, up_ref, by_gate_ref, by_up_ref, rows_ref):
    @pl.when(pl.program_id(0) == 0)
    def _():
        unpack_blocks(block_ref, rows_ref)

    gate_pre = dot(rows_ref[...], gate_ref[...])
    up_pre = dot(rows_ref[...], up_ref[...])
    s = jax.nn.sigmoid(gate_pre)
    by_gate_ref[...] = up_pre * s * (1.0 + gate_pre * (1.0 - s))
    by_up_ref[...] = gate_pre * s


def backward_kernel(
    block_ref, down_ref, gate_ref, up_ref, by_gate_ref, by_up_ref, out_ref, rows_ref, total_ref
):
    step = pl.program_id(0)

    @pl.when(step == 0)
    def _():
        unpack_blocks(block_ref, rows_ref)

    back = dot(rows_ref[...], down_ref[...])
    part = dot_last((back * by_gate_ref[...]).astype(BF), gate_ref[...]) + dot_last(
        (back * by_up_ref[...]).astype(BF), up_ref[...]
    )

    @pl.when(step == 0)
    def _():
        total_ref[...] = part

    @pl.when(step > 0)
    def _():
        total_ref[...] += part

    @pl.when(step == pl.num_programs(0) - 1)
    def _():
        pack_blocks(total_ref, out_ref)


def finish_kernel(
    block_ref, residual_ref, gain_ref, q_ref, units_ref, code_grad_ref, lengths_ref, out_ref, grad_ref
):
    total, q = block_ref.shape[0], q_ref[...]
    gates = units_ref[...].astype(F32) * (1.0 / 256.0)
    first, second = gates[0:1], gates[1:2]
    tokens = q.shape[1]
    main = picks(total, q, first, second)
    tail = jnp.zeros((tokens, SECTION), F32)
    for k in range(SECTIONS):
        both = dot_first(
            jnp.concatenate([main, picks(total, tail_row(q, k), first, second)], axis=1),
            block_ref[:, section(k)],
        )
        grad_ref[:, section(k)] = both[:tokens]
        tail = tail + both[tokens:]
    grad_ref[:, section(SECTIONS)] = tail
    stream = residual_ref[...].astype(F32)
    root = inverse_rms(stream)
    scaled = gain_ref[...].astype(F32) * grad_ref[...]
    correction = jnp.mean(scaled * stream, axis=-1, keepdims=True)
    cot = token_cotangent(code_grad_ref, lengths_ref, tokens)
    out_ref[...] = (cot + root * scaled - stream * (root * root * root * correction)).astype(BF)


PARAMS = pltpu.CompilerParams(vmem_limit_bytes=56 << 20)
IN_SMEM = pl.BlockSpec(memory_space=pltpu.SMEM)
IN_VMEM = pl.BlockSpec(memory_space=pltpu.VMEM)


def halve_over_dp(rows, files):
    me = lax.axis_index("dp")
    size = lax.axis_size("dp")
    value = rows.reshape(size, files, rows.shape[1])
    bit = 1
    while bit < size:
        value = value.reshape(value.shape[0] // 2, 2, files, rows.shape[1])
        mine = (me // bit) % 2
        keep = lax.dynamic_index_in_dim(value, mine, 1, keepdims=False)
        give = lax.dynamic_index_in_dim(value, 1 - mine, 1, keepdims=False)
        value = keep + lax.ppermute(give, "dp", [(d, d ^ bit) for d in range(size)])
        bit *= 2
    return value.reshape(files, rows.shape[1])


def per_device(
    query_reps,
    code_reps,
    positives,
    file_lengths,
    residual,
    norm_gain,
    expert_ids,
    gate_units,
    w_gate,
    w_up,
    w_down,
):
    owners = lax.axis_size("expert")
    columns = code_reps.shape[0]
    queries, width = query_reps.shape
    files = file_lengths.shape[2]
    tokens = residual.shape[1]
    hidden = w_gate.shape[2]
    total = owners * BLOCK
    lengths = file_lengths.reshape(1, files)
    stream = residual[0]
    gain = norm_gain.reshape(1, width)
    ids = expert_ids[0].T
    units = gate_units[0].T

    weights = lax.all_gather(
        jnp.concatenate([w_gate[0], w_up[0], w_down[0]], axis=1), "dp", axis=0, tiled=True
    )

    scores = dot_last(code_reps, query_reps) * SCORE_SCALE
    local_top = jnp.max(scores, axis=0)
    local_total = jnp.sum(jnp.exp(scores - local_top[None, :]), axis=0)
    stats = jnp.concatenate([local_top, local_total])
    stats = lax.all_to_all(
        jnp.broadcast_to(stats[None, None], (owners, 1, 2 * queries)), "expert", 0, 0, tiled=True
    ).reshape(owners, 2 * queries)
    tops, totals = stats[:, :queries], stats[:, queries:]
    row_top = jnp.max(tops, axis=0)
    row_total = jnp.sum(totals * jnp.exp(tops - row_top[None, :]), axis=0)
    probabilities = jnp.exp(scores - row_top[None, :]) / row_total[None, :]
    column_ids = lax.axis_index("expert") * columns + jnp.arange(columns, dtype=jnp.int32)
    onehot = (positives[None, :] == column_ids[:, None]).astype(F32)
    code_weights = (GRAD_SCALE * (probabilities - onehot)).astype(BF)
    code_grad = halve_over_dp(dot(code_weights, query_reps), files)

    blocks, q = pl.pallas_call(
        functools.partial(dispatch_kernel, experts=owners),
        out_shape=(
            jax.ShapeDtypeStruct((total, SECTIONS * SECTION), BF),
            jax.ShapeDtypeStruct((2, tokens), jnp.int32),
        ),
        in_specs=[IN_VMEM] * 3,
        out_specs=(IN_VMEM, IN_VMEM),
        scratch_shapes=[pltpu.VMEM((tokens, width), BF)],
        compiler_params=PARAMS,
        name="dispatch",
    )(stream, gain, ids)

    def exchange(value):
        shape = value.shape
        return lax.all_to_all(
            value.reshape(owners, BLOCK, shape[1]), "expert", 0, 0, tiled=True
        ).reshape(shape)

    blocks = exchange(blocks)
    cot_blocks = exchange(
        pl.pallas_call(
            cotangent_kernel,
            out_shape=jax.ShapeDtypeStruct((total, SECTIONS * SECTION), BF),
            in_specs=[IN_VMEM, IN_SMEM, IN_VMEM],
            out_specs=IN_VMEM,
            scratch_shapes=[pltpu.VMEM((tokens, width), BF)],
            compiler_params=PARAMS,
            name="cotangent",
        )(code_grad, lengths, q)
    )

    step = 256
    steps = hidden // step
    rows = owners * SLOTS
    whole = pl.BlockSpec((total, SECTIONS * SECTION), lambda f: (0, 0), pipeline_mode=pl.Buffered(1))
    part = pl.BlockSpec((rows, step), lambda f: (0, f))
    gate_part = pl.BlockSpec((width, step), lambda f: (0, f))
    up_part = pl.BlockSpec((width, step), lambda f: (0, steps + f))
    down_part = pl.BlockSpec((width, step), lambda f: (0, 2 * steps + f))
    by_gate, by_up = pl.pallas_call(
        forward_kernel,
        out_shape=(jax.ShapeDtypeStruct((rows, hidden), F32),) * 2,
        grid=(steps,),
        in_specs=[whole, gate_part, up_part],
        out_specs=(part, part),
        scratch_shapes=[pltpu.VMEM((rows, width), BF)],
        compiler_params=PARAMS,
        name="expert_forward",
    )(blocks, weights, weights)
    result = pl.pallas_call(
        backward_kernel,
        out_shape=jax.ShapeDtypeStruct((total, SECTIONS * SECTION), BF),
        grid=(steps,),
        in_specs=[whole, down_part, gate_part, up_part, part, part],
        out_specs=whole,
        scratch_shapes=[pltpu.VMEM((rows, width), BF), pltpu.VMEM((rows, width), F32)],
        compiler_params=PARAMS,
        name="expert_backward",
    )(cot_blocks, weights, weights, weights, by_gate, by_up)

    token_grad = pl.pallas_call(
        finish_kernel,
        out_shape=jax.ShapeDtypeStruct((tokens, width), BF),
        in_specs=[IN_VMEM] * 6 + [IN_SMEM],
        out_specs=IN_VMEM,
        scratch_shapes=[pltpu.VMEM((tokens, width), F32)],
        compiler_params=PARAMS,
        name="finish",
    )(exchange(result), stream, gain, q, units, code_grad, lengths)
    return token_grad[None]


def solution(mesh):
    return jax.shard_map(
        per_device,
        mesh=mesh,
        in_specs=(
            P("dp", None),
            P("expert", None),
            P("dp"),
            P("expert", "dp", None),
            P("expert", "dp", None),
            P(),
            P("expert", "dp", None),
            P("expert", "dp", None),
            P("expert", "dp", None),
            P("expert", "dp", None),
            P("expert", "dp", None),
        ),
        out_specs=P("expert", "dp", None),
        check_vma=False,
    )
```

time: 367 us -> 202 us (0.55)
  blocking collectives: 104 us -> 45.7 us
  waiting for transfers between devices: 115 us -> 67.9 us
  local copies, waits for them, and re-layouts: 44.3 us -> 1.56 us
  Pallas kernels: 0 us -> 30.8 us
  matrix products: 28.7 us -> 1.3 us
  starting transfers between devices: 47.3 us -> 37 us
  other arithmetic: 9.64 us -> 3.29 us
    all_gather x2 -> x0, blocking collectives: 104 us -> none  [joined(): pieces = jax.tree.map(lambda part: lax.all_gather(part, axis), value)]
    all_to_all x4 -> x3, waiting for transfers between devices: 113 us -> 52.7 us  [the longest x2 41.5 us: exchange(): lax.all_to_all(value.reshape(owners, BLOCK, shape[1]), 'expert', 0, 0, ti...]
    all_to_all x0 -> x1, blocking collectives: none -> 45.7 us  [exchange(): lax.all_to_all(value.reshape(owners, BLOCK, shape[1]), 'expert', 0, 0, ti...]
    pallas_call x0 -> x5, Pallas kernels: none -> 30.8 us  [the longest x1 13.7 us: per_device(): pl.pallas_call(backward_kernel, out_shape=jax.ShapeDtypeStruct((total, SE...]
    dot_general x7 -> x2, matrix products: 28.7 us -> 1.3 us  [the longest x1 0.77 us: dot_last(): lax.dot_general(a, b, (((1,), (1,)), ((), ())), preferred_element_type=F32)]
    reshape x6 -> x1, local copies, waits for them, and re-layouts: 22.2 us -> 0.59 us  [per_device(): gain = norm_gain.reshape(1, width)]
    all_to_all x4 -> x3, starting transfers between devices: 47.1 us -> 28.9 us  [the longest x1 16.6 us: per_device(): lax.all_to_all(jnp.broadcast_to(stats[None, None], (owners, 1, 2 * querie...]
    ppermute x0 -> x3, waiting for transfers between devices: none -> 15.2 us  [halve_over_dp(): value = keep + lax.ppermute(give, 'dp', [(d, d ^ bit) for d in range(size)])]
  transfers between devices with their start and end apart: 8 -> 7, of which waited for: 4 -> 6; matrix products, arithmetic and copies ran while one was open for 11% -> 2% of each run, Pallas kernels for 0% -> 7%
where the time goes in v1:
time: 202 us; the launch traced here: 201 us
  waiting for transfers between devices  67.9 us (34%)
  blocking collectives  45.7 us (23%)
  starting transfers between devices  37 us (18%)
  Pallas kernels  30.8 us (15%)
  between operations  13.6 us (7%)
  other arithmetic  3.29 us (2%)
    all_to_all x1, blocking collectives, exchange(): lax.all_to_all(value.reshape(owners, BLOCK, shape[1]), 'expert', 0, 0, ti...  45.7 us
    all_to_all x2, waiting for transfers between devices, exchange(): lax.all_to_all(value.reshape(owners, BLOCK, shape[1]), 'expert', 0, 0, ti...  41.5 us
    all_to_all x1, starting transfers between devices, per_device(): lax.all_to_all(jnp.broadcast_to(stats[None, None], (owners, 1, 2 * querie...  16.6 us
    ppermute x3, waiting for transfers between devices, halve_over_dp(): value = keep + lax.ppermute(give, 'dp', [(d, d ^ bit) for d in range(size)])  15.2 us
    pallas_call x1, Pallas kernels, per_device(): pl.pallas_call(backward_kernel, out_shape=jax.ShapeDtypeStruct((total, SE...  13.7 us
    all_to_all x2, starting transfers between devices, exchange(): lax.all_to_all(value.reshape(owners, BLOCK, shape[1]), 'expert', 0, 0, ti...  12.3 us
    all_to_all x1, waiting for transfers between devices, per_device(): lax.all_to_all(jnp.broadcast_to(stats[None, None], (owners, 1, 2 * querie...  11.2 us
    ppermute x3, starting transfers between devices, halve_over_dp(): value = keep + lax.ppermute(give, 'dp', [(d, d ^ bit) for d in range(size)])  8.12 us
  transfers between devices with their start and end apart: 7, of which 6 were waited for; matrix products, arithmetic and copies ran while one was open for 2% of the time, Pallas kernels for 7%

profile of v1, /device:TPU:6, one launch (start us, length us, event | category | flops | bytes accessed | tf_op | source)
XLA Modules:
  0.0 201.2 jit_solution(17882666367666684964)
XLA Ops:
  6.5 2.5 %pad_maximum_fusion = bf16[256,2304]{1,0:T(8,128)(2,1)} fusion(bf16[256,768]{1,0:T(8,128)(2,1)} %bitcast.48, bf16[256,768]{1,0:T(8,128)(2,1)} %bitcast.49, bf16[256,768]{1,0:T(8,128)(2,1)} %bitcast.50), kind=kLoop, calls=%fused_computation | loop fusion | flops 3538944 | bytes 2359296 | tf_op jit(solution)/shard_map/concatenate | solution.py:263
  9.1 0.8 fusion.8
  9.9 0.8 broadcast_in_dim.4
  10.8 16.6 %all-to-all-start = ((f32[64,1,1024]{2,1,0:T(1,128)}), f32[64,1,1024]{2,1,0:T(1,128)S(1)}, u32[]{:S(2)}, u32[]{:S(2)}) async-start(f32[64,1,1024]{2,1,0:T(1,128)} %broadcast_in_dim.4), calls=%async_computation | async-start | bytes 524288 | tf_op jit(solution)/shard_map/all_to_all | solution.py:270
  27.4 0.6 reshape.53.gain_ref
  28.0 3.1 %dispatch.1 = (bf16[512,1536]{1,0:T(8,128)(2,1)}, s32[2,128]{1,0:T(2,128)}) custom-call(bf16[128,2048]{1,0:T(8,128)(2,1)} %bitcast.39, bf16[1,2048]{1,0:T(2,128)(2,1)} %reshape.53.gain_ref, s32[2,128]{1,0:T(2,128)} %bitcast.54), custom_call_target="tpu_custom_call" | custom-call | tf_op jit(solution)/shard_map/dispatch/pallas_call | solution.py:282
  31.1 11.2 %all-to-all-done = f32[64,1,1024]{2,1,0:T(1,128)S(1)} async-done(((f32[64,1,1024]{2,1,0:T(1,128)}), f32[64,1,1024]{2,1,0:T(1,128)S(1)}, u32[]{:S(2)}, u32[]{:S(2)}) %all-to-all-start) | async-done | bytes 262176 | tf_op jit(solution)/shard_map/all_to_all | solution.py:270
  42.3 5.5 %all-to-all-start.2 = ((bf16[64,8,1536]{2,1,0:T(8,128)(2,1)}), bf16[64,8,1536]{2,1,0:T(8,128)(2,1)}, u32[]{:S(2)}, u32[]{:S(2)}) async-start(bf16[64,8,1536]{2,1,0:T(8,128)(2,1)} %bitcast.45), calls=%async_computation.2 | async-start | bytes 3145728 | tf_op jit(solution)/shard_map/all_to_all | solution.py:297
  47.9 0.5 fusion.1
  48.5 1.9 collective-permute-start
  50.5 1.5 collective-permute-done
  52.0 2.9 %collective-permute-start.1 = (f32[2,8,2048]{2,1,0:T(8,128)S(1)}, f32[2,8,2048]{2,1,0:T(8,128)S(1)}, u32[]{:S(2)}, u32[]{:S(2)}) collective-permute-start(f32[2,8,2048]{2,1,0:T(8,128)S(1)} %dynamic-slice_bitcast_fusion.1), channel_id=1, source_target_pairs={{0,128},{64,192},{128,0},{192,64},{256,384},{320,448},{384,256},{4... | collective-permute-start | bytes 393224 | tf_op jit(solution)/shard_map/ppermute | solution.py:231
  54.9 7.8 %collective-permute-done.1 = f32[2,8,2048]{2,1,0:T(8,128)S(1)} collective-permute-done((f32[2,8,2048]{2,1,0:T(8,128)S(1)}, f32[2,8,2048]{2,1,0:T(8,128)S(1)}, u32[]{:S(2)}, u32[]{:S(2)}) %collective-permute-start.1) | collective-permute-done | bytes 131104 | tf_op jit(solution)/shard_map/ppermute | solution.py:231
  62.8 3.3 %collective-permute-start.2 = (f32[1,8,2048]{2,1,0:T(8,128)S(1)}, f32[1,8,2048]{2,1,0:T(8,128)S(1)}, u32[]{:S(2)}, u32[]{:S(2)}) collective-permute-start(f32[1,8,2048]{2,1,0:T(8,128)S(1)} %constant_dynamic-slice_fusion), channel_id=1, source_target_pairs={{0,256},{64,320},{128,384},{192,448},{256,0},{320,64},{384,128},{4... | collective-permute-start | bytes 196616 | tf_op jit(solution)/shard_map/ppermute | solution.py:231
  66.1 5.9 %collective-permute-done.2 = f32[1,8,2048]{2,1,0:T(8,128)S(1)} collective-permute-done((f32[1,8,2048]{2,1,0:T(8,128)S(1)}, f32[1,8,2048]{2,1,0:T(8,128)S(1)}, u32[]{:S(2)}, u32[]{:S(2)}) %collective-permute-start.2) | collective-permute-done | bytes 65568 | tf_op jit(solution)/shard_map/ppermute | solution.py:231
  72.0 0.6 add_bitcast_fusion.code_grad_ref
  72.6 2.9 %cotangent.1 = bf16[512,1536]{1,0:T(8,128)(2,1)} custom-call(f32[8,2048]{1,0:T(8,128)} %add_bitcast_fusion.code_grad_ref, s32[1,8]{1,0:T(1,128)} %bitcast.51, s32[2,128]{1,0:T(2,128)} %get-tuple-element.9.q_ref), custom_call_target="tpu_custom_call" | custom-call | tf_op jit(solution)/shard_map/cotangent/pallas_call | solution.py:303
  75.6 11.4 %all-to-all-done.2 = bf16[64,8,1536]{2,1,0:T(8,128)(2,1)} async-done(((bf16[64,8,1536]{2,1,0:T(8,128)(2,1)}), bf16[64,8,1536]{2,1,0:T(8,128)(2,1)}, u32[]{:S(2)}, u32[]{:S(2)}) %all-to-all-start.2) | async-done | bytes 1572896 | tf_op jit(solution)/shard_map/all_to_all | solution.py:297
  87.0 6.8 %all-to-all-start.1 = ((bf16[64,8,1536]{2,1,0:T(8,128)(2,1)}), bf16[64,8,1536]{2,1,0:T(8,128)(2,1)}, u32[]{:S(2)}, u32[]{:S(2)}) async-start(bf16[64,8,1536]{2,1,0:T(8,128)(2,1)} %bitcast.37), calls=%async_computation.1 | async-start | bytes 3145728 | tf_op jit(solution)/shard_map/all_to_all | solution.py:297
  93.8 7.7 %expert_forward.1 = (f32[384,768]{1,0:T(8,128)}, f32[384,768]{1,0:T(8,128)}) custom-call(bf16[512,1536]{1,0:T(8,128)(2,1)} %bitcast.17.block_ref, bf16[2048,2304]{1,0:T(8,128)(2,1)} %all-gather.2.cloned.1.call-done.gate_ref.up_ref.down_ref, bf16[2048,2304]{1,0:T(8,128)(2,1)} %all-gather.2.cloned.1.call-done.gate_ref.up_ref.down_ref), custom_call_target="tpu_custom_call" | custom-call | tf_op jit(solution)/shard_map/expert_forward/pallas_call | solution.py:322
  101.5 30.1 %all-to-all-done.1 = bf16[64,8,1536]{2,1,0:T(8,128)(2,1)} async-done(((bf16[64,8,1536]{2,1,0:T(8,128)(2,1)}), bf16[64,8,1536]{2,1,0:T(8,128)(2,1)}, u32[]{:S(2)}, u32[]{:S(2)}) %all-to-all-start.1) | async-done | bytes 1572896 | tf_op jit(solution)/shard_map/all_to_all | solution.py:297
  131.6 13.7 %expert_backward.1 = bf16[512,1536]{1,0:T(8,128)(2,1)} custom-call(bf16[512,1536]{1,0:T(8,128)(2,1)} %bitcast.12.block_ref, bf16[2048,2304]{1,0:T(8,128)(2,1)} %all-gather.2.cloned.1.call-done.gate_ref.up_ref.down_ref, bf16[2048,2304]{1,0:T(8,128)(2,1)} %all-gather.2.cloned.1.call-done.gate_ref.up_ref.down_ref, ...), custom_call_target="tpu_custom_call" | custom-call | tf_op jit(solution)/shard_map/expert_backward/pallas_call | solution.py:332
  145.3 45.7 %all_to_all.20 = bf16[64,8,1536]{2,1,0:T(8,128)(2,1)} all-to-all(bf16[64,8,1536]{2,1,0:T(8,128)(2,1)} %bitcast.36), channel_id=1, replica_groups=mesh['dp'=8,'expert'=64] {'expert'}, dimensions={0} | all-to-all | bytes 3145728 | tf_op jit(solution)/shard_map/all_to_all | solution.py:297
  191.0 3.3 %finish.1 = bf16[128,2048]{1,0:T(8,128)(2,1)} custom-call(bf16[512,1536]{1,0:T(8,128)(2,1)} %bitcast.38, bf16[128,2048]{1,0:T(8,128)(2,1)} %bitcast.40, bf16[1,2048]{1,0:T(2,128)(2,1)} %reshape.53.gain_ref, s32[2,128]{1,0:T(2,128)} %get-tuple-element.9.q_ref, s32[2,128]{1,0:T(2,128)} %bitcast.53, f32[8,2048]{1,0:T(8,128)} %add_bitcast_fusion.code_grad_ref, ...), custom_call_target="tpu_custom_call" | custom-call | tf_op jit(solution)/shard_map/finish/pallas_call | solution.py:343
  (22 shorter events, 0.3 us)
Async XLA Ops:
  6.5 2.5 %copy-start = (bf16[512,2048]{1,0:T(8,128)(2,1)S(1)}, bf16[512,2048]{1,0:T(8,128)(2,1)}, u32[]{:S(2)}) copy-start(bf16[512,2048]{1,0:T(8,128)(2,1)} %param.11) | copy-start | bytes 6291460
  6.5 2.5 %copy-start.1 = (bf16[64,2048]{1,0:T(8,128)(2,1)S(1)}, bf16[64,2048]{1,0:T(8,128)(2,1)}, u32[]{:S(2)}) copy-start(bf16[64,2048]{1,0:T(8,128)(2,1)} %param.12) | copy-start | bytes 786436
  6.5 87.2 %all-gather.2.cloned.1.call-start = ((), (), s32[]{:S(2)}) async-start(), calls=%async_computation.4 | async-start | bytes 10616832 | tf_op jit(solution)/shard_map/all_gather | solution.py:262
  9.0 18.3 %copy-start.2 = (bf16[2048]{0:T(1024)(128)(2,1)S(1)}, bf16[2048]{0:T(1024)(128)(2,1)}, u32[]{:S(2)}) copy-start(bf16[2048]{0:T(1024)(128)(2,1)} %param.16) | copy-start | bytes 12292
  10.8 31.5 %all-to-all-start = ((f32[64,1,1024]{2,1,0:T(1,128)}), f32[64,1,1024]{2,1,0:T(1,128)S(1)}, u32[]{:S(2)}, u32[]{:S(2)}) async-start(f32[64,1,1024]{2,1,0:T(1,128)} %broadcast_in_dim.4), calls=%async_computation | async-start | bytes 524288 | tf_op jit(solution)/shard_map/all_to_all | solution.py:270
  31.1 16.9 %copy-start.3 = (s32[512]{0:T(512)S(1)}, s32[512]{0:T(512)}, u32[]{:S(2)}) copy-start(s32[512]{0:T(512)} %param.13) | copy-start | bytes 6148
  42.3 44.7 %all-to-all-start.2 = ((bf16[64,8,1536]{2,1,0:T(8,128)(2,1)}), bf16[64,8,1536]{2,1,0:T(8,128)(2,1)}, u32[]{:S(2)}, u32[]{:S(2)}) async-start(bf16[64,8,1536]{2,1,0:T(8,128)(2,1)} %bitcast.45), calls=%async_computation.2 | async-start | bytes 3145728 | tf_op jit(solution)/shard_map/all_to_all | solution.py:297
  48.5 3.4 %collective-permute-start = (f32[4,8,2048]{2,1,0:T(8,128)S(1)}, f32[4,8,2048]{2,1,0:T(8,128)S(1)}, u32[]{:S(2)}, u32[]{:S(2)}) collective-permute-start(f32[4,8,2048]{2,1,0:T(8,128)S(1)} %dynamic-slice_bitcast_fusion), channel_id=1, source_target_pairs={{0,64},{64,0},{128,192},{192,128},{256,320},{320,256},{384,448},{4... | collective-permute-start | bytes 786440 | tf_op jit(solution)/shard_map/ppermute | solution.py:231
  52.0 10.8 %collective-permute-start.1 = (f32[2,8,2048]{2,1,0:T(8,128)S(1)}, f32[2,8,2048]{2,1,0:T(8,128)S(1)}, u32[]{:S(2)}, u32[]{:S(2)}) collective-permute-start(f32[2,8,2048]{2,1,0:T(8,128)S(1)} %dynamic-slice_bitcast_fusion.1), channel_id=1, source_target_pairs={{0,128},{64,192},{128,0},{192,64},{256,384},{320,448},{384,256},{4... | collective-permute-start | bytes 393224 | tf_op jit(solution)/shard_map/ppermute | solution.py:231
  62.8 9.2 %collective-permute-start.2 = (f32[1,8,2048]{2,1,0:T(8,128)S(1)}, f32[1,8,2048]{2,1,0:T(8,128)S(1)}, u32[]{:S(2)}, u32[]{:S(2)}) collective-permute-start(f32[1,8,2048]{2,1,0:T(8,128)S(1)} %constant_dynamic-slice_fusion), channel_id=1, source_target_pairs={{0,256},{64,320},{128,384},{192,448},{256,0},{320,64},{384,128},{4... | collective-permute-start | bytes 196616 | tf_op jit(solution)/shard_map/ppermute | solution.py:231
  87.0 44.6 %all-to-all-start.1 = ((bf16[64,8,1536]{2,1,0:T(8,128)(2,1)}), bf16[64,8,1536]{2,1,0:T(8,128)(2,1)}, u32[]{:S(2)}, u32[]{:S(2)}) async-start(bf16[64,8,1536]{2,1,0:T(8,128)(2,1)} %bitcast.37), calls=%async_computation.1 | async-start | bytes 3145728 | tf_op jit(solution)/shard_map/all_to_all | solution.py:297
Sparse Core Ops, SparseCore 0:
  9.5 66.3 all-gather.1

commit v2 on v1

--- a/solution.py
+++ b/solution.py
@@ -64,7 +64,16 @@
     return lax.rsqrt(jnp.mean(stream * stream, axis=-1, keepdims=True) + EPSILON)
 
 
-def dispatch_kernel(residual_ref, gain_ref, ids_ref, out_ref, q_ref, normed_ref, *, experts):
+def dispatch_kernel(
+    residual_ref, gain_ref, ids_ref, w0_ref, w1_ref, w2_ref, out_ref, q_ref, joined_ref, normed_ref, sems, *, experts
+):
+    hidden = w0_ref.shape[1]
+    copies = [
+        pltpu.make_async_copy(w_ref, joined_ref.at[:, k * hidden : (k + 1) * hidden], sems.at[k])
+        for k, w_ref in enumerate((w0_ref, w1_ref, w2_ref))
+    ]
+    for copy in copies:
+        copy.start()
     stream = residual_ref[...].astype(F32)
     normed_ref[...] = (stream * inverse_rms(stream) * gain_ref[...].astype(F32)).astype(BF)
     ids = jnp.concatenate([ids_ref[0:1, :], ids_ref[1:2, :]], axis=1)
@@ -79,6 +88,8 @@
     q = jnp.concatenate([q_flat[:, :half], q_flat[:, half:]], axis=0)
     q_ref[...] = q
     pack_rows(normed_ref, q, out_ref)
+    for copy in copies:
+        copy.wait()
 
 
 def file_cotangent(code_grad_ref, lengths_ref):
@@ -141,51 +152,55 @@
     main = ((i == peer * SLOTS + j) & (j < SLOTS)).astype(F32).astype(BF)
     for g in range(parts):
         rows = slice(g * wide, (g + 1) * wide)
-        tail = rows_ref[rows, section(SECTIONS)].astype(BF)
+        tail = rows_ref[rows, section(SECTIONS)]
         for k in range(SECTIONS):
             last = ((i == peer * SLOTS + (j - SLOTS) * 3 + k) & (j >= SLOTS)).astype(F32).astype(BF)
             block_ref[g * height : (g + 1) * height, section(k)] = (
-                dot(main, rows_ref[rows, section(k)].astype(BF)) + dot(last, tail)
+                dot(main, rows_ref[rows, section(k)]) + dot(last, tail)
             ).astype(BF)
 
 
-def forward_kernel(block_ref, gate_ref, up_ref, by_gate_ref, by_up_ref, rows_ref):
-    @pl.when(pl.program_id(0) == 0)
-    def _():
-        unpack_blocks(block_ref, rows_ref)
-
-    gate_pre = dot(rows_ref[...], gate_ref[...])
-    up_pre = dot(rows_ref[...], up_ref[...])
+def forward_kernel(block_ref, weights_ref, factor_ref, rows_ref):
+    hidden = factor_ref.shape[1] // 2
+    unpack_blocks(block_ref, rows_ref)
+    gate_pre = dot(rows_ref[...], weights_ref[:, :hidden])
+    up_pre = dot(rows_ref[...], weights_ref[:, hidden : 2 * hidden])
     s = jax.nn.sigmoid(gate_pre)
-    by_gate_ref[...] = up_pre * s * (1.0 + gate_pre * (1.0 - s))
-    by_up_ref[...] = gate_pre * s
+    factor_ref[:, :hidden] = up_pre * s * (1.0 + gate_pre * (1.0 - s))
+    factor_ref[:, hidden:] = gate_pre * s
 
 
 def backward_kernel(
-    block_ref, down_ref, gate_ref, up_ref, by_gate_ref, by_up_ref, out_ref, rows_ref, total_ref
+    block_hbm, weights_hbm, factor_hbm, out_ref, block_ref, weights_ref, factor_ref, rows_ref, hidden_ref, sems
 ):
-    step = pl.program_id(0)
-
-    @pl.when(step == 0)
-    def _():
-        unpack_blocks(block_ref, rows_ref)
-
-    back = dot(rows_ref[...], down_ref[...])
-    part = dot_last((back * by_gate_ref[...]).astype(BF), gate_ref[...]) + dot_last(
-        (back * by_up_ref[...]).astype(BF), up_ref[...]
-    )
-
-    @pl.when(step == 0)
-    def _():
-        total_ref[...] = part
-
-    @pl.when(step > 0)
-    def _():
-        total_ref[...] += part
-
-    @pl.when(step == pl.num_programs(0) - 1)
-    def _():
-        pack_blocks(total_ref, out_ref)
+    hidden = factor_ref.shape[1] // 2
+    parts = halves(block_ref.shape[0])
+    height = block_ref.shape[0] // parts
+    pieces = [(block_hbm, block_ref, (slice(g * height, (g + 1) * height), slice(None))) for g in range(parts)]
+    pieces.append((weights_hbm, weights_ref, (slice(None), slice(2 * hidden, 3 * hidden))))
+    pieces.append((factor_hbm, factor_ref, (slice(None), slice(None))))
+    for k in range(SECTIONS + 1):
+        pieces.append((weights_hbm, weights_ref, (section(k), slice(0, 2 * hidden))))
+    copies = [
+        pltpu.make_async_copy(source.at[at], target.at[at], sems.at[n])
+        for n, (source, target, at) in enumerate(pieces)
+    ]
+    for copy in copies:
+        copy.start()
+    for copy in copies[:parts]:
+        copy.wait()
+    unpack_blocks(block_ref, rows_ref)
+    copies[parts].wait()
+    back = dot(rows_ref[...], weights_ref[:, 2 * hidden :])
+    copies[parts + 1].wait()
+    hidden_ref[:, :hidden] = (back * factor_ref[:, :hidden]).astype(BF)
+    hidden_ref[:, hidden:] = (back * factor_ref[:, hidden:]).astype(BF)
+    for k in range(SECTIONS + 1):
+        copies[parts + 2 + k].wait()
+        rows_ref[:, section(k)] = dot_last(
+            hidden_ref[...], weights_ref[section(k), : 2 * hidden]
+        ).astype(BF)
+    pack_blocks(rows_ref, out_ref)
 
 
 def finish_kernel(
@@ -213,9 +228,17 @@
     out_ref[...] = (cot + root * scaled - stream * (root * root * root * correction)).astype(BF)
 
 
-PARAMS = pltpu.CompilerParams(vmem_limit_bytes=56 << 20)
+def params(mib):
+    return pltpu.CompilerParams(vmem_limit_bytes=mib << 20)
+
+
 IN_SMEM = pl.BlockSpec(memory_space=pltpu.SMEM)
 IN_VMEM = pl.BlockSpec(memory_space=pltpu.VMEM)
+IN_HBM = pl.BlockSpec(memory_space=pltpu.HBM)
+
+
+def hbm(value):
+    return pltpu.with_memory_space_constraint(value, pltpu.HBM)
 
 
 def halve_over_dp(rows, files):
@@ -225,7 +248,7 @@
     bit = 1
     while bit < size:
         value = value.reshape(value.shape[0] // 2, 2, files, rows.shape[1])
-        mine = (me // bit) % 2
+        mine = jnp.minimum(me & bit, 1)
         keep = lax.dynamic_index_in_dim(value, mine, 1, keepdims=False)
         give = lax.dynamic_index_in_dim(value, 1 - mine, 1, keepdims=False)
         value = keep + lax.ppermute(give, "dp", [(d, d ^ bit) for d in range(size)])
@@ -259,38 +282,39 @@
     ids = expert_ids[0].T
     units = gate_units[0].T
 
-    weights = lax.all_gather(
-        jnp.concatenate([w_gate[0], w_up[0], w_down[0]], axis=1), "dp", axis=0, tiled=True
-    )
-
-    scores = dot_last(code_reps, query_reps) * SCORE_SCALE
-    local_top = jnp.max(scores, axis=0)
-    local_total = jnp.sum(jnp.exp(scores - local_top[None, :]), axis=0)
-    stats = jnp.concatenate([local_top, local_total])
-    stats = lax.all_to_all(
-        jnp.broadcast_to(stats[None, None], (owners, 1, 2 * queries)), "expert", 0, 0, tiled=True
-    ).reshape(owners, 2 * queries)
-    tops, totals = stats[:, :queries], stats[:, queries:]
-    row_top = jnp.max(tops, axis=0)
-    row_total = jnp.sum(totals * jnp.exp(tops - row_top[None, :]), axis=0)
-    probabilities = jnp.exp(scores - row_top[None, :]) / row_total[None, :]
-    column_ids = lax.axis_index("expert") * columns + jnp.arange(columns, dtype=jnp.int32)
-    onehot = (positives[None, :] == column_ids[:, None]).astype(F32)
-    code_weights = (GRAD_SCALE * (probabilities - onehot)).astype(BF)
-    code_grad = halve_over_dp(dot(code_weights, query_reps), files)
-
-    blocks, q = pl.pallas_call(
+    blocks, q, joined = pl.pallas_call(
         functools.partial(dispatch_kernel, experts=owners),
         out_shape=(
             jax.ShapeDtypeStruct((total, SECTIONS * SECTION), BF),
             jax.ShapeDtypeStruct((2, tokens), jnp.int32),
+            jax.ShapeDtypeStruct((w_gate.shape[1], 3 * hidden), BF),
         ),
-        in_specs=[IN_VMEM] * 3,
-        out_specs=(IN_VMEM, IN_VMEM),
-        scratch_shapes=[pltpu.VMEM((tokens, width), BF)],
-        compiler_params=PARAMS,
+        in_specs=[IN_VMEM] * 3 + [IN_HBM] * 3,
+        out_specs=(IN_VMEM, IN_VMEM, IN_HBM),
+        scratch_shapes=[pltpu.VMEM((tokens, width), BF), pltpu.SemaphoreType.DMA((3,))],
+        compiler_params=params(12),
         name="dispatch",
-    )(stream, gain, ids)
+    )(stream, gain, ids, hbm(w_gate[0]), hbm(w_up[0]), hbm(w_down[0]))
+    scores = dot_last(code_reps, query_reps) * SCORE_SCALE
+    owner = lax.axis_index("expert")
+    column_ids = owner * columns + jnp.arange(columns, dtype=jnp.int32)
+    positive = positives[None, :] == column_ids[:, None]
+    local_top = jnp.max(scores, axis=0)
+    exponent = jnp.exp(scores - local_top[None, :])
+    local_rest = jnp.sum(jnp.where(positive, 0.0, exponent), axis=0)
+    local_sum = local_top + jnp.log(jnp.sum(exponent, axis=0))
+    sent = jnp.broadcast_to(local_sum[None, None], (owners, 1, queries))
+    sums = lax.all_to_all(sent, "expert", 0, 0, tiled=True).reshape(owners, queries)
+    sums, joined = lax.optimization_barrier((sums, joined))
+    weights = lax.all_gather(joined, "dp", axis=0, tiled=True)
+    row_top = jnp.max(sums, axis=0)
+    shares = jnp.exp(sums - row_top[None, :])
+    row_total = jnp.sum(shares, axis=0)
+    own = (jnp.arange(owners, dtype=jnp.int32) == owner)[:, None]
+    row_rest = jnp.sum(jnp.where(own, 0.0, shares), axis=0) + local_rest * jnp.exp(local_top - row_top)
+    part = jnp.where(positive, -row_rest[None, :], jnp.exp(scores - row_top[None, :]))
+    code_weights = (GRAD_SCALE * (part / row_total[None, :])).astype(BF)
+    code_grad = halve_over_dp(dot(code_weights, query_reps), files)
 
     def exchange(value):
         shape = value.shape
@@ -306,39 +330,37 @@
             in_specs=[IN_VMEM, IN_SMEM, IN_VMEM],
             out_specs=IN_VMEM,
             scratch_shapes=[pltpu.VMEM((tokens, width), BF)],
-            compiler_params=PARAMS,
+            compiler_params=params(12),
             name="cotangent",
         )(code_grad, lengths, q)
     )
 
-    step = 256
-    steps = hidden // step
     rows = owners * SLOTS
-    whole = pl.BlockSpec((total, SECTIONS * SECTION), lambda f: (0, 0), pipeline_mode=pl.Buffered(1))
-    part = pl.BlockSpec((rows, step), lambda f: (0, f))
-    gate_part = pl.BlockSpec((width, step), lambda f: (0, f))
-    up_part = pl.BlockSpec((width, step), lambda f: (0, steps + f))
-    down_part = pl.BlockSpec((width, step), lambda f: (0, 2 * steps + f))
-    by_gate, by_up = pl.pallas_call(
+    factor = pl.pallas_call(
         forward_kernel,
-        out_shape=(jax.ShapeDtypeStruct((rows, hidden), F32),) * 2,
-        grid=(steps,),
-        in_specs=[whole, gate_part, up_part],
-        out_specs=(part, part),
+        out_shape=jax.ShapeDtypeStruct((rows, 2 * hidden), F32),
+        in_specs=[IN_VMEM] * 2,
+        out_specs=IN_VMEM,
         scratch_shapes=[pltpu.VMEM((rows, width), BF)],
-        compiler_params=PARAMS,
+        compiler_params=params(16),
         name="expert_forward",
-    )(blocks, weights, weights)
+    )(blocks, weights)
     result = pl.pallas_call(
         backward_kernel,
         out_shape=jax.ShapeDtypeStruct((total, SECTIONS * SECTION), BF),
-        grid=(steps,),
-        in_specs=[whole, down_part, gate_part, up_part, part, part],
-        out_specs=whole,
-        scratch_shapes=[pltpu.VMEM((rows, width), BF), pltpu.VMEM((rows, width), F32)],
-        compiler_params=PARAMS,
+        in_specs=[IN_HBM] * 3,
+        out_specs=IN_VMEM,
+        scratch_shapes=[
+            pltpu.VMEM((total, SECTIONS * SECTION), BF),
+            pltpu.VMEM((width, 3 * hidden), BF),
+            pltpu.VMEM((rows, 2 * hidden), F32),
+            pltpu.VMEM((rows, width), BF),
+            pltpu.VMEM((rows, 2 * hidden), BF),
+            pltpu.SemaphoreType.DMA((halves(total) + SECTIONS + 3,)),
+        ],
+        compiler_params=params(32),
         name="expert_backward",
-    )(cot_blocks, weights, weights, weights, by_gate, by_up)
+    )(hbm(cot_blocks), hbm(weights), hbm(factor))
 
     token_grad = pl.pallas_call(
         finish_kernel,
@@ -346,7 +368,7 @@
         in_specs=[IN_VMEM] * 6 + [IN_SMEM],
         out_specs=IN_VMEM,
         scratch_shapes=[pltpu.VMEM((tokens, width), F32)],
-        compiler_params=PARAMS,
+        compiler_params=params(12),
         name="finish",
     )(exchange(result), stream, gain, q, units, code_grad, lengths)
     return token_grad[None]

time: 202 us -> 195 us (0.965)
  Pallas kernels: 30.8 us -> 19.4 us
  local copies, waits for them, and re-layouts: 1.56 us -> 10.9 us
  waiting for transfers between devices: 67.9 us -> 64.8 us
    unnamed x9 -> x25, local copies, waits for them, and re-layouts: 0.06 us -> 10.1 us
    pallas_call x1, Pallas kernels: 13.7 us -> 9.49 us  [per_device(): pl.pallas_call(backward_kernel, out_shape=jax.ShapeDtypeStruct((total, SE...]
    pallas_call x1, Pallas kernels: 7.72 us -> 4.71 us  [per_device(): pl.pallas_call(forward_kernel, out_shape=jax.ShapeDtypeStruct((rows, 2 *...]
    concatenate x2 -> x0, other arithmetic: 2.49 us -> none  [the longest x1 2.48 us: per_device(): jnp.concatenate([w_gate[0], w_up[0], w_down[0]], axis=1)]
    all_to_all x1, waiting for transfers between devices: 11.2 us -> 8.83 us  [per_device(): lax.all_to_all(sent, 'expert', 0, 0, tiled=True).reshape(owners, queries)]
    all_to_all x2, waiting for transfers between devices: 41.5 us -> 39.2 us  [exchange(): lax.all_to_all(value.reshape(owners, BLOCK, shape[1]), 'expert', 0, 0, ti...]
  transfers between devices with their start and end apart: 7 -> 7, of which waited for: 6 -> 7; matrix products, arithmetic and copies ran while one was open for 2% -> 1% of each run, Pallas kernels for 7% -> 4%
where the time goes in v2:
time: 195 us; the launch traced here: 194 us
  waiting for transfers between devices  64.8 us (33%)
  blocking collectives  44.6 us (23%)
  starting transfers between devices  37.3 us (19%)
  Pallas kernels  19.4 us (10%)
  between operations  13.7 us (7%)
  local copies, waits for them, and re-layouts  10.9 us (6%)
  matrix products  2.25 us (1%)
    all_to_all x1, blocking collectives, exchange(): lax.all_to_all(value.reshape(owners, BLOCK, shape[1]), 'expert', 0, 0, ti...  44.6 us
    all_to_all x2, waiting for transfers between devices, exchange(): lax.all_to_all(value.reshape(owners, BLOCK, shape[1]), 'expert', 0, 0, ti...  39.2 us
    all_to_all x1, starting transfers between devices, per_device(): lax.all_to_all(sent, 'expert', 0, 0, tiled=True).reshape(owners, queries)  16.6 us
    ppermute x3, waiting for transfers between devices, halve_over_dp(): value = keep + lax.ppermute(give, 'dp', [(d, d ^ bit) for d in range(size)])  15.5 us
    all_to_all x2, starting transfers between devices, exchange(): lax.all_to_all(value.reshape(owners, BLOCK, shape[1]), 'expert', 0, 0, ti...  12.7 us
    unnamed x25, local copies, waits for them, and re-layouts  10.1 us
    pallas_call x1, Pallas kernels, per_device(): pl.pallas_call(backward_kernel, out_shape=jax.ShapeDtypeStruct((total, SE...  9.49 us
    all_to_all x1, waiting for transfers between devices, per_device(): lax.all_to_all(sent, 'expert', 0, 0, tiled=True).reshape(owners, queries)  8.83 us
  transfers between devices with their start and end apart: 7, of which 7 were waited for; matrix products, arithmetic and copies ran while one was open for 1% of the time, Pallas kernels for 4%

profile of v2, /device:TPU:6, one launch (start us, length us, event | category | flops | bytes accessed | tf_op | source)
XLA Modules:
  0.0 194.3 jit_solution(13159477749293914412)
XLA Ops:
  6.6 1.6 copy-done
  8.1 1.7 fusion.15
  10.7 16.6 %all-to-all-start = ((f32[64,1,512]{2,1,0:T(1,128)}), f32[64,1,512]{2,1,0:T(1,128)S(1)}, u32[]{:S(2)}, u32[]{:S(2)}) async-start(f32[64,1,512]{2,1,0:T(1,128)} %broadcast_in_dim.28), calls=%async_computation | async-start | bytes 262144 | tf_op jit(solution)/shard_map/all_to_all | solution.py:307
  27.4 1.5 dispatch.1
  28.9 1.2 copy-done.5
  31.2 8.8 %all-to-all-done = f32[64,1,512]{2,1,0:T(1,128)S(1)} async-done(((f32[64,1,512]{2,1,0:T(1,128)}), f32[64,1,512]{2,1,0:T(1,128)S(1)}, u32[]{:S(2)}, u32[]{:S(2)}) %all-to-all-start) | async-done | bytes 131104 | tf_op jit(solution)/shard_map/all_to_all | solution.py:307
  40.0 5.5 %all-to-all-start.2 = ((bf16[64,8,1536]{2,1,0:T(8,128)(2,1)}), bf16[64,8,1536]{2,1,0:T(8,128)(2,1)}, u32[]{:S(2)}, u32[]{:S(2)}) async-start(bf16[64,8,1536]{2,1,0:T(8,128)(2,1)} %bitcast.41), calls=%async_computation.2 | async-start | bytes 3145728 | tf_op jit(solution)/shard_map/all_to_all | solution.py:321
  46.3 1.9 collective-permute-start
  48.2 1.6 collective-permute-done
  50.9 2.7 %collective-permute-start.1 = (f32[2,8,2048]{2,1,0:T(8,128)S(1)}, f32[2,8,2048]{2,1,0:T(8,128)S(1)}, u32[]{:S(2)}, u32[]{:S(2)}) collective-permute-start(f32[2,8,2048]{2,1,0:T(8,128)S(1)} %dynamic-slice_bitcast_fusion.1), channel_id=1, source_target_pairs={{0,128},{64,192},{128,0},{192,64},{256,384},{320,448},{384,256},{4... | collective-permute-start | bytes 393224 | tf_op jit(solution)/shard_map/ppermute | solution.py:254
  53.6 8.0 %collective-permute-done.1 = f32[2,8,2048]{2,1,0:T(8,128)S(1)} collective-permute-done((f32[2,8,2048]{2,1,0:T(8,128)S(1)}, f32[2,8,2048]{2,1,0:T(8,128)S(1)}, u32[]{:S(2)}, u32[]{:S(2)}) %collective-permute-start.1) | collective-permute-done | bytes 131104 | tf_op jit(solution)/shard_map/ppermute | solution.py:254
  61.7 3.3 %collective-permute-start.2 = (f32[1,8,2048]{2,1,0:T(8,128)S(1)}, f32[1,8,2048]{2,1,0:T(8,128)S(1)}, u32[]{:S(2)}, u32[]{:S(2)}) collective-permute-start(f32[1,8,2048]{2,1,0:T(8,128)S(1)} %constant_dynamic-slice_fusion), channel_id=1, source_target_pairs={{0,256},{64,320},{128,384},{192,448},{256,0},{320,64},{384,128},{4... | collective-permute-start | bytes 196616 | tf_op jit(solution)/shard_map/ppermute | solution.py:254
  65.1 5.9 %collective-permute-done.2 = f32[1,8,2048]{2,1,0:T(8,128)S(1)} collective-permute-done((f32[1,8,2048]{2,1,0:T(8,128)S(1)}, f32[1,8,2048]{2,1,0:T(8,128)S(1)}, u32[]{:S(2)}, u32[]{:S(2)}) %collective-permute-start.2) | collective-permute-done | bytes 65568 | tf_op jit(solution)/shard_map/ppermute | solution.py:254
  71.0 1.4 cotangent.1
  73.6 11.9 %all-to-all-done.2 = bf16[64,8,1536]{2,1,0:T(8,128)(2,1)} async-done(((bf16[64,8,1536]{2,1,0:T(8,128)(2,1)}), bf16[64,8,1536]{2,1,0:T(8,128)(2,1)}, u32[]{:S(2)}, u32[]{:S(2)}) %all-to-all-start.2) | async-done | bytes 1572896 | tf_op jit(solution)/shard_map/all_to_all | solution.py:321
  85.4 7.2 %all-to-all-start.1 = ((bf16[64,8,1536]{2,1,0:T(8,128)(2,1)}), bf16[64,8,1536]{2,1,0:T(8,128)(2,1)}, u32[]{:S(2)}, u32[]{:S(2)}) async-start(bf16[64,8,1536]{2,1,0:T(8,128)(2,1)} %bitcast.36), calls=%async_computation.1 | async-start | bytes 3145728 | tf_op jit(solution)/shard_map/all_to_all | solution.py:321
  92.6 1.3 all-gather.2.cloned.1.call-done.weights_ref.weights_hbm
  93.9 3.7 %copy-done.1 = bf16[2048,2304]{1,0:T(8,128)(2,1)S(1)} copy-done((bf16[2048,2304]{1,0:T(8,128)(2,1)S(1)}, bf16[2048,2304]{1,0:T(8,128)(2,1)}, u32[]{:S(2)}) %copy-start.1) | copy-done | bytes 9437208
  97.6 4.7 %expert_forward.1.factor_hbm = f32[384,1536]{1,0:T(8,128)S(1)} custom-call(bf16[512,1536]{1,0:T(8,128)(2,1)} %bitcast.17.block_ref, bf16[2048,2304]{1,0:T(8,128)(2,1)S(1)} %copy-done.1), custom_call_target="tpu_custom_call" | custom-call | tf_op jit(solution)/shard_map/expert_forward/pallas_call | solution.py:339
  102.3 1.4 copy-done.2
  103.7 27.3 %all-to-all-done.1 = bf16[64,8,1536]{2,1,0:T(8,128)(2,1)} async-done(((bf16[64,8,1536]{2,1,0:T(8,128)(2,1)}), bf16[64,8,1536]{2,1,0:T(8,128)(2,1)}, u32[]{:S(2)}, u32[]{:S(2)}) %all-to-all-start.1) | async-done | bytes 1572896 | tf_op jit(solution)/shard_map/all_to_all | solution.py:321
  131.0 9.5 %expert_backward.1 = bf16[512,1536]{1,0:T(8,128)(2,1)S(1)} custom-call(bf16[512,1536]{1,0:T(8,128)(2,1)} %bitcast.15.block_hbm, bf16[2048,2304]{1,0:T(8,128)(2,1)} %all-gather.2.cloned.1.call-done.weights_ref.weights_hbm, f32[384,1536]{1,0:T(8,128)} %copy-done.2), custom_call_target="tpu_custom_call" | custom-call | tf_op jit(solution)/shard_map/expert_backward/pallas_call | solution.py:348
  140.5 44.6 %all_to_all.20 = bf16[64,8,1536]{2,1,0:T(8,128)(2,1)S(1)} all-to-all(bf16[64,8,1536]{2,1,0:T(8,128)(2,1)S(1)} %bitcast.38), channel_id=1, replica_groups=mesh['dp'=8,'expert'=64] {'expert'}, dimensions={0} | all-to-all | bytes 3145728 | tf_op jit(solution)/shard_map/all_to_all | solution.py:321
  185.1 2.3 %finish.1 = bf16[128,2048]{1,0:T(8,128)(2,1)} custom-call(bf16[512,1536]{1,0:T(8,128)(2,1)S(1)} %bitcast.37, bf16[128,2048]{1,0:T(8,128)(2,1)S(1)} %bitcast.40, bf16[1,2048]{1,0:T(2,128)(2,1)S(1)} %reshape.73.gain_ref, s32[2,128]{1,0:T(2,128)S(1)} %get-tuple-element.12.q_ref, s32[2,128]{1,0:T(2,128)S(1)} %bitcast.44, ...), custom_call_target="tpu_custom_call" | custom-call | tf_op jit(solution)/shard_map/finish/pallas_call | solution.py:365
  (39 shorter events, 4.9 us)
Async XLA Ops:
  6.5 1.6 copy-start
  6.5 3.3 %copy-start.10 = (s32[512]{0:T(512)S(1)}, s32[512]{0:T(512)}, u32[]{:S(2)}) copy-start(s32[512]{0:T(512)} %param.13) | copy-start | bytes 6148
  6.5 20.8 %copy-start.11 = (bf16[2048]{0:T(1024)(128)(2,1)S(1)}, bf16[2048]{0:T(1024)(128)(2,1)}, u32[]{:S(2)}) copy-start(bf16[2048]{0:T(1024)(128)(2,1)} %param.16) | copy-start | bytes 12292
  6.5 20.8 %copy-start.4 = (bf16[1,128,2048]{2,1,0:T(8,128)(2,1)S(1)}, bf16[1,128,2048]{2,1,0:T(8,128)(2,1)}, u32[]{:S(2)}) copy-start(bf16[1,128,2048]{2,1,0:T(8,128)(2,1)} %param.15) | copy-start | bytes 1572868
  6.5 20.8 %copy-start.9 = (s32[1,128,2]{1,2,0:T(2,128)S(1)}, s32[1,128,2]{1,2,0:T(2,128)}, u32[]{:S(2)}) copy-start(s32[1,128,2]{1,2,0:T(2,128)} %param.17) | copy-start | bytes 3076
  10.7 29.3 %all-to-all-start = ((f32[64,1,512]{2,1,0:T(1,128)}), f32[64,1,512]{2,1,0:T(1,128)S(1)}, u32[]{:S(2)}, u32[]{:S(2)}) async-start(f32[64,1,512]{2,1,0:T(1,128)} %broadcast_in_dim.28), calls=%async_computation | async-start | bytes 262144 | tf_op jit(solution)/shard_map/all_to_all | solution.py:307
  27.3 66.6 %all-gather.2.cloned.1.call-start = ((), (), s32[]{:S(2)}) async-start(), calls=%async_computation.4 | async-start | bytes 10616832 | tf_op jit(solution)/shard_map/all_gather | solution.py:309
  28.9 1.2 copy-start.5
  30.1 1.0 copy-start.6
  40.0 45.4 %all-to-all-start.2 = ((bf16[64,8,1536]{2,1,0:T(8,128)(2,1)}), bf16[64,8,1536]{2,1,0:T(8,128)(2,1)}, u32[]{:S(2)}, u32[]{:S(2)}) async-start(bf16[64,8,1536]{2,1,0:T(8,128)(2,1)} %bitcast.41), calls=%async_computation.2 | async-start | bytes 3145728 | tf_op jit(solution)/shard_map/all_to_all | solution.py:321
  45.7 25.2 %copy-start.7 = (s32[1,1,8]{2,1,0:T(1,128)S(1)}, s32[1,1,8]{2,1,0:T(1,128)}, u32[]{:S(2)}) copy-start(s32[1,1,8]{2,1,0:T(1,128)} %param.14) | copy-start | bytes 100
  46.3 3.6 %collective-permute-start = (f32[4,8,2048]{2,1,0:T(8,128)S(1)}, f32[4,8,2048]{2,1,0:T(8,128)}, u32[]{:S(2)}, u32[]{:S(2)}) collective-permute-start(f32[4,8,2048]{2,1,0:T(8,128)S(1)} %dynamic-slice_bitcast_fusion), channel_id=1, source_target_pairs={{0,64},{64,0},{128,192},{192,128},{256,320},{320,256},{384,448},{4... | collective-permute-start | bytes 786440 | tf_op jit(solution)/shard_map/ppermute | solution.py:254
  50.9 10.8 %collective-permute-start.1 = (f32[2,8,2048]{2,1,0:T(8,128)S(1)}, f32[2,8,2048]{2,1,0:T(8,128)S(1)}, u32[]{:S(2)}, u32[]{:S(2)}) collective-permute-start(f32[2,8,2048]{2,1,0:T(8,128)S(1)} %dynamic-slice_bitcast_fusion.1), channel_id=1, source_target_pairs={{0,128},{64,192},{128,0},{192,64},{256,384},{320,448},{384,256},{4... | collective-permute-start | bytes 393224 | tf_op jit(solution)/shard_map/ppermute | solution.py:254
  61.7 9.2 %collective-permute-start.2 = (f32[1,8,2048]{2,1,0:T(8,128)S(1)}, f32[1,8,2048]{2,1,0:T(8,128)S(1)}, u32[]{:S(2)}, u32[]{:S(2)}) collective-permute-start(f32[1,8,2048]{2,1,0:T(8,128)S(1)} %constant_dynamic-slice_fusion), channel_id=1, source_target_pairs={{0,256},{64,320},{128,384},{192,448},{256,0},{320,64},{384,128},{4... | collective-permute-start | bytes 196616 | tf_op jit(solution)/shard_map/ppermute | solution.py:254
  72.4 1.1 copy-start.3
  85.4 45.6 %all-to-all-start.1 = ((bf16[64,8,1536]{2,1,0:T(8,128)(2,1)}), bf16[64,8,1536]{2,1,0:T(8,128)(2,1)}, u32[]{:S(2)}, u32[]{:S(2)}) async-start(bf16[64,8,1536]{2,1,0:T(8,128)(2,1)} %bitcast.36), calls=%async_computation.1 | async-start | bytes 3145728 | tf_op jit(solution)/shard_map/all_to_all | solution.py:321
  93.9 3.7 %copy-start.1 = (bf16[2048,2304]{1,0:T(8,128)(2,1)S(1)}, bf16[2048,2304]{1,0:T(8,128)(2,1)}, u32[]{:S(2)}) copy-start(bf16[2048,2304]{1,0:T(8,128)(2,1)} %all-gather.2.cloned.1.call-done.weights_ref.weights_hbm) | copy-start | bytes 28311556
  102.3 1.4 copy-start.2
  140.5 44.7 %copy-start.8 = (s32[1,128,2]{1,2,0:T(2,128)S(1)}, s32[1,128,2]{1,2,0:T(2,128)}, u32[]{:S(2)}) copy-start(s32[1,128,2]{1,2,0:T(2,128)} %param.18) | copy-start | bytes 3076
Sparse Core Ops, SparseCore 0:
  40.2 53.6 all-gather.1

commit v3 on v2

v3 whole, which is shorter than its diff:
```python
import functools
import jax
import jax.numpy as jnp
from jax import lax
from jax.experimental import pallas as pl
from jax.experimental.pallas import tpu as pltpu
from jax.sharding import PartitionSpec as P

SCORE_SCALE = 20.0
GRAD_SCALE = 2560.0
EPSILON = 1e-06
BF = jnp.bfloat16
F32 = jnp.float32

SLOTS = 6
BLOCK = 8
SECTION = 512
SECTIONS = 3
BLOCK_WIDTH = SECTIONS * SECTION
LANES = 128
PIECES = 4


def iota(shape, dim):
    return lax.broadcasted_iota(jnp.int32, shape, dim)


def dot(a, b):
    return jnp.dot(a, b, preferred_element_type=F32)


def dot_first(a, b):
    return lax.dot_general(a, b, (((0,), (0,)), ((), ())), preferred_element_type=F32)


def dot_last(a, b):
    return lax.dot_general(a, b, (((1,), (1,)), ((), ())), preferred_element_type=F32)


def section(k):
    return slice(k * SECTION, (k + 1) * SECTION)


def tail_row(q, k):
    rank = jnp.bitwise_and(q, BLOCK - 1)
    high = (rank >= 3).astype(jnp.int32)
    return jnp.where(rank - 3 * high == k, q - rank + SLOTS + high, -1)


def picks(rows, q, first, second):
    r = iota((rows, q.shape[1]), 0)
    zero = jnp.zeros((), F32)
    return (jnp.where(r == q[0:1], first, zero) + jnp.where(r == q[1:2], second, zero)).astype(BF)


def pack_rows(rows_ref, q, stage_ref, out_hbm, sems):
    total = stage_ref.shape[0]
    main = picks(total, q, 1.0, 1.0)
    tail = rows_ref[:, section(SECTIONS)]
    copies = []
    for k in range(SECTIONS):
        left = jnp.concatenate([main, picks(total, tail_row(q, k), 1.0, 1.0)], axis=1)
        right = jnp.concatenate([rows_ref[:, section(k)], tail], axis=0)
        stage_ref[:, section(k)] = dot(left, right).astype(BF)
        copies.append(
            pltpu.make_async_copy(stage_ref.at[:, section(k)], out_hbm.at[:, section(k)], sems.at[k])
        )
        copies[-1].start()
    return copies


def inverse_rms(stream):
    return lax.rsqrt(jnp.mean(stream * stream, axis=-1, keepdims=True) + EPSILON)


def dispatch_kernel(
    owner_ref,
    residual_ref,
    gain_ref,
    ids_ref,
    code_ref,
    positives_ref,
    query_hbm,
    w0_hbm,
    w1_hbm,
    w2_hbm,
    out_hbm,
    scores_hbm,
    q_ref,
    top_ref,
    rest_ref,
    joined_ref,
    query_ref,
    scores_ref,
    normed_ref,
    stage_ref,
    sems,
    *,
    experts,
):
    hidden, columns = w0_hbm.shape[1], code_ref.shape[0]
    parts = [slice(c * LANES, (c + 1) * LANES) for c in range(PIECES)]
    queries = [
        pltpu.make_async_copy(query_hbm.at[part], query_ref.at[part], sems.at[c])
        for c, part in enumerate(parts)
    ]
    for copy in queries:
        copy.start()
    copies = [
        pltpu.make_async_copy(w_hbm, joined_ref.at[:, k * hidden : (k + 1) * hidden], sems.at[PIECES + k])
        for k, w_hbm in enumerate((w0_hbm, w1_hbm, w2_hbm))
    ]
    for copy in copies:
        copy.start()
    stream = residual_ref[...].astype(F32)
    normed_ref[...] = (stream * inverse_rms(stream) * gain_ref[...].astype(F32)).astype(BF)
    ids = jnp.concatenate([ids_ref[0:1, :], ids_ref[1:2, :]], axis=1)
    count = ids.shape[1]
    table = (iota((experts, count), 0) == ids).astype(F32)
    earlier = dot(
        table.astype(BF), (iota((count, count), 0) < iota((count, count), 1)).astype(F32).astype(BF)
    )
    rank = jnp.sum(table * earlier, axis=0, keepdims=True).astype(jnp.int32)
    q_flat = ids * BLOCK + rank
    half = count // 2
    q = jnp.concatenate([q_flat[:, :half], q_flat[:, half:]], axis=0)
    q_ref[...] = q
    copies += pack_rows(normed_ref, q, stage_ref, out_hbm, sems.at[PIECES + 3 : PIECES + 3 + SECTIONS])
    column = owner_ref[0] * columns + iota((columns, 1), 0)
    high, low = [], []
    for copy, part in zip(queries, parts):
        copy.wait()
        scores = dot_last(code_ref[...], query_ref[part, :]) * SCORE_SCALE
        scores_ref[:, part] = scores
        top = jnp.max(scores, axis=0, keepdims=True)
        exponent = jnp.exp(scores - top)
        top_ref[:, part] = top
        rest_ref[:, part] = jnp.sum(
            jnp.where(positives_ref[:, part] == column, 0.0, exponent), axis=0, keepdims=True
        )
        log_sum = top + jnp.log(jnp.sum(exponent, axis=0, keepdims=True))
        high.append(log_sum.astype(BF).astype(F32))
        low.append(log_sum - high[-1])
    pieces = jnp.concatenate(high + low, axis=0)
    stage_ref[:, BLOCK_WIDTH:] = jnp.concatenate([pieces] * experts, axis=0).astype(BF)
    first = PIECES + 3 + SECTIONS
    copies += [
        pltpu.make_async_copy(stage_ref.at[:, BLOCK_WIDTH:], out_hbm.at[:, BLOCK_WIDTH:], sems.at[first]),
        pltpu.make_async_copy(scores_ref, scores_hbm, sems.at[first + 1]),
    ]
    for copy in copies[-2:]:
        copy.start()
    for copy in copies:
        copy.wait()


def weights_kernel(
    block_ref,
    owner_ref,
    top_ref,
    rest_ref,
    positives_ref,
    scores_hbm,
    query_hbm,
    _left_hbm,
    _right_hbm,
    out_ref,
    pieces_ref,
    code_weights_ref,
    scores_ref,
    query_ref,
    sems,
):
    copies = [
        pltpu.make_async_copy(scores_hbm, scores_ref, sems.at[0]),
        pltpu.make_async_copy(query_hbm, query_ref, sems.at[1]),
    ]
    for copy in copies:
        copy.start()
    pieces_ref[...] = block_ref[:, BLOCK_WIDTH:].astype(F32)
    peers, columns = block_ref.shape[0] // BLOCK, scores_ref.shape[0]
    owner = owner_ref[0]
    own = iota((peers, 1), 0) == owner
    column = owner * columns + iota((columns, 1), 0)
    copies[0].wait()
    for c in range(PIECES):
        lanes = slice(c * LANES, (c + 1) * LANES)
        sums = (
            pieces_ref[pl.ds(c, peers, stride=BLOCK), :]
            + pieces_ref[pl.ds(PIECES + c, peers, stride=BLOCK), :]
        )
        row_top = jnp.max(sums, axis=0, keepdims=True)
        shares = jnp.exp(sums - row_top)
        total = jnp.sum(shares, axis=0, keepdims=True)
        rest = jnp.sum(jnp.where(own, 0.0, shares), axis=0, keepdims=True)
        rest = rest + rest_ref[:, lanes] * jnp.exp(top_ref[:, lanes] - row_top)
        part = jnp.where(positives_ref[:, lanes] == column, -rest, jnp.exp(scores_ref[:, lanes] - row_top))
        code_weights_ref[:, lanes] = (part * (GRAD_SCALE / total)).astype(BF)
    copies[1].wait()
    out_ref[...] = dot(code_weights_ref[...], query_ref[...]).astype(BF)


def cotangent_kernel(parts_ref, lengths_ref, q_ref, out_hbm, token_hbm, token_ref, stage_ref, sems):
    files, tokens = lengths_ref.shape[1], token_ref.shape[0]
    row, position = iota((files, 1), 0), iota((1, tokens), 1)
    length = jnp.zeros((files, 1), jnp.int32)
    segment = jnp.zeros((1, tokens), jnp.int32)
    end = jnp.int32(0)
    for f in range(files):
        length = jnp.where(row == f, lengths_ref[0, f], length)
        end = end + lengths_ref[0, f]
        segment = segment + (position >= end).astype(jnp.int32)
    code_grad = parts_ref[0:files, :].astype(F32)
    for part in range(1, parts_ref.shape[0] // files):
        code_grad = code_grad + parts_ref[part * files : (part + 1) * files, :].astype(F32)
    file_cot = (code_grad / length.astype(F32)).astype(BF)
    member = (iota((files, tokens), 0) == segment).astype(F32).astype(BF)
    token_ref[...] = dot_first(member, file_cot).astype(BF)
    keep = pltpu.make_async_copy(token_ref, token_hbm, sems.at[SECTIONS])
    keep.start()
    for copy in pack_rows(token_ref, q_ref[...], stage_ref, out_hbm, sems.at[0:SECTIONS]):
        copy.wait()
    keep.wait()


def halves(total):
    return 2 if total % 512 == 0 else 1


def unpack_blocks(block_ref, rows_ref):
    parts = halves(block_ref.shape[0])
    height = block_ref.shape[0] // parts
    wide = height // BLOCK * SLOTS
    i, r = iota((wide, height), 0), iota((wide, height), 1)
    peer, j = r >> 3, r & (BLOCK - 1)
    main = ((i == peer * SLOTS + j) & (j < SLOTS)).astype(F32).astype(BF)
    for g in range(parts):
        rows = slice(g * wide, (g + 1) * wide)
        tail = jnp.zeros((wide, SECTION), F32)
        for k in range(SECTIONS):
            last = ((i == peer * SLOTS + (j - SLOTS) * 3 + k) & (j >= SLOTS)).astype(F32).astype(BF)
            both = dot(
                jnp.concatenate([main, last], axis=0),
                block_ref[g * height : (g + 1) * height, section(k)],
            )
            rows_ref[rows, section(k)] = both[:wide].astype(BF)
            tail = tail + both[wide:]
        rows_ref[rows, section(SECTIONS)] = tail.astype(BF)


def pack_blocks(rows_ref, block_ref):
    parts = halves(block_ref.shape[0])
    height = block_ref.shape[0] // parts
    wide = height // BLOCK * SLOTS
    r, i = iota((height, wide), 0), iota((height, wide), 1)
    peer, j = r >> 3, r & (BLOCK - 1)
    main = ((i == peer * SLOTS + j) & (j < SLOTS)).astype(F32).astype(BF)
    for g in range(parts):
        rows = slice(g * wide, (g + 1) * wide)
        tail = rows_ref[rows, section(SECTIONS)]
        for k in range(SECTIONS):
            last = ((i == peer * SLOTS + (j - SLOTS) * 3 + k) & (j >= SLOTS)).astype(F32).astype(BF)
            block_ref[g * height : (g + 1) * height, section(k)] = (
                dot(main, rows_ref[rows, section(k)]) + dot(last, tail)
            ).astype(BF)


def place_weights(shards, order_ref, weights_ref, columns, sems, first):
    copies = []
    for n, shard in enumerate(shards):
        rows = pl.ds(pl.multiple_of(order_ref[n], LANES), shard.shape[0])
        copies.append(
            pltpu.make_async_copy(
                shard.at[:, columns], weights_ref.at[rows, columns], sems.at[first + n]
            )
        )
    return copies


def forward_kernel(order_ref, block_ref, *refs):
    *shards, factor_ref, weights_ref, rows_ref, sems = refs
    hidden = factor_ref.shape[1] // 2
    copies = place_weights(shards, order_ref, weights_ref, slice(0, 2 * hidden), sems, 0)
    for copy in copies:
        copy.start()
    unpack_blocks(block_ref, rows_ref)
    for copy in copies:
        copy.wait()
    gate_pre = dot(rows_ref[...], weights_ref[:, :hidden])
    up_pre = dot(rows_ref[...], weights_ref[:, hidden:])
    s = jax.nn.sigmoid(gate_pre)
    factor_ref[:, :hidden] = up_pre * s * (1.0 + gate_pre * (1.0 - s))
    factor_ref[:, hidden:] = gate_pre * s


def backward_kernel(order_ref, block_hbm, factor_hbm, *refs):
    *shards, out_ref, block_ref, weights_ref, factor_ref, rows_ref, hidden_ref, sems = refs
    hidden = factor_ref.shape[1] // 2
    parts = halves(block_ref.shape[0])
    height = block_ref.shape[0] // parts
    first = [
        pltpu.make_async_copy(
            block_hbm.at[g * height : (g + 1) * height], block_ref.at[g * height : (g + 1) * height], sems.at[g]
        )
        for g in range(parts)
    ]
    down = place_weights(shards, order_ref, weights_ref, slice(2 * hidden, 3 * hidden), sems, parts)
    factor = pltpu.make_async_copy(factor_hbm, factor_ref, sems.at[parts + len(shards)])
    rest = place_weights(
        shards, order_ref, weights_ref, slice(0, 2 * hidden), sems, parts + len(shards) + 1
    )
    for copy in (*first, *down, factor, *rest):
        copy.start()
    for copy in first:
        copy.wait()
    unpack_blocks(block_ref, rows_ref)
    for copy in down:
        copy.wait()
    back = dot(rows_ref[...], weights_ref[:, 2 * hidden :])
    factor.wait()
    hidden_ref[:, :hidden] = (back * factor_ref[:, :hidden]).astype(BF)
    hidden_ref[:, hidden:] = (back * factor_ref[:, hidden:]).astype(BF)
    for copy in rest:
        copy.wait()
    for k in range(SECTIONS + 1):
        rows_ref[:, section(k)] = dot_last(
            hidden_ref[...], weights_ref[section(k), : 2 * hidden]
        ).astype(BF)
    pack_blocks(rows_ref, out_ref)


def finish_kernel(
    block_ref, residual_ref, gain_ref, q_ref, units_ref, token_ref, out_ref, grad_ref
):
    total, q = block_ref.shape[0], q_ref[...]
    gates = units_ref[...].astype(F32) * (1.0 / 256.0)
    first, second = gates[0:1], gates[1:2]
    tokens = q.shape[1]
    main = picks(total, q, first, second)
    tail = jnp.zeros((tokens, SECTION), F32)
    for k in range(SECTIONS):
        both = dot_first(
            jnp.concatenate([main, picks(total, tail_row(q, k), first, second)], axis=1),
            block_ref[:, section(k)],
        )
        grad_ref[:, section(k)] = both[:tokens]
        tail = tail + both[tokens:]
    grad_ref[:, section(SECTIONS)] = tail
    stream = residual_ref[...].astype(F32)
    root = inverse_rms(stream)
    scaled = gain_ref[...].astype(F32) * grad_ref[...]
    correction = jnp.mean(scaled * stream, axis=-1, keepdims=True)
    cot = token_ref[...].astype(F32)
    out_ref[...] = (cot + root * scaled - stream * (root * root * root * correction)).astype(BF)


def params(mib):
    return pltpu.CompilerParams(vmem_limit_bytes=mib << 20)


IN_SMEM = pl.BlockSpec(memory_space=pltpu.SMEM)
IN_VMEM = pl.BlockSpec(memory_space=pltpu.VMEM)
IN_HBM = pl.BlockSpec(memory_space=pltpu.HBM)


def hbm(value):
    return pltpu.with_memory_space_constraint(value, pltpu.HBM)


def per_device(
    query_reps,
    code_reps,
    positives,
    file_lengths,
    residual,
    norm_gain,
    expert_ids,
    gate_units,
    w_gate,
    w_up,
    w_down,
):
    owners = lax.axis_size("expert")
    columns = code_reps.shape[0]
    queries, width = query_reps.shape
    files = file_lengths.shape[2]
    tokens = residual.shape[1]
    hidden = w_gate.shape[2]
    total = owners * BLOCK
    lengths = file_lengths.reshape(1, files)
    stream = residual[0]
    gain = norm_gain.reshape(1, width)
    ids = expert_ids[0].T
    units = gate_units[0].T

    owner = lax.axis_index("expert")[None]

    def exchange(value):
        shape = value.shape
        return lax.all_to_all(
            value.reshape(owners, BLOCK, shape[1]), "expert", 0, 0, tiled=True
        ).reshape(shape)

    blocks, scores, q, local_top, local_rest, joined = pl.pallas_call(
        functools.partial(dispatch_kernel, experts=owners),
        out_shape=(
            pltpu.HBM((total, BLOCK_WIDTH + LANES), BF),
            pltpu.HBM((columns, queries), F32),
            jax.ShapeDtypeStruct((2, tokens), jnp.int32),
            jax.ShapeDtypeStruct((1, queries), F32),
            jax.ShapeDtypeStruct((1, queries), F32),
            jax.ShapeDtypeStruct((w_gate.shape[1], 3 * hidden), BF),
        ),
        in_specs=[IN_SMEM] + [IN_VMEM] * 5 + [IN_HBM] * 4,
        out_specs=(IN_HBM, IN_HBM) + (IN_VMEM,) * 4,
        scratch_shapes=[
            pltpu.VMEM((queries, width), BF),
            pltpu.VMEM((columns, queries), F32),
            pltpu.VMEM((tokens, width), BF),
            pltpu.VMEM((total, BLOCK_WIDTH + LANES), BF),
            pltpu.SemaphoreType.DMA((PIECES + 5 + SECTIONS,)),
        ],
        compiler_params=params(16),
        name="dispatch",
    )(
        owner,
        stream,
        gain,
        ids,
        code_reps,
        positives[None],
        hbm(query_reps),
        hbm(w_gate[0]),
        hbm(w_up[0]),
        hbm(w_down[0]),
    )
    size = lax.axis_size("dp")
    me = lax.axis_index("dp")
    half = joined.shape[0] // 2

    def ahead(value, step):
        return lax.ppermute(value, "dp", [(d, (d + step) % size) for d in range(size)])

    def partner(value):
        return lax.ppermute(value, "dp", [(d, d ^ 1) for d in range(size)])

    from_left, from_right = ahead(joined, 2), ahead(joined, size - 2)
    blocks = exchange(blocks)
    parts = pl.pallas_call(
        weights_kernel,
        out_shape=jax.ShapeDtypeStruct((columns, width), BF),
        in_specs=[IN_VMEM, IN_SMEM] + [IN_VMEM] * 3 + [IN_HBM] * 4,
        out_specs=IN_VMEM,
        scratch_shapes=[
            pltpu.VMEM((total, LANES), F32),
            pltpu.VMEM((columns, queries), BF),
            pltpu.VMEM((columns, queries), F32),
            pltpu.VMEM((queries, width), BF),
            pltpu.SemaphoreType.DMA((2,)),
        ],
        compiler_params=params(12),
        name="code_weights",
    )(
        blocks,
        owner,
        local_top,
        local_rest,
        positives[None],
        hbm(scores),
        hbm(query_reps),
        hbm(from_left),
        hbm(from_right),
    )
    parts = lax.all_to_all(
        parts.reshape(columns // files, files, width), "dp", 0, 0, tiled=True
    ).reshape(columns, width)
    cot_blocks, token_cot = pl.pallas_call(
        cotangent_kernel,
        out_shape=(
            pltpu.HBM((total, BLOCK_WIDTH), BF),
            pltpu.HBM((tokens, width), BF),
        ),
        in_specs=[IN_VMEM, IN_SMEM, IN_VMEM],
        out_specs=(IN_HBM, IN_HBM),
        scratch_shapes=[
            pltpu.VMEM((tokens, width), BF),
            pltpu.VMEM((total, BLOCK_WIDTH), BF),
            pltpu.SemaphoreType.DMA((SECTIONS + 1,)),
        ],
        compiler_params=params(12),
        name="cotangent",
    )(parts, lengths, q)
    cot_blocks = exchange(cot_blocks)
    joined, from_left, from_right, _ = lax.optimization_barrier((joined, from_left, from_right, parts))
    shards = [
        joined,
        from_left,
        from_right,
        ahead(from_left[:half], 2),
        ahead(from_right[half:], size - 2),
    ]
    shards = [hbm(shard) for shard in shards + [partner(shard) for shard in shards]]
    height = joined.shape[0]
    order = jnp.stack(
        [
            jnp.bitwise_and(d + step, size - 1) * height + start
            for d in (me, me ^ 1)
            for step, start in ((0, 0), (size - 2, 0), (2, 0), (4, 0), (4, half))
        ]
    ).astype(jnp.int32)

    rows = owners * SLOTS
    factor = pl.pallas_call(
        forward_kernel,
        out_shape=jax.ShapeDtypeStruct((rows, 2 * hidden), F32),
        in_specs=[IN_SMEM, IN_VMEM] + [IN_HBM] * len(shards),
        out_specs=IN_VMEM,
        scratch_shapes=[
            pltpu.VMEM((width, 2 * hidden), BF),
            pltpu.VMEM((rows, width), BF),
            pltpu.SemaphoreType.DMA((len(shards),)),
        ],
        compiler_params=params(24),
        name="expert_forward",
    )(order, blocks, *shards)
    result = pl.pallas_call(
        backward_kernel,
        out_shape=jax.ShapeDtypeStruct((total, BLOCK_WIDTH), BF),
        in_specs=[IN_SMEM] + [IN_HBM] * (2 + len(shards)),
        out_specs=IN_VMEM,
        scratch_shapes=[
            pltpu.VMEM((total, BLOCK_WIDTH), BF),
            pltpu.VMEM((width, 3 * hidden), BF),
            pltpu.VMEM((rows, 2 * hidden), F32),
            pltpu.VMEM((rows, width), BF),
            pltpu.VMEM((rows, 2 * hidden), BF),
            pltpu.SemaphoreType.DMA((halves(total) + 2 * len(shards) + 1,)),
        ],
        compiler_params=params(32),
        name="expert_backward",
    )(order, hbm(cot_blocks), hbm(factor), *shards)

    token_grad = pl.pallas_call(
        finish_kernel,
        out_shape=jax.ShapeDtypeStruct((tokens, width), BF),
        in_specs=[IN_VMEM] * 6,
        out_specs=IN_VMEM,
        scratch_shapes=[pltpu.VMEM((tokens, width), F32)],
        compiler_params=params(12),
        name="finish",
    )(exchange(result), stream, gain, q, units, token_cot)
    return token_grad[None]


def solution(mesh):
    return jax.shard_map(
        per_device,
        mesh=mesh,
        in_specs=(
            P("dp", None),
            P("expert", None),
            P("dp"),
            P("expert", "dp", None),
            P("expert", "dp", None),
            P(),
            P("expert", "dp", None),
            P("expert", "dp", None),
            P("expert", "dp", None),
            P("expert", "dp", None),
            P("expert", "dp", None),
        ),
        out_specs=P("expert", "dp", None),
        check_vma=False,
    )
```

time: 195 us -> 194 us (level)
  the two profiles are of different devices: /device:TPU:6 before, /device:TPU:8 now
where the time goes in v3:
time: 194 us; the launch traced here: 193 us
  blocking collectives  59.9 us (31%)
  waiting for transfers between devices  51.2 us (26%)
  starting transfers between devices  47.5 us (24%)
  Pallas kernels  26.7 us (14%)
  local copies, waits for them, and re-layouts  7.81 us (4%)
    all_to_all x1, blocking collectives, exchange(): lax.all_to_all(value.reshape(owners, BLOCK, shape[1]), 'expert', 0, 0, ti...  48.3 us
    ppermute x4, waiting for transfers between devices, ahead(): lax.ppermute(value, 'dp', [(d, (d + step) % size) for d in range(size)])  34.2 us
    all_to_all x2, starting transfers between devices, exchange(): lax.all_to_all(value.reshape(owners, BLOCK, shape[1]), 'expert', 0, 0, ti...  24.8 us
    all_to_all x2, waiting for transfers between devices, exchange(): lax.all_to_all(value.reshape(owners, BLOCK, shape[1]), 'expert', 0, 0, ti...  14.9 us
    ppermute x4, starting transfers between devices, ahead(): lax.ppermute(value, 'dp', [(d, (d + step) % size) for d in range(size)])  12.4 us
    all_to_all x1, blocking collectives, per_device(): lax.all_to_all(parts.reshape(columns // files, files, width), 'dp', 0, 0,...  11.6 us
    ppermute x5, starting transfers between devices, partner(): return lax.ppermute(value, 'dp', [(d, d ^ 1) for d in range(size)])  10.3 us
    pallas_call x1, Pallas kernels, per_device(): pl.pallas_call(backward_kernel, out_shape=jax.ShapeDtypeStruct((total, BL...  9.86 us
  transfers between devices with their start and end apart: 11, of which 7 were waited for; matrix products, arithmetic and copies ran while one was open for 1% of the time, Pallas kernels for 3%

profile of v3, /device:TPU:8, one launch (start us, length us, event | category | flops | bytes accessed | tf_op | source)
XLA Modules:
  0.0 193.4 jit_solution(11420719549620281431)
XLA Ops:
  4.0 4.0 %dispatch.1 = (bf16[512,1664]{1,0:T(8,128)(2,1)}, f32[64,512]{1,0:T(8,128)}, s32[2,128]{1,0:T(2,128)S(1)}, f32[1,512]{1,0:T(1,128)S(1)}, f32[1,512]{1,0:T(1,128)S(1)}, /*index=5*/bf16[256,2304]{1,0:T(8,128)(2,1)S(1)}) custom-call(s32[1]{0:T(128)} %bitcast.10.owner_ref, bf16[128,2048]{1,0:T(8,128)(2,1)S(1)} %bitcast.36, ...), custom_call_target="tpu_custom_call" | custom-call | tf_op jit(solution)/shard_map/dispatch/pallas_call | solution.py:404
  8.0 16.7 %all-to-all-start = ((bf16[64,8,1664]{2,1,0:T(8,128)(2,1)}), bf16[64,8,1664]{2,1,0:T(8,128)(2,1)S(1)}, u32[]{:S(2)}, u32[]{:S(2)}) async-start(bf16[64,8,1664]{2,1,0:T(8,128)(2,1)} %bitcast.45), calls=%async_computation | async-start | bytes 3407872 | tf_op jit(solution)/shard_map/all_to_all | solution.py:400
  24.8 4.7 %collective-permute-start.1 = (bf16[256,2304]{1,0:T(8,128)(2,1)S(1)}, bf16[256,2304]{1,0:T(8,128)(2,1)}, u32[]{:S(2)}, u32[]{:S(2)}) collective-permute-start(bf16[256,2304]{1,0:T(8,128)(2,1)S(1)} %get-tuple-element.23.refs_0_), channel_id=1, source_target_pairs={{0,384},{64,448},{128,0},{192,64},{256,128},{320,192},{384,256},{4... | collective-permute-start | bytes 3538952 | tf_op jit(solution)/shard_map/ppermute | solution.py:442
  29.4 1.9 collective-permute-start
  31.4 22.7 %collective-permute-done.1._right_hbm.refs_2_ = bf16[256,2304]{1,0:T(8,128)(2,1)} collective-permute-done((bf16[256,2304]{1,0:T(8,128)(2,1)S(1)}, bf16[256,2304]{1,0:T(8,128)(2,1)}, u32[]{:S(2)}, u32[]{:S(2)}) %collective-permute-start.1) | collective-permute-done | bytes 1179680 | tf_op jit(solution)/shard_map/ppermute | solution.py:442
  54.1 5.4 %collective-permute-done._left_hbm.refs_1_ = bf16[256,2304]{1,0:T(8,128)(2,1)} collective-permute-done((bf16[256,2304]{1,0:T(8,128)(2,1)S(1)}, bf16[256,2304]{1,0:T(8,128)(2,1)}, u32[]{:S(2)}, u32[]{:S(2)}) %collective-permute-start) | collective-permute-done | bytes 1179680 | tf_op jit(solution)/shard_map/ppermute | solution.py:442
  59.5 9.1 %all-to-all-done = bf16[64,8,1664]{2,1,0:T(8,128)(2,1)S(1)} async-done(((bf16[64,8,1664]{2,1,0:T(8,128)(2,1)}), bf16[64,8,1664]{2,1,0:T(8,128)(2,1)S(1)}, u32[]{:S(2)}, u32[]{:S(2)}) %all-to-all-start) | async-done | bytes 1703968 | tf_op jit(solution)/shard_map/all_to_all | solution.py:400
  68.6 2.2 %code_weights.1 = bf16[64,2048]{1,0:T(8,128)(2,1)S(1)} custom-call(bf16[512,1664]{1,0:T(8,128)(2,1)S(1)} %bitcast.32, s32[1]{0:T(128)} %bitcast.10.owner_ref, f32[1,512]{1,0:T(1,128)S(1)} %get-tuple-element.17.top_ref, f32[1,512]{1,0:T(1,128)S(1)} %get-tuple-element.18.rest_ref, s32[1,512]{1,0:T(1,128)S(1)} %bitcast.41, ...), custom_call_target="tpu_custom_call" | custom-call | tf_op jit(solution)/shard_map/code_weights/pallas_call | solution.py:449
  70.8 11.6 %all_to_all.20 = bf16[8,8,2048]{2,1,0:T(8,128)(2,1)S(1)} all-to-all(bf16[8,8,2048]{2,1,0:T(8,128)(2,1)S(1)} %bitcast.38), channel_id=1, replica_groups=mesh['dp'=8,'expert'=64] {'dp'}, dimensions={0} | all-to-all | bytes 524288 | tf_op jit(solution)/shard_map/all_to_all | solution.py:474
  82.4 2.4 %cotangent.1 = (bf16[512,1536]{1,0:T(8,128)(2,1)}, bf16[128,2048]{1,0:T(8,128)(2,1)}) custom-call(bf16[64,2048]{1,0:T(8,128)(2,1)S(1)} %bitcast.39, s32[1,8]{1,0:T(1,128)S(1)} %bitcast.44, s32[2,128]{1,0:T(2,128)S(1)} %get-tuple-element.21.q_ref), custom_call_target="tpu_custom_call" | custom-call | tf_op jit(solution)/shard_map/cotangent/pallas_call | solution.py:477
  84.9 8.1 %all-to-all-start.2 = ((bf16[64,8,1536]{2,1,0:T(8,128)(2,1)}), bf16[64,8,1536]{2,1,0:T(8,128)(2,1)}, u32[]{:S(2)}, u32[]{:S(2)}) async-start(bf16[64,8,1536]{2,1,0:T(8,128)(2,1)} %bitcast.46), calls=%async_computation.2 | async-start | bytes 3145728 | tf_op jit(solution)/shard_map/all_to_all | solution.py:400
  94.1 3.1 %collective-permute-start.3 = (bf16[128,2304]{1,0:T(8,128)(2,1)S(1)}, bf16[128,2304]{1,0:T(8,128)(2,1)S(1)}, u32[]{:S(2)}, u32[]{:S(2)}) collective-permute-start(bf16[128,2304]{1,0:T(8,128)(2,1)S(1)} %slice.7), channel_id=1, source_target_pairs={{0,384},{64,448},{128,0},{192,64},{256,128},{320,192},{384,256},{4... | collective-permute-start | bytes 1769480 | tf_op jit(solution)/shard_map/ppermute | solution.py:442
  98.3 2.8 %collective-permute-start.2 = (bf16[128,2304]{1,0:T(8,128)(2,1)S(1)}, bf16[128,2304]{1,0:T(8,128)(2,1)}, u32[]{:S(2)}, u32[]{:S(2)}) collective-permute-start(bf16[128,2304]{1,0:T(8,128)(2,1)S(1)} %slice.6), channel_id=1, source_target_pairs={{0,128},{64,192},{128,256},{192,320},{256,384},{320,448},{384,0},{... | collective-permute-start | bytes 1769480 | tf_op jit(solution)/shard_map/ppermute | solution.py:442
  101.1 1.9 collective-permute-start.4
  103.0 2.4 %collective-permute-start.5 = (bf16[256,2304]{1,0:T(8,128)(2,1)}, bf16[256,2304]{1,0:T(8,128)(2,1)}, u32[]{:S(2)}, u32[]{:S(2)}) collective-permute-start(bf16[256,2304]{1,0:T(8,128)(2,1)} %collective-permute-done._left_hbm.refs_1_), channel_id=1, source_target_pairs={{0,64},{64,0},{128,192},{192,128},{256,320},{320,256},{384,448},{4... | collective-permute-start | bytes 3538952 | tf_op jit(solution)/shard_map/ppermute | solution.py:445
  105.4 1.9 collective-permute-start.6
  107.3 2.8 %collective-permute-done.3.refs_4_ = bf16[128,2304]{1,0:T(8,128)(2,1)S(1)} collective-permute-done((bf16[128,2304]{1,0:T(8,128)(2,1)S(1)}, bf16[128,2304]{1,0:T(8,128)(2,1)S(1)}, u32[]{:S(2)}, u32[]{:S(2)}) %collective-permute-start.3) | collective-permute-done | bytes 589856 | tf_op jit(solution)/shard_map/ppermute | solution.py:442
  112.0 3.3 %collective-permute-done.2.refs_3_ = bf16[128,2304]{1,0:T(8,128)(2,1)} collective-permute-done((bf16[128,2304]{1,0:T(8,128)(2,1)S(1)}, bf16[128,2304]{1,0:T(8,128)(2,1)}, u32[]{:S(2)}, u32[]{:S(2)}) %collective-permute-start.2) | collective-permute-done | bytes 589856 | tf_op jit(solution)/shard_map/ppermute | solution.py:442
  115.3 2.1 %collective-permute-start.7 = (bf16[128,2304]{1,0:T(8,128)(2,1)}, bf16[128,2304]{1,0:T(8,128)(2,1)}, u32[]{:S(2)}, u32[]{:S(2)}) collective-permute-start(bf16[128,2304]{1,0:T(8,128)(2,1)} %collective-permute-done.2.refs_3_), channel_id=1, source_target_pairs={{0,64},{64,0},{128,192},{192,128},{256,320},{320,256},{384,448},{4... | collective-permute-start | bytes 1769480 | tf_op jit(solution)/shard_map/ppermute | solution.py:445
  117.5 2.0 %collective-permute-done.7.refs_8_ = bf16[128,2304]{1,0:T(8,128)(2,1)} collective-permute-done((bf16[128,2304]{1,0:T(8,128)(2,1)}, bf16[128,2304]{1,0:T(8,128)(2,1)}, u32[]{:S(2)}, u32[]{:S(2)}) %collective-permute-start.7) | collective-permute-done | bytes 589856 | tf_op jit(solution)/shard_map/ppermute | solution.py:445
  119.6 6.6 %expert_forward.1.factor_hbm = f32[384,1536]{1,0:T(8,128)S(1)} custom-call(s32[10]{0:T(128)S(1)} %stack.43.order_ref, bf16[512,1664]{1,0:T(8,128)(2,1)S(1)} %bitcast.33, bf16[256,2304]{1,0:T(8,128)(2,1)} %copy-done.1, bf16[256,2304]{1,0:T(8,128)(2,1)} %collective-permute-done._left_hbm.refs_1_, bf16[256,2304]{1,0:T(8,128)(2,1)} %collective-permute-done.1._right_hbm.refs_2_, ...), custom_call_target="tpu_custom_call" | custom-call | tf_op jit(solution)/shard_map/expert_forward/pallas_call | solution.py:513
  127.6 5.8 %all-to-all-done.2 = bf16[64,8,1536]{2,1,0:T(8,128)(2,1)} async-done(((bf16[64,8,1536]{2,1,0:T(8,128)(2,1)}), bf16[64,8,1536]{2,1,0:T(8,128)(2,1)}, u32[]{:S(2)}, u32[]{:S(2)}) %all-to-all-start.2) | async-done | bytes 1572896 | tf_op jit(solution)/shard_map/all_to_all | solution.py:400
  133.5 9.9 %expert_backward.1 = bf16[512,1536]{1,0:T(8,128)(2,1)S(1)} custom-call(s32[10]{0:T(128)S(1)} %stack.43.order_ref, bf16[512,1536]{1,0:T(8,128)(2,1)} %bitcast.24.block_hbm, f32[384,1536]{1,0:T(8,128)} %copy-done, bf16[256,2304]{1,0:T(8,128)(2,1)} %copy-done.1, bf16[256,2304]{1,0:T(8,128)(2,1)} %collective-permute-done._left_hbm.refs_1_, ...), custom_call_target="tpu_custom_call" | custom-call | tf_op jit(solution)/shard_map/expert_backward/pallas_call | solution.py:526
  143.4 48.3 %all_to_all.21 = bf16[64,8,1536]{2,1,0:T(8,128)(2,1)S(1)} all-to-all(bf16[64,8,1536]{2,1,0:T(8,128)(2,1)S(1)} %bitcast.34), channel_id=1, replica_groups=mesh['dp'=8,'expert'=64] {'expert'}, dimensions={0} | all-to-all | bytes 3145728 | tf_op jit(solution)/shard_map/all_to_all | solution.py:400
  (34 shorter events, 11.4 us)
Async XLA Ops:
  0.7 1.0 copy-start.2
  1.7 0.9 copy-start.5
  2.7 0.7 copy-start.6
  3.4 0.7 copy-start.8
  8.0 93.0 %copy-start.1 = (bf16[256,2304]{1,0:T(8,128)(2,1)}, bf16[256,2304]{1,0:T(8,128)(2,1)S(1)}, u32[]{:S(2)}) copy-start(bf16[256,2304]{1,0:T(8,128)(2,1)S(1)} %get-tuple-element.23.refs_0_) | copy-start | bytes 3538948
  8.0 60.6 %copy-start.7 = (s32[512]{0:T(512)S(1)}, s32[512]{0:T(512)}, u32[]{:S(2)}) copy-start(s32[512]{0:T(512)} %param.13) | copy-start | bytes 6148
  8.0 60.6 %all-to-all-start = ((bf16[64,8,1664]{2,1,0:T(8,128)(2,1)}), bf16[64,8,1664]{2,1,0:T(8,128)(2,1)S(1)}, u32[]{:S(2)}, u32[]{:S(2)}) async-start(bf16[64,8,1664]{2,1,0:T(8,128)(2,1)} %bitcast.45), calls=%async_computation | async-start | bytes 3407872 | tf_op jit(solution)/shard_map/all_to_all | solution.py:400
  24.8 29.3 %collective-permute-start.1 = (bf16[256,2304]{1,0:T(8,128)(2,1)S(1)}, bf16[256,2304]{1,0:T(8,128)(2,1)}, u32[]{:S(2)}, u32[]{:S(2)}) collective-permute-start(bf16[256,2304]{1,0:T(8,128)(2,1)S(1)} %get-tuple-element.23.refs_0_), channel_id=1, source_target_pairs={{0,384},{64,448},{128,0},{192,64},{256,128},{320,192},{384,256},{4... | collective-permute-start | bytes 3538952 | tf_op jit(solution)/shard_map/ppermute | solution.py:442
  29.4 30.1 %collective-permute-start = (bf16[256,2304]{1,0:T(8,128)(2,1)S(1)}, bf16[256,2304]{1,0:T(8,128)(2,1)}, u32[]{:S(2)}, u32[]{:S(2)}) collective-permute-start(bf16[256,2304]{1,0:T(8,128)(2,1)S(1)} %get-tuple-element.23.refs_0_), channel_id=1, source_target_pairs={{0,128},{64,192},{128,256},{192,320},{256,384},{320,448},{384,0},{... | collective-permute-start | bytes 3538952 | tf_op jit(solution)/shard_map/ppermute | solution.py:442
  68.6 13.8 %copy-start.10 = (s32[1,1,8]{2,1,0:T(1,128)S(1)}, s32[1,1,8]{2,1,0:T(1,128)}, u32[]{:S(2)}) copy-start(s32[1,1,8]{2,1,0:T(1,128)} %param.14) | copy-start | bytes 100
  84.9 48.6 %all-to-all-start.2 = ((bf16[64,8,1536]{2,1,0:T(8,128)(2,1)}), bf16[64,8,1536]{2,1,0:T(8,128)(2,1)}, u32[]{:S(2)}, u32[]{:S(2)}) async-start(bf16[64,8,1536]{2,1,0:T(8,128)(2,1)} %bitcast.46), calls=%async_computation.2 | async-start | bytes 3145728 | tf_op jit(solution)/shard_map/all_to_all | solution.py:400
  94.1 16.0 %collective-permute-start.3 = (bf16[128,2304]{1,0:T(8,128)(2,1)S(1)}, bf16[128,2304]{1,0:T(8,128)(2,1)S(1)}, u32[]{:S(2)}, u32[]{:S(2)}) collective-permute-start(bf16[128,2304]{1,0:T(8,128)(2,1)S(1)} %slice.7), channel_id=1, source_target_pairs={{0,384},{64,448},{128,0},{192,64},{256,128},{320,192},{384,256},{4... | collective-permute-start | bytes 1769480 | tf_op jit(solution)/shard_map/ppermute | solution.py:442
  98.3 17.1 %collective-permute-start.2 = (bf16[128,2304]{1,0:T(8,128)(2,1)S(1)}, bf16[128,2304]{1,0:T(8,128)(2,1)}, u32[]{:S(2)}, u32[]{:S(2)}) collective-permute-start(bf16[128,2304]{1,0:T(8,128)(2,1)S(1)} %slice.6), channel_id=1, source_target_pairs={{0,128},{64,192},{128,256},{192,320},{256,384},{320,448},{384,0},{... | collective-permute-start | bytes 1769480 | tf_op jit(solution)/shard_map/ppermute | solution.py:442
  101.1 18.5 %collective-permute-start.4 = (bf16[256,2304]{1,0:T(8,128)(2,1)S(1)}, bf16[256,2304]{1,0:T(8,128)(2,1)}, u32[]{:S(2)}, u32[]{:S(2)}) collective-permute-start(bf16[256,2304]{1,0:T(8,128)(2,1)S(1)} %get-tuple-element.23.refs_0_), channel_id=1, source_target_pairs={{0,64},{64,0},{128,192},{192,128},{256,320},{320,256},{384,448},{4... | collective-permute-start | bytes 3538952 | tf_op jit(solution)/shard_map/ppermute | solution.py:445
  103.0 16.6 %collective-permute-start.5 = (bf16[256,2304]{1,0:T(8,128)(2,1)}, bf16[256,2304]{1,0:T(8,128)(2,1)}, u32[]{:S(2)}, u32[]{:S(2)}) collective-permute-start(bf16[256,2304]{1,0:T(8,128)(2,1)} %collective-permute-done._left_hbm.refs_1_), channel_id=1, source_target_pairs={{0,64},{64,0},{128,192},{192,128},{256,320},{320,256},{384,448},{4... | collective-permute-start | bytes 3538952 | tf_op jit(solution)/shard_map/ppermute | solution.py:445
  105.4 14.2 %collective-permute-start.6 = (bf16[256,2304]{1,0:T(8,128)(2,1)}, bf16[256,2304]{1,0:T(8,128)(2,1)}, u32[]{:S(2)}, u32[]{:S(2)}) collective-permute-start(bf16[256,2304]{1,0:T(8,128)(2,1)} %collective-permute-done.1._right_hbm.refs_2_), channel_id=1, source_target_pairs={{0,64},{64,0},{128,192},{192,128},{256,320},{320,256},{384,448},{4... | collective-permute-start | bytes 3538952 | tf_op jit(solution)/shard_map/ppermute | solution.py:445
  110.1 9.5 %copy-start.11 = (bf16[128,2304]{1,0:T(8,128)(2,1)}, bf16[128,2304]{1,0:T(8,128)(2,1)S(1)}, u32[]{:S(2)}) copy-start(bf16[128,2304]{1,0:T(8,128)(2,1)S(1)} %collective-permute-done.3.refs_4_) | copy-start | bytes 1769476
  110.1 7.4 %collective-permute-start.8 = (bf16[128,2304]{1,0:T(8,128)(2,1)S(1)}, bf16[128,2304]{1,0:T(8,128)(2,1)}, u32[]{:S(2)}, u32[]{:S(2)}) collective-permute-start(bf16[128,2304]{1,0:T(8,128)(2,1)S(1)} %collective-permute-done.3.refs_4_), channel_id=1, source_target_pairs={{0,64},{64,0},{128,192},{192,128},{256,320},{320,256},{384,448},{4... | collective-permute-start | bytes 1769480 | tf_op jit(solution)/shard_map/ppermute | solution.py:445
  115.3 4.2 %collective-permute-start.7 = (bf16[128,2304]{1,0:T(8,128)(2,1)}, bf16[128,2304]{1,0:T(8,128)(2,1)}, u32[]{:S(2)}, u32[]{:S(2)}) collective-permute-start(bf16[128,2304]{1,0:T(8,128)(2,1)} %collective-permute-done.2.refs_3_), channel_id=1, source_target_pairs={{0,64},{64,0},{128,192},{192,128},{256,320},{320,256},{384,448},{4... | collective-permute-start | bytes 1769480 | tf_op jit(solution)/shard_map/ppermute | solution.py:445
  126.2 1.4 copy-start
  143.3 48.3 %copy-start.3 = (bf16[1,128,2048]{2,1,0:T(8,128)(2,1)S(1)}, bf16[1,128,2048]{2,1,0:T(8,128)(2,1)}, u32[]{:S(2)}) copy-start(bf16[1,128,2048]{2,1,0:T(8,128)(2,1)} %param.15) | copy-start | bytes 1572868
  143.3 48.3 %copy-start.4 = (bf16[128,2048]{1,0:T(8,128)(2,1)S(1)}, bf16[128,2048]{1,0:T(8,128)(2,1)}, u32[]{:S(2)}) copy-start(bf16[128,2048]{1,0:T(8,128)(2,1)} %get-tuple-element.26.token_ref) | copy-start | bytes 1572868
  143.3 48.3 %copy-start.9 = (s32[1,128,2]{1,2,0:T(2,128)S(1)}, s32[1,128,2]{1,2,0:T(2,128)}, u32[]{:S(2)}) copy-start(s32[1,128,2]{1,2,0:T(2,128)} %param.18) | copy-start | bytes 3076

commit v4 on v3

--- a/solution.py
+++ b/solution.py
@@ -75,11 +75,11 @@
 
 def dispatch_kernel(
     owner_ref,
-    residual_ref,
-    gain_ref,
-    ids_ref,
-    code_ref,
-    positives_ref,
+    ids_hbm,
+    residual_hbm,
+    gain_hbm,
+    code_hbm,
+    positives_hbm,
     query_hbm,
     w0_hbm,
     w1_hbm,
@@ -90,6 +90,11 @@
     top_ref,
     rest_ref,
     joined_ref,
+    ids_ref,
+    residual_ref,
+    gain_ref,
+    code_ref,
+    positives_ref,
     query_ref,
     scores_ref,
     normed_ref,
@@ -99,6 +104,21 @@
     experts,
 ):
     hidden, columns = w0_hbm.shape[1], code_ref.shape[0]
+    base = PIECES + 5 + SECTIONS
+    inputs = [
+        pltpu.make_async_copy(source, target, sems.at[base + n])
+        for n, (source, target) in enumerate(
+            (
+                (ids_hbm, ids_ref),
+                (residual_hbm, residual_ref),
+                (gain_hbm, gain_ref),
+                (code_hbm, code_ref),
+                (positives_hbm, positives_ref),
+            )
+        )
+    ]
+    for copy in inputs:
+        copy.start()
     parts = [slice(c * LANES, (c + 1) * LANES) for c in range(PIECES)]
     queries = [
         pltpu.make_async_copy(query_hbm.at[part], query_ref.at[part], sems.at[c])
@@ -112,8 +132,14 @@
     ]
     for copy in copies:
         copy.start()
+    for copy in inputs:
+        copy.wait()
     stream = residual_ref[...].astype(F32)
-    normed_ref[...] = (stream * inverse_rms(stream) * gain_ref[...].astype(F32)).astype(BF)
+    scaled = stream * inverse_rms(stream)
+    gain = gain_ref[...].astype(F32)
+    for c in range(gain.shape[0]):
+        lanes = slice(c * LANES, (c + 1) * LANES)
+        normed_ref[:, lanes] = (scaled[:, lanes] * gain[c : c + 1]).astype(BF)
     ids = jnp.concatenate([ids_ref[0:1, :], ids_ref[1:2, :]], axis=1)
     count = ids.shape[1]
     table = (iota((experts, count), 0) == ids).astype(F32)
@@ -265,67 +291,61 @@
             ).astype(BF)
 
 
-def place_weights(shards, order_ref, weights_ref, columns, sems, first):
+def forward_kernel(order_ref, block_ref, *refs):
+    *shards, weights_hbm, factor_hbm, weights_ref, factor_ref, rows_ref, sems = refs
+    hidden = factor_ref.shape[1] // 2
     copies = []
     for n, shard in enumerate(shards):
         rows = pl.ds(pl.multiple_of(order_ref[n], LANES), shard.shape[0])
-        copies.append(
-            pltpu.make_async_copy(
-                shard.at[:, columns], weights_ref.at[rows, columns], sems.at[first + n]
-            )
-        )
-    return copies
-
-
-def forward_kernel(order_ref, block_ref, *refs):
-    *shards, factor_ref, weights_ref, rows_ref, sems = refs
-    hidden = factor_ref.shape[1] // 2
-    copies = place_weights(shards, order_ref, weights_ref, slice(0, 2 * hidden), sems, 0)
+        copies.append(pltpu.make_async_copy(shard, weights_ref.at[rows], sems.at[n]))
     for copy in copies:
         copy.start()
     unpack_blocks(block_ref, rows_ref)
     for copy in copies:
         copy.wait()
+    keep = [
+        pltpu.make_async_copy(weights_ref, weights_hbm, sems.at[len(shards)]),
+        pltpu.make_async_copy(factor_ref, factor_hbm, sems.at[len(shards) + 1]),
+    ]
+    keep[0].start()
     gate_pre = dot(rows_ref[...], weights_ref[:, :hidden])
-    up_pre = dot(rows_ref[...], weights_ref[:, hidden:])
+    up_pre = dot(rows_ref[...], weights_ref[:, hidden : 2 * hidden])
     s = jax.nn.sigmoid(gate_pre)
     factor_ref[:, :hidden] = up_pre * s * (1.0 + gate_pre * (1.0 - s))
     factor_ref[:, hidden:] = gate_pre * s
-
-
-def backward_kernel(order_ref, block_hbm, factor_hbm, *refs):
-    *shards, out_ref, block_ref, weights_ref, factor_ref, rows_ref, hidden_ref, sems = refs
+    keep[1].start()
+    for copy in keep:
+        copy.wait()
+
+
+def backward_kernel(
+    block_hbm, weights_hbm, factor_hbm, out_ref, block_ref, weights_ref, factor_ref, rows_ref, hidden_ref, sems
+):
     hidden = factor_ref.shape[1] // 2
-    parts = halves(block_ref.shape[0])
-    height = block_ref.shape[0] // parts
-    first = [
-        pltpu.make_async_copy(
-            block_hbm.at[g * height : (g + 1) * height], block_ref.at[g * height : (g + 1) * height], sems.at[g]
+    down, rest = slice(2 * hidden, 3 * hidden), slice(0, 2 * hidden)
+    copies = [
+        pltpu.make_async_copy(source, target, sems.at[n])
+        for n, (source, target) in enumerate(
+            (
+                (block_hbm, block_ref),
+                (weights_hbm.at[:, down], weights_ref.at[:, down]),
+                (factor_hbm, factor_ref),
+                (weights_hbm.at[:, rest], weights_ref.at[:, rest]),
+            )
         )
-        for g in range(parts)
-    ]
-    down = place_weights(shards, order_ref, weights_ref, slice(2 * hidden, 3 * hidden), sems, parts)
-    factor = pltpu.make_async_copy(factor_hbm, factor_ref, sems.at[parts + len(shards)])
-    rest = place_weights(
-        shards, order_ref, weights_ref, slice(0, 2 * hidden), sems, parts + len(shards) + 1
-    )
-    for copy in (*first, *down, factor, *rest):
+    ]
+    for copy in copies:
         copy.start()
-    for copy in first:
-        copy.wait()
+    copies[0].wait()
     unpack_blocks(block_ref, rows_ref)
-    for copy in down:
-        copy.wait()
-    back = dot(rows_ref[...], weights_ref[:, 2 * hidden :])
-    factor.wait()
+    copies[1].wait()
+    back = dot(rows_ref[...], weights_ref[:, down])
+    copies[2].wait()
     hidden_ref[:, :hidden] = (back * factor_ref[:, :hidden]).astype(BF)
     hidden_ref[:, hidden:] = (back * factor_ref[:, hidden:]).astype(BF)
-    for copy in rest:
-        copy.wait()
+    copies[3].wait()
     for k in range(SECTIONS + 1):
-        rows_ref[:, section(k)] = dot_last(
-            hidden_ref[...], weights_ref[section(k), : 2 * hidden]
-        ).astype(BF)
+        rows_ref[:, section(k)] = dot_last(hidden_ref[...], weights_ref[section(k), rest]).astype(BF)
     pack_blocks(rows_ref, out_ref)
 
 
@@ -348,7 +368,11 @@
     grad_ref[:, section(SECTIONS)] = tail
     stream = residual_ref[...].astype(F32)
     root = inverse_rms(stream)
-    scaled = gain_ref[...].astype(F32) * grad_ref[...]
+    gain = gain_ref[...].astype(F32)
+    for c in range(gain.shape[0]):
+        lanes = slice(c * LANES, (c + 1) * LANES)
+        grad_ref[:, lanes] = gain[c : c + 1] * grad_ref[:, lanes]
+    scaled = grad_ref[...]
     correction = jnp.mean(scaled * stream, axis=-1, keepdims=True)
     cot = token_ref[...].astype(F32)
     out_ref[...] = (cot + root * scaled - stream * (root * root * root * correction)).astype(BF)
@@ -389,7 +413,7 @@
     total = owners * BLOCK
     lengths = file_lengths.reshape(1, files)
     stream = residual[0]
-    gain = norm_gain.reshape(1, width)
+    gain = norm_gain.reshape(width // LANES, LANES)
     ids = expert_ids[0].T
     units = gate_units[0].T
 
@@ -411,24 +435,29 @@
             jax.ShapeDtypeStruct((1, queries), F32),
             jax.ShapeDtypeStruct((w_gate.shape[1], 3 * hidden), BF),
         ),
-        in_specs=[IN_SMEM] + [IN_VMEM] * 5 + [IN_HBM] * 4,
+        in_specs=[IN_SMEM] + [IN_HBM] * 9,
         out_specs=(IN_HBM, IN_HBM) + (IN_VMEM,) * 4,
         scratch_shapes=[
+            pltpu.VMEM((2, tokens), jnp.int32),
+            pltpu.VMEM((tokens, width), BF),
+            pltpu.VMEM(gain.shape, BF),
+            pltpu.VMEM((columns, width), BF),
+            pltpu.VMEM((1, queries), jnp.int32),
             pltpu.VMEM((queries, width), BF),
             pltpu.VMEM((columns, queries), F32),
             pltpu.VMEM((tokens, width), BF),
             pltpu.VMEM((total, BLOCK_WIDTH + LANES), BF),
-            pltpu.SemaphoreType.DMA((PIECES + 5 + SECTIONS,)),
+            pltpu.SemaphoreType.DMA((PIECES + 10 + SECTIONS,)),
         ],
         compiler_params=params(16),
         name="dispatch",
     )(
         owner,
-        stream,
-        gain,
-        ids,
-        code_reps,
-        positives[None],
+        hbm(ids),
+        hbm(stream),
+        hbm(gain),
+        hbm(code_reps),
+        hbm(positives[None]),
         hbm(query_reps),
         hbm(w_gate[0]),
         hbm(w_up[0]),
@@ -510,23 +539,24 @@
     ).astype(jnp.int32)
 
     rows = owners * SLOTS
-    factor = pl.pallas_call(
+    weights, factor = pl.pallas_call(
         forward_kernel,
-        out_shape=jax.ShapeDtypeStruct((rows, 2 * hidden), F32),
+        out_shape=(pltpu.HBM((width, 3 * hidden), BF), pltpu.HBM((rows, 2 * hidden), F32)),
         in_specs=[IN_SMEM, IN_VMEM] + [IN_HBM] * len(shards),
-        out_specs=IN_VMEM,
+        out_specs=(IN_HBM, IN_HBM),
         scratch_shapes=[
-            pltpu.VMEM((width, 2 * hidden), BF),
+            pltpu.VMEM((width, 3 * hidden), BF),
+            pltpu.VMEM((rows, 2 * hidden), F32),
             pltpu.VMEM((rows, width), BF),
-            pltpu.SemaphoreType.DMA((len(shards),)),
+            pltpu.SemaphoreType.DMA((len(shards) + 2,)),
         ],
-        compiler_params=params(24),
+        compiler_params=params(32),
         name="expert_forward",
     )(order, blocks, *shards)
     result = pl.pallas_call(
         backward_kernel,
         out_shape=jax.ShapeDtypeStruct((total, BLOCK_WIDTH), BF),
-        in_specs=[IN_SMEM] + [IN_HBM] * (2 + len(shards)),
+        in_specs=[IN_HBM] * 3,
         out_specs=IN_VMEM,
         scratch_shapes=[
             pltpu.VMEM((total, BLOCK_WIDTH), BF),
@@ -534,11 +564,11 @@
             pltpu.VMEM((rows, 2 * hidden), F32),
             pltpu.VMEM((rows, width), BF),
             pltpu.VMEM((rows, 2 * hidden), BF),
-            pltpu.SemaphoreType.DMA((halves(total) + 2 * len(shards) + 1,)),
+            pltpu.SemaphoreType.DMA((4,)),
         ],
         compiler_params=params(32),
         name="expert_backward",
-    )(order, hbm(cot_blocks), hbm(factor), *shards)
+    )(hbm(cot_blocks), hbm(weights), hbm(factor))
 
     token_grad = pl.pallas_call(
         finish_kernel,

time: 194 us -> 191 us (0.985)
  the two profiles are of different devices: /device:TPU:8 before, /device:TPU:6 now
where the time goes in v4:
time: 191 us; the launch traced here: 187 us
  blocking collectives  57.5 us (30%)
  waiting for transfers between devices  49.2 us (26%)
  starting transfers between devices  48.7 us (25%)
  Pallas kernels  29.5 us (15%)
  local copies, waits for them, and re-layouts  2.34 us (1%)
    all_to_all x1, blocking collectives, exchange(): lax.all_to_all(value.reshape(owners, BLOCK, shape[1]), 'expert', 0, 0, ti...  47.4 us
    ppermute x4, waiting for transfers between devices, ahead(): lax.ppermute(value, 'dp', [(d, (d + step) % size) for d in range(size)])  28.3 us
    all_to_all x2, starting transfers between devices, exchange(): lax.all_to_all(value.reshape(owners, BLOCK, shape[1]), 'expert', 0, 0, ti...  24.2 us
    all_to_all x2, waiting for transfers between devices, exchange(): lax.all_to_all(value.reshape(owners, BLOCK, shape[1]), 'expert', 0, 0, ti...  19.1 us
    ppermute x4, starting transfers between devices, ahead(): lax.ppermute(value, 'dp', [(d, (d + step) % size) for d in range(size)])  14.1 us
    ppermute x5, starting transfers between devices, partner(): return lax.ppermute(value, 'dp', [(d, d ^ 1) for d in range(size)])  10.4 us
    all_to_all x1, blocking collectives, per_device(): lax.all_to_all(parts.reshape(columns // files, files, width), 'dp', 0, 0,...  10 us
    pallas_call x1, Pallas kernels, per_device(): pl.pallas_call(backward_kernel, out_shape=jax.ShapeDtypeStruct((total, BL...  9.27 us
  transfers between devices with their start and end apart: 11, of which 7 were waited for; matrix products, arithmetic and copies ran while one was open for 1% of the time, Pallas kernels for 5%

profile of v4, /device:TPU:6, one launch (start us, length us, event | category | flops | bytes accessed | tf_op | source)
XLA Modules:
  0.0 187.5 jit_solution(1409617148358498040)
XLA Ops:
  0.0 4.6 %dispatch.1 = (bf16[512,1664]{1,0:T(8,128)(2,1)}, f32[64,512]{1,0:T(8,128)}, s32[2,128]{1,0:T(2,128)S(1)}, f32[1,512]{1,0:T(1,128)S(1)}, f32[1,512]{1,0:T(1,128)S(1)}, /*index=5*/bf16[256,2304]{1,0:T(8,128)(2,1)S(1)}) custom-call(s32[1]{0:T(128)} %bitcast.owner_ref, s32[2,128]{1,0:T(2,128)} %bitcast.52, bf16[128,2048]{1,0:T(8,128)(2,1)} %bitcast.37, ...), custom_call_target="tpu_custom_call" | custom-call | tf_op jit(solution)/shard_map/dispatch/pallas_call | solution.py:428
  4.7 16.7 %all-to-all-start = ((bf16[64,8,1664]{2,1,0:T(8,128)(2,1)}), bf16[64,8,1664]{2,1,0:T(8,128)(2,1)S(1)}, u32[]{:S(2)}, u32[]{:S(2)}) async-start(bf16[64,8,1664]{2,1,0:T(8,128)(2,1)} %bitcast.47), calls=%async_computation | async-start | bytes 3407872 | tf_op jit(solution)/shard_map/all_to_all | solution.py:424
  21.4 2.7 %collective-permute-start.1 = (bf16[256,2304]{1,0:T(8,128)(2,1)S(1)}, bf16[256,2304]{1,0:T(8,128)(2,1)}, u32[]{:S(2)}, u32[]{:S(2)}) collective-permute-start(bf16[256,2304]{1,0:T(8,128)(2,1)S(1)} %get-tuple-element.25.refs_0_), channel_id=1, source_target_pairs={{0,384},{64,448},{128,0},{192,64},{256,128},{320,192},{384,256},{4... | collective-permute-start | bytes 3538952 | tf_op jit(solution)/shard_map/ppermute | solution.py:471
  24.2 4.3 %collective-permute-start = (bf16[256,2304]{1,0:T(8,128)(2,1)S(1)}, bf16[256,2304]{1,0:T(8,128)(2,1)}, u32[]{:S(2)}, u32[]{:S(2)}) collective-permute-start(bf16[256,2304]{1,0:T(8,128)(2,1)S(1)} %get-tuple-element.25.refs_0_), channel_id=1, source_target_pairs={{0,128},{64,192},{128,256},{192,320},{256,384},{320,448},{384,0},{... | collective-permute-start | bytes 3538952 | tf_op jit(solution)/shard_map/ppermute | solution.py:471
  28.5 23.6 %collective-permute-done.1._right_hbm.refs_2_ = bf16[256,2304]{1,0:T(8,128)(2,1)} collective-permute-done((bf16[256,2304]{1,0:T(8,128)(2,1)S(1)}, bf16[256,2304]{1,0:T(8,128)(2,1)}, u32[]{:S(2)}, u32[]{:S(2)}) %collective-permute-start.1) | collective-permute-done | bytes 1179680 | tf_op jit(solution)/shard_map/ppermute | solution.py:471
  53.3 12.3 %all-to-all-done = bf16[64,8,1664]{2,1,0:T(8,128)(2,1)S(1)} async-done(((bf16[64,8,1664]{2,1,0:T(8,128)(2,1)}), bf16[64,8,1664]{2,1,0:T(8,128)(2,1)S(1)}, u32[]{:S(2)}, u32[]{:S(2)}) %all-to-all-start) | async-done | bytes 1703968 | tf_op jit(solution)/shard_map/all_to_all | solution.py:424
  65.7 2.2 %code_weights.1 = bf16[64,2048]{1,0:T(8,128)(2,1)S(1)} custom-call(bf16[512,1664]{1,0:T(8,128)(2,1)S(1)} %bitcast.33, s32[1]{0:T(128)} %bitcast.owner_ref, f32[1,512]{1,0:T(1,128)S(1)} %get-tuple-element.19.top_ref, f32[1,512]{1,0:T(1,128)S(1)} %get-tuple-element.20.rest_ref, s32[1,512]{1,0:T(1,128)S(1)} %bitcast.44, ...), custom_call_target="tpu_custom_call" | custom-call | tf_op jit(solution)/shard_map/code_weights/pallas_call | solution.py:478
  67.8 10.0 %all_to_all.20 = bf16[8,8,2048]{2,1,0:T(8,128)(2,1)S(1)} all-to-all(bf16[8,8,2048]{2,1,0:T(8,128)(2,1)S(1)} %bitcast.39), channel_id=1, replica_groups=mesh['dp'=8,'expert'=64] {'dp'}, dimensions={0} | all-to-all | bytes 524288 | tf_op jit(solution)/shard_map/all_to_all | solution.py:503
  77.9 2.5 %cotangent.1 = (bf16[512,1536]{1,0:T(8,128)(2,1)}, bf16[128,2048]{1,0:T(8,128)(2,1)}) custom-call(bf16[64,2048]{1,0:T(8,128)(2,1)S(1)} %bitcast.40, s32[1,8]{1,0:T(1,128)S(1)} %bitcast.46, s32[2,128]{1,0:T(2,128)S(1)} %get-tuple-element.23.q_ref), custom_call_target="tpu_custom_call" | custom-call | tf_op jit(solution)/shard_map/cotangent/pallas_call | solution.py:506
  80.4 7.5 %all-to-all-start.2 = ((bf16[64,8,1536]{2,1,0:T(8,128)(2,1)}), bf16[64,8,1536]{2,1,0:T(8,128)(2,1)}, u32[]{:S(2)}, u32[]{:S(2)}) async-start(bf16[64,8,1536]{2,1,0:T(8,128)(2,1)} %bitcast.48), calls=%async_computation.2 | async-start | bytes 3145728 | tf_op jit(solution)/shard_map/all_to_all | solution.py:424
  89.0 1.9 %collective-permute-start.3 = (bf16[128,2304]{1,0:T(8,128)(2,1)S(1)}, bf16[128,2304]{1,0:T(8,128)(2,1)S(1)}, u32[]{:S(2)}, u32[]{:S(2)}) collective-permute-start(bf16[128,2304]{1,0:T(8,128)(2,1)S(1)} %slice.7), channel_id=1, source_target_pairs={{0,384},{64,448},{128,0},{192,64},{256,128},{320,192},{384,256},{4... | collective-permute-start | bytes 1769480 | tf_op jit(solution)/shard_map/ppermute | solution.py:471
  92.0 5.1 %collective-permute-start.2 = (bf16[128,2304]{1,0:T(8,128)(2,1)S(1)}, bf16[128,2304]{1,0:T(8,128)(2,1)}, u32[]{:S(2)}, u32[]{:S(2)}) collective-permute-start(bf16[128,2304]{1,0:T(8,128)(2,1)S(1)} %slice.6), channel_id=1, source_target_pairs={{0,128},{64,192},{128,256},{192,320},{256,384},{320,448},{384,0},{... | collective-permute-start | bytes 1769480 | tf_op jit(solution)/shard_map/ppermute | solution.py:471
  97.2 1.9 %collective-permute-start.4 = (bf16[256,2304]{1,0:T(8,128)(2,1)S(1)}, bf16[256,2304]{1,0:T(8,128)(2,1)}, u32[]{:S(2)}, u32[]{:S(2)}) collective-permute-start(bf16[256,2304]{1,0:T(8,128)(2,1)S(1)} %get-tuple-element.25.refs_0_), channel_id=1, source_target_pairs={{0,64},{64,0},{128,192},{192,128},{256,320},{320,256},{384,448},{4... | collective-permute-start | bytes 3538952 | tf_op jit(solution)/shard_map/ppermute | solution.py:474
  99.1 2.4 %collective-permute-start.5 = (bf16[256,2304]{1,0:T(8,128)(2,1)}, bf16[256,2304]{1,0:T(8,128)(2,1)}, u32[]{:S(2)}, u32[]{:S(2)}) collective-permute-start(bf16[256,2304]{1,0:T(8,128)(2,1)} %collective-permute-done._left_hbm.refs_1_), channel_id=1, source_target_pairs={{0,64},{64,0},{128,192},{192,128},{256,320},{320,256},{384,448},{4... | collective-permute-start | bytes 3538952 | tf_op jit(solution)/shard_map/ppermute | solution.py:474
  101.5 1.9 %collective-permute-start.6 = (bf16[256,2304]{1,0:T(8,128)(2,1)}, bf16[256,2304]{1,0:T(8,128)(2,1)}, u32[]{:S(2)}, u32[]{:S(2)}) collective-permute-start(bf16[256,2304]{1,0:T(8,128)(2,1)} %collective-permute-done.1._right_hbm.refs_2_), channel_id=1, source_target_pairs={{0,64},{64,0},{128,192},{192,128},{256,320},{320,256},{384,448},{4... | collective-permute-start | bytes 3538952 | tf_op jit(solution)/shard_map/ppermute | solution.py:474
  103.4 3.1 %collective-permute-done.3.refs_4_ = bf16[128,2304]{1,0:T(8,128)(2,1)S(1)} collective-permute-done((bf16[128,2304]{1,0:T(8,128)(2,1)S(1)}, bf16[128,2304]{1,0:T(8,128)(2,1)S(1)}, u32[]{:S(2)}, u32[]{:S(2)}) %collective-permute-start.3) | collective-permute-done | bytes 589856 | tf_op jit(solution)/shard_map/ppermute | solution.py:471
  106.5 1.9 %collective-permute-start.8 = (bf16[128,2304]{1,0:T(8,128)(2,1)S(1)}, bf16[128,2304]{1,0:T(8,128)(2,1)}, u32[]{:S(2)}, u32[]{:S(2)}) collective-permute-start(bf16[128,2304]{1,0:T(8,128)(2,1)S(1)} %collective-permute-done.3.refs_4_), channel_id=1, source_target_pairs={{0,64},{64,0},{128,192},{192,128},{256,320},{320,256},{384,448},{4... | collective-permute-start | bytes 1769480 | tf_op jit(solution)/shard_map/ppermute | solution.py:474
  108.8 2.2 %collective-permute-start.7 = (bf16[128,2304]{1,0:T(8,128)(2,1)}, bf16[128,2304]{1,0:T(8,128)(2,1)}, u32[]{:S(2)}, u32[]{:S(2)}) collective-permute-start(bf16[128,2304]{1,0:T(8,128)(2,1)} %collective-permute-done.2.refs_3_), channel_id=1, source_target_pairs={{0,64},{64,0},{128,192},{192,128},{256,320},{320,256},{384,448},{4... | collective-permute-start | bytes 1769480 | tf_op jit(solution)/shard_map/ppermute | solution.py:474
  111.2 1.9 %collective-permute-done.7.refs_8_ = bf16[128,2304]{1,0:T(8,128)(2,1)} collective-permute-done((bf16[128,2304]{1,0:T(8,128)(2,1)}, bf16[128,2304]{1,0:T(8,128)(2,1)}, u32[]{:S(2)}, u32[]{:S(2)}) %collective-permute-start.7) | collective-permute-done | bytes 589856 | tf_op jit(solution)/shard_map/ppermute | solution.py:474
  113.1 9.2 %expert_forward.1 = (bf16[2048,2304]{1,0:T(8,128)(2,1)}, f32[384,1536]{1,0:T(8,128)}) custom-call(s32[10]{0:T(128)S(1)} %stack.43.order_ref, bf16[512,1664]{1,0:T(8,128)(2,1)S(1)} %bitcast.34, bf16[256,2304]{1,0:T(8,128)(2,1)} %copy-done.1, bf16[256,2304]{1,0:T(8,128)(2,1)} %collective-permute-done._left_hbm.refs_1_, ...), custom_call_target="tpu_custom_call" | custom-call | tf_op jit(solution)/shard_map/expert_forward/pallas_call | solution.py:542
  122.2 6.7 %all-to-all-done.2 = bf16[64,8,1536]{2,1,0:T(8,128)(2,1)} async-done(((bf16[64,8,1536]{2,1,0:T(8,128)(2,1)}), bf16[64,8,1536]{2,1,0:T(8,128)(2,1)}, u32[]{:S(2)}, u32[]{:S(2)}) %all-to-all-start.2) | async-done | bytes 1572896 | tf_op jit(solution)/shard_map/all_to_all | solution.py:424
  129.0 9.3 %expert_backward.1 = bf16[512,1536]{1,0:T(8,128)(2,1)S(1)} custom-call(bf16[512,1536]{1,0:T(8,128)(2,1)} %bitcast.15.block_hbm, bf16[2048,2304]{1,0:T(8,128)(2,1)} %get-tuple-element.28.weights_hbm, f32[384,1536]{1,0:T(8,128)} %get-tuple-element.29.factor_hbm), custom_call_target="tpu_custom_call" | custom-call | tf_op jit(solution)/shard_map/expert_backward/pallas_call | solution.py:556
  138.3 47.4 %all_to_all.21 = bf16[64,8,1536]{2,1,0:T(8,128)(2,1)S(1)} all-to-all(bf16[64,8,1536]{2,1,0:T(8,128)(2,1)S(1)} %bitcast.35), channel_id=1, replica_groups=mesh['dp'=8,'expert'=64] {'expert'}, dimensions={0} | all-to-all | bytes 3145728 | tf_op jit(solution)/shard_map/all_to_all | solution.py:424
  185.8 1.7 finish.1
  (25 shorter events, 4.0 us)
Async XLA Ops:
  4.7 92.5 %copy-start.1 = (bf16[256,2304]{1,0:T(8,128)(2,1)}, bf16[256,2304]{1,0:T(8,128)(2,1)S(1)}, u32[]{:S(2)}) copy-start(bf16[256,2304]{1,0:T(8,128)(2,1)S(1)} %get-tuple-element.25.refs_0_) | copy-start | bytes 3538948
  4.7 61.0 %copy-start.4 = (s32[512]{0:T(512)S(1)}, s32[512]{0:T(512)}, u32[]{:S(2)}) copy-start(s32[512]{0:T(512)} %param.13) | copy-start | bytes 6148
  4.7 61.0 %all-to-all-start = ((bf16[64,8,1664]{2,1,0:T(8,128)(2,1)}), bf16[64,8,1664]{2,1,0:T(8,128)(2,1)S(1)}, u32[]{:S(2)}, u32[]{:S(2)}) async-start(bf16[64,8,1664]{2,1,0:T(8,128)(2,1)} %bitcast.47), calls=%async_computation | async-start | bytes 3407872 | tf_op jit(solution)/shard_map/all_to_all | solution.py:424
  21.4 30.6 %collective-permute-start.1 = (bf16[256,2304]{1,0:T(8,128)(2,1)S(1)}, bf16[256,2304]{1,0:T(8,128)(2,1)}, u32[]{:S(2)}, u32[]{:S(2)}) collective-permute-start(bf16[256,2304]{1,0:T(8,128)(2,1)S(1)} %get-tuple-element.25.refs_0_), channel_id=1, source_target_pairs={{0,384},{64,448},{128,0},{192,64},{256,128},{320,192},{384,256},{4... | collective-permute-start | bytes 3538952 | tf_op jit(solution)/shard_map/ppermute | solution.py:471
  24.2 29.1 %collective-permute-start = (bf16[256,2304]{1,0:T(8,128)(2,1)S(1)}, bf16[256,2304]{1,0:T(8,128)(2,1)}, u32[]{:S(2)}, u32[]{:S(2)}) collective-permute-start(bf16[256,2304]{1,0:T(8,128)(2,1)S(1)} %get-tuple-element.25.refs_0_), channel_id=1, source_target_pairs={{0,128},{64,192},{128,256},{192,320},{256,384},{320,448},{384,0},{... | collective-permute-start | bytes 3538952 | tf_op jit(solution)/shard_map/ppermute | solution.py:471
  65.7 12.2 %copy-start.6 = (s32[1,1,8]{2,1,0:T(1,128)S(1)}, s32[1,1,8]{2,1,0:T(1,128)}, u32[]{:S(2)}) copy-start(s32[1,1,8]{2,1,0:T(1,128)} %param.14) | copy-start | bytes 100
  80.4 48.6 %all-to-all-start.2 = ((bf16[64,8,1536]{2,1,0:T(8,128)(2,1)}), bf16[64,8,1536]{2,1,0:T(8,128)(2,1)}, u32[]{:S(2)}, u32[]{:S(2)}) async-start(bf16[64,8,1536]{2,1,0:T(8,128)(2,1)} %bitcast.48), calls=%async_computation.2 | async-start | bytes 3145728 | tf_op jit(solution)/shard_map/all_to_all | solution.py:424
  89.0 17.5 %collective-permute-start.3 = (bf16[128,2304]{1,0:T(8,128)(2,1)S(1)}, bf16[128,2304]{1,0:T(8,128)(2,1)S(1)}, u32[]{:S(2)}, u32[]{:S(2)}) collective-permute-start(bf16[128,2304]{1,0:T(8,128)(2,1)S(1)} %slice.7), channel_id=1, source_target_pairs={{0,384},{64,448},{128,0},{192,64},{256,128},{320,192},{384,256},{4... | collective-permute-start | bytes 1769480 | tf_op jit(solution)/shard_map/ppermute | solution.py:471
  92.0 16.8 %collective-permute-start.2 = (bf16[128,2304]{1,0:T(8,128)(2,1)S(1)}, bf16[128,2304]{1,0:T(8,128)(2,1)}, u32[]{:S(2)}, u32[]{:S(2)}) collective-permute-start(bf16[128,2304]{1,0:T(8,128)(2,1)S(1)} %slice.6), channel_id=1, source_target_pairs={{0,128},{64,192},{128,256},{192,320},{256,384},{320,448},{384,0},{... | collective-permute-start | bytes 1769480 | tf_op jit(solution)/shard_map/ppermute | solution.py:471
  97.2 15.9 %collective-permute-start.4 = (bf16[256,2304]{1,0:T(8,128)(2,1)S(1)}, bf16[256,2304]{1,0:T(8,128)(2,1)}, u32[]{:S(2)}, u32[]{:S(2)}) collective-permute-start(bf16[256,2304]{1,0:T(8,128)(2,1)S(1)} %get-tuple-element.25.refs_0_), channel_id=1, source_target_pairs={{0,64},{64,0},{128,192},{192,128},{256,320},{320,256},{384,448},{4... | collective-permute-start | bytes 3538952 | tf_op jit(solution)/shard_map/ppermute | solution.py:474
  99.1 13.9 %collective-permute-start.5 = (bf16[256,2304]{1,0:T(8,128)(2,1)}, bf16[256,2304]{1,0:T(8,128)(2,1)}, u32[]{:S(2)}, u32[]{:S(2)}) collective-permute-start(bf16[256,2304]{1,0:T(8,128)(2,1)} %collective-permute-done._left_hbm.refs_1_), channel_id=1, source_target_pairs={{0,64},{64,0},{128,192},{192,128},{256,320},{320,256},{384,448},{4... | collective-permute-start | bytes 3538952 | tf_op jit(solution)/shard_map/ppermute | solution.py:474
  101.5 11.5 %collective-permute-start.6 = (bf16[256,2304]{1,0:T(8,128)(2,1)}, bf16[256,2304]{1,0:T(8,128)(2,1)}, u32[]{:S(2)}, u32[]{:S(2)}) collective-permute-start(bf16[256,2304]{1,0:T(8,128)(2,1)} %collective-permute-done.1._right_hbm.refs_2_), channel_id=1, source_target_pairs={{0,64},{64,0},{128,192},{192,128},{256,320},{320,256},{384,448},{4... | collective-permute-start | bytes 3538952 | tf_op jit(solution)/shard_map/ppermute | solution.py:474
  106.5 6.5 %copy-start.7 = (bf16[128,2304]{1,0:T(8,128)(2,1)}, bf16[128,2304]{1,0:T(8,128)(2,1)S(1)}, u32[]{:S(2)}) copy-start(bf16[128,2304]{1,0:T(8,128)(2,1)S(1)} %collective-permute-done.3.refs_4_) | copy-start | bytes 1769476
  106.5 4.6 %collective-permute-start.8 = (bf16[128,2304]{1,0:T(8,128)(2,1)S(1)}, bf16[128,2304]{1,0:T(8,128)(2,1)}, u32[]{:S(2)}, u32[]{:S(2)}) collective-permute-start(bf16[128,2304]{1,0:T(8,128)(2,1)S(1)} %collective-permute-done.3.refs_4_), channel_id=1, source_target_pairs={{0,64},{64,0},{128,192},{192,128},{256,320},{320,256},{384,448},{4... | collective-permute-start | bytes 1769480 | tf_op jit(solution)/shard_map/ppermute | solution.py:474
  108.8 4.2 %collective-permute-start.7 = (bf16[128,2304]{1,0:T(8,128)(2,1)}, bf16[128,2304]{1,0:T(8,128)(2,1)}, u32[]{:S(2)}, u32[]{:S(2)}) collective-permute-start(bf16[128,2304]{1,0:T(8,128)(2,1)} %collective-permute-done.2.refs_3_), channel_id=1, source_target_pairs={{0,64},{64,0},{128,192},{192,128},{256,320},{320,256},{384,448},{4... | collective-permute-start | bytes 1769480 | tf_op jit(solution)/shard_map/ppermute | solution.py:474
  138.3 47.5 %copy-start = (bf16[1,128,2048]{2,1,0:T(8,128)(2,1)S(1)}, bf16[1,128,2048]{2,1,0:T(8,128)(2,1)}, u32[]{:S(2)}) copy-start(bf16[1,128,2048]{2,1,0:T(8,128)(2,1)} %param.15) | copy-start | bytes 1572868
  138.3 47.5 %copy-start.2 = (bf16[128,2048]{1,0:T(8,128)(2,1)S(1)}, bf16[128,2048]{1,0:T(8,128)(2,1)}, u32[]{:S(2)}) copy-start(bf16[128,2048]{1,0:T(8,128)(2,1)} %get-tuple-element.30.token_ref) | copy-start | bytes 1572868
  138.3 47.5 %copy-start.3 = (bf16[2048]{0:T(1024)(128)(2,1)S(1)}, bf16[2048]{0:T(1024)(128)(2,1)}, u32[]{:S(2)}) copy-start(bf16[2048]{0:T(1024)(128)(2,1)} %param.16) | copy-start | bytes 12292
  138.3 47.5 %copy-start.5 = (s32[1,128,2]{1,2,0:T(2,128)S(1)}, s32[1,128,2]{1,2,0:T(2,128)}, u32[]{:S(2)}) copy-start(s32[1,128,2]{1,2,0:T(2,128)} %param.18) | copy-start | bytes 3076

commit v5 on v4

--- a/solution.py
+++ b/solution.py
@@ -89,7 +89,8 @@
     q_ref,
     top_ref,
     rest_ref,
-    joined_ref,
+    joined_a_ref,
+    joined_b_ref,
     ids_ref,
     residual_ref,
     gain_ref,
@@ -104,7 +105,7 @@
     experts,
 ):
     hidden, columns = w0_hbm.shape[1], code_ref.shape[0]
-    base = PIECES + 5 + SECTIONS
+    base = PIECES + 8 + SECTIONS
     inputs = [
         pltpu.make_async_copy(source, target, sems.at[base + n])
         for n, (source, target) in enumerate(
@@ -126,14 +127,20 @@
     ]
     for copy in queries:
         copy.start()
+    half = joined_a_ref.shape[0]
     copies = [
-        pltpu.make_async_copy(w_hbm, joined_ref.at[:, k * hidden : (k + 1) * hidden], sems.at[PIECES + k])
+        pltpu.make_async_copy(
+            w_hbm.at[n * half : (n + 1) * half],
+            joined_ref.at[:, k * hidden : (k + 1) * hidden],
+            sems.at[PIECES + 2 * k + n],
+        )
         for k, w_hbm in enumerate((w0_hbm, w1_hbm, w2_hbm))
-    ]
+        for n, joined_ref in enumerate((joined_a_ref, joined_b_ref))
+    ]
+    for copy in inputs:
+        copy.wait()
     for copy in copies:
         copy.start()
-    for copy in inputs:
-        copy.wait()
     stream = residual_ref[...].astype(F32)
     scaled = stream * inverse_rms(stream)
     gain = gain_ref[...].astype(F32)
@@ -148,10 +155,9 @@
     )
     rank = jnp.sum(table * earlier, axis=0, keepdims=True).astype(jnp.int32)
     q_flat = ids * BLOCK + rank
-    half = count // 2
-    q = jnp.concatenate([q_flat[:, :half], q_flat[:, half:]], axis=0)
+    q = jnp.concatenate([q_flat[:, : count // 2], q_flat[:, count // 2 :]], axis=0)
     q_ref[...] = q
-    copies += pack_rows(normed_ref, q, stage_ref, out_hbm, sems.at[PIECES + 3 : PIECES + 3 + SECTIONS])
+    copies += pack_rows(normed_ref, q, stage_ref, out_hbm, sems.at[PIECES + 6 : PIECES + 6 + SECTIONS])
     column = owner_ref[0] * columns + iota((columns, 1), 0)
     high, low = [], []
     for copy, part in zip(queries, parts):
@@ -169,7 +175,7 @@
         low.append(log_sum - high[-1])
     pieces = jnp.concatenate(high + low, axis=0)
     stage_ref[:, BLOCK_WIDTH:] = jnp.concatenate([pieces] * experts, axis=0).astype(BF)
-    first = PIECES + 3 + SECTIONS
+    first = PIECES + 6 + SECTIONS
     copies += [
         pltpu.make_async_copy(stage_ref.at[:, BLOCK_WIDTH:], out_hbm.at[:, BLOCK_WIDTH:], sems.at[first]),
         pltpu.make_async_copy(scores_ref, scores_hbm, sems.at[first + 1]),
@@ -188,18 +194,15 @@
     positives_ref,
     scores_hbm,
     query_hbm,
-    _left_hbm,
-    _right_hbm,
-    out_ref,
-    pieces_ref,
-    code_weights_ref,
-    scores_ref,
-    query_ref,
-    sems,
+    *refs,
 ):
-    copies = [
-        pltpu.make_async_copy(scores_hbm, scores_ref, sems.at[0]),
-        pltpu.make_async_copy(query_hbm, query_ref, sems.at[1]),
+    out_ref, pieces_ref, code_weights_ref, scores_ref, query_ref, sems = refs[-6:]
+    copies = [pltpu.make_async_copy(scores_hbm, scores_ref, sems.at[PIECES])]
+    copies += [
+        pltpu.make_async_copy(
+            query_hbm.at[c * LANES : (c + 1) * LANES], query_ref.at[c * LANES : (c + 1) * LANES], sems.at[c]
+        )
+        for c in range(PIECES)
     ]
     for copy in copies:
         copy.start()
@@ -222,7 +225,8 @@
         rest = rest + rest_ref[:, lanes] * jnp.exp(top_ref[:, lanes] - row_top)
         part = jnp.where(positives_ref[:, lanes] == column, -rest, jnp.exp(scores_ref[:, lanes] - row_top))
         code_weights_ref[:, lanes] = (part * (GRAD_SCALE / total)).astype(BF)
-    copies[1].wait()
+    for copy in copies[1:]:
+        copy.wait()
     out_ref[...] = dot(code_weights_ref[...], query_ref[...]).astype(BF)
 
 
@@ -334,9 +338,11 @@
             )
         )
     ]
-    for copy in copies:
-        copy.start()
+    copies[0].start()
+    copies[1].start()
     copies[0].wait()
+    copies[2].start()
+    copies[3].start()
     unpack_blocks(block_ref, rows_ref)
     copies[1].wait()
     back = dot(rows_ref[...], weights_ref[:, down])
@@ -418,6 +424,7 @@
     units = gate_units[0].T
 
     owner = lax.axis_index("expert")[None]
+    half = w_gate.shape[1] // 2
 
     def exchange(value):
         shape = value.shape
@@ -425,7 +432,7 @@
             value.reshape(owners, BLOCK, shape[1]), "expert", 0, 0, tiled=True
         ).reshape(shape)
 
-    blocks, scores, q, local_top, local_rest, joined = pl.pallas_call(
+    blocks, scores, q, local_top, local_rest, upper, lower = pl.pallas_call(
         functools.partial(dispatch_kernel, experts=owners),
         out_shape=(
             pltpu.HBM((total, BLOCK_WIDTH + LANES), BF),
@@ -433,10 +440,11 @@
             jax.ShapeDtypeStruct((2, tokens), jnp.int32),
             jax.ShapeDtypeStruct((1, queries), F32),
             jax.ShapeDtypeStruct((1, queries), F32),
-            jax.ShapeDtypeStruct((w_gate.shape[1], 3 * hidden), BF),
+            jax.ShapeDtypeStruct((half, 3 * hidden), BF),
+            jax.ShapeDtypeStruct((half, 3 * hidden), BF),
         ),
         in_specs=[IN_SMEM] + [IN_HBM] * 9,
-        out_specs=(IN_HBM, IN_HBM) + (IN_VMEM,) * 4,
+        out_specs=(IN_HBM, IN_HBM) + (IN_VMEM,) * 5,
         scratch_shapes=[
             pltpu.VMEM((2, tokens), jnp.int32),
             pltpu.VMEM((tokens, width), BF),
@@ -447,7 +455,7 @@
             pltpu.VMEM((columns, queries), F32),
             pltpu.VMEM((tokens, width), BF),
             pltpu.VMEM((total, BLOCK_WIDTH + LANES), BF),
-            pltpu.SemaphoreType.DMA((PIECES + 10 + SECTIONS,)),
+            pltpu.SemaphoreType.DMA((PIECES + 13 + SECTIONS,)),
         ],
         compiler_params=params(16),
         name="dispatch",
@@ -465,7 +473,6 @@
     )
     size = lax.axis_size("dp")
     me = lax.axis_index("dp")
-    half = joined.shape[0] // 2
 
     def ahead(value, step):
         return lax.ppermute(value, "dp", [(d, (d + step) % size) for d in range(size)])
@@ -473,19 +480,23 @@
     def partner(value):
         return lax.ppermute(value, "dp", [(d, d ^ 1) for d in range(size)])
 
-    from_left, from_right = ahead(joined, 2), ahead(joined, size - 2)
+    left, right = 2, size - 2
+    upper_left, lower_right = ahead(upper, left), ahead(lower, right)
+    lower_left, upper_right = ahead(lower, left), ahead(upper, right)
+    partner_upper, partner_lower = partner(upper), partner(lower)
+    moved = [upper_left, lower_right, lower_left, upper_right, partner_upper, partner_lower]
     blocks = exchange(blocks)
     parts = pl.pallas_call(
         weights_kernel,
         out_shape=jax.ShapeDtypeStruct((columns, width), BF),
-        in_specs=[IN_VMEM, IN_SMEM] + [IN_VMEM] * 3 + [IN_HBM] * 4,
+        in_specs=[IN_VMEM, IN_SMEM] + [IN_VMEM] * 3 + [IN_HBM] * (2 + len(moved)),
         out_specs=IN_VMEM,
         scratch_shapes=[
             pltpu.VMEM((total, LANES), F32),
             pltpu.VMEM((columns, queries), BF),
             pltpu.VMEM((columns, queries), F32),
             pltpu.VMEM((queries, width), BF),
-            pltpu.SemaphoreType.DMA((2,)),
+            pltpu.SemaphoreType.DMA((PIECES + 1,)),
         ],
         compiler_params=params(12),
         name="code_weights",
@@ -497,8 +508,7 @@
         positives[None],
         hbm(scores),
         hbm(query_reps),
-        hbm(from_left),
-        hbm(from_right),
+        *[hbm(shard) for shard in moved],
     )
     parts = lax.all_to_all(
         parts.reshape(columns // files, files, width), "dp", 0, 0, tiled=True
@@ -520,22 +530,17 @@
         name="cotangent",
     )(parts, lengths, q)
     cot_blocks = exchange(cot_blocks)
-    joined, from_left, from_right, _ = lax.optimization_barrier((joined, from_left, from_right, parts))
-    shards = [
-        joined,
-        from_left,
-        from_right,
-        ahead(from_left[:half], 2),
-        ahead(from_right[half:], size - 2),
-    ]
-    shards = [hbm(shard) for shard in shards + [partner(shard) for shard in shards]]
-    height = joined.shape[0]
+    moved = lax.optimization_barrier((*moved, parts))[:-1]
+    upper_left, lower_right, lower_left, upper_right, partner_upper, partner_lower = moved
+    shards = [upper_left, lower_left, upper_right, lower_right, ahead(upper_left, left), ahead(lower_right, right)]
+    shards += [partner(shard) for shard in shards]
+    shards = [hbm(shard) for shard in (upper, lower, partner_upper, partner_lower, *shards)]
+    places = [(d, 0, start) for d in (me, me ^ 1) for start in (0, half)]
+    places += [
+        (d, step, start) for d in (me, me ^ 1) for step in (size - 2, 2, 4) for start in (0, half)
+    ]
     order = jnp.stack(
-        [
-            jnp.bitwise_and(d + step, size - 1) * height + start
-            for d in (me, me ^ 1)
-            for step, start in ((0, 0), (size - 2, 0), (2, 0), (4, 0), (4, half))
-        ]
+        [jnp.bitwise_and(d + step, size - 1) * (2 * half) + start for d, step, start in places]
     ).astype(jnp.int32)
 
     rows = owners * SLOTS

time: 191 us -> 193 us (1.010); the launches traced: 187 us -> 192 us
  starting transfers between devices: 48.7 us -> 59.2 us
  waiting for transfers between devices: 49.2 us -> 39.9 us
  blocking collectives: 57.5 us -> 61.5 us
    all_to_all x2, waiting for transfers between devices: 19.1 us -> 11.6 us  [exchange(): lax.all_to_all(value.reshape(owners, BLOCK, shape[1]), 'expert', 0, 0, ti...]
    ppermute x5 -> x8, starting transfers between devices: 10.4 us -> 16.2 us  [partner(): return lax.ppermute(value, 'dp', [(d, d ^ 1) for d in range(size)])]
    ppermute x4 -> x6, starting transfers between devices: 14.1 us -> 18.8 us  [ahead(): lax.ppermute(value, 'dp', [(d, (d + step) % size) for d in range(size)])]
    all_to_all x1, blocking collectives: 47.4 us -> 51.4 us  [exchange(): lax.all_to_all(value.reshape(owners, BLOCK, shape[1]), 'expert', 0, 0, ti...]
    slice x2 -> x0, local copies, waits for them, and re-layouts: 2.21 us -> none  [the longest x1 1.1 us: per_device(): from_right[half:]]
    ppermute x4 -> x6, waiting for transfers between devices: 28.3 us -> 26.3 us  [ahead(): lax.ppermute(value, 'dp', [(d, (d + step) % size) for d in range(size)])]
  transfers between devices with their start and end apart: 11 -> 16, of which waited for: 7 -> 8; matrix products, arithmetic and copies ran while one was open for 1% -> 0% of each run, Pallas kernels for 5% -> 5%
where the time goes in v5:
time: 193 us; the launch traced here: 192 us
  blocking collectives  61.5 us (32%)
  starting transfers between devices  59.2 us (31%)
  waiting for transfers between devices  39.9 us (21%)
  Pallas kernels  29.7 us (15%)
    all_to_all x1, blocking collectives, exchange(): lax.all_to_all(value.reshape(owners, BLOCK, shape[1]), 'expert', 0, 0, ti...  51.4 us
    ppermute x6, waiting for transfers between devices, ahead(): lax.ppermute(value, 'dp', [(d, (d + step) % size) for d in range(size)])  26.3 us
    all_to_all x2, starting transfers between devices, exchange(): lax.all_to_all(value.reshape(owners, BLOCK, shape[1]), 'expert', 0, 0, ti...  24.2 us
    ppermute x6, starting transfers between devices, ahead(): lax.ppermute(value, 'dp', [(d, (d + step) % size) for d in range(size)])  18.8 us
    ppermute x8, starting transfers between devices, partner(): return lax.ppermute(value, 'dp', [(d, d ^ 1) for d in range(size)])  16.2 us
    all_to_all x2, waiting for transfers between devices, exchange(): lax.all_to_all(value.reshape(owners, BLOCK, shape[1]), 'expert', 0, 0, ti...  11.6 us
    all_to_all x1, blocking collectives, per_device(): lax.all_to_all(parts.reshape(columns // files, files, width), 'dp', 0, 0,...  10 us
    pallas_call x1, Pallas kernels, per_device(): pl.pallas_call(backward_kernel, out_shape=jax.ShapeDtypeStruct((total, BL...  9.52 us
  transfers between devices with their start and end apart: 16, of which 8 were waited for; matrix products, arithmetic and copies ran while one was open for 0% of the time, Pallas kernels for 5%

profile of v5, /device:TPU:6, one launch (start us, length us, event | category | flops | bytes accessed | tf_op | source)
XLA Modules:
  0.0 191.7 jit_solution(2786410491653457360)
XLA Ops:
  0.0 4.7 %dispatch.1 = (bf16[512,1664]{1,0:T(8,128)(2,1)}, f32[64,512]{1,0:T(8,128)}, s32[2,128]{1,0:T(2,128)S(1)}, f32[1,512]{1,0:T(1,128)S(1)}, f32[1,512]{1,0:T(1,128)...) custom-call(s32[1]{0:T(128)} %bitcast.owner_ref, s32[2,128]{1,0:T(2,128)} %bitcast.58, ...), custom_call_target="tpu_custom_call" | custom-call | tf_op jit(solution)/shard_map/dispatch/pallas_call | solution.py:435
  4.7 16.7 %all-to-all-start = ((bf16[64,8,1664]{2,1,0:T(8,128)(2,1)}), bf16[64,8,1664]{2,1,0:T(8,128)(2,1)S(1)}, u32[]{:S(2)}, u32[]{:S(2)}) async-start(bf16[64,8,1664]{2,1,0:T(8,128)(2,1)} %bitcast.53), calls=%async_computation | async-start | bytes 3407872 | tf_op jit(solution)/shard_map/all_to_all | solution.py:431
  23.4 2.7 %collective-permute-start.3 = (bf16[128,2304]{1,0:T(8,128)(2,1)S(1)}, bf16[128,2304]{1,0:T(8,128)(2,1)S(1)}, u32[]{:S(2)}, u32[]{:S(2)}) collective-permute-start(bf16[128,2304]{1,0:T(8,128)(2,1)S(1)} %get-tuple-element.26.refs_0_), channel_id=1, source_target_pairs={{0,384},{64,448},{128,0},{192,64},{256,128},{320,192},{384,256},{4... | collective-permute-start | bytes 1769480 | tf_op jit(solution)/shard_map/ppermute | solution.py:478
  26.1 4.3 %collective-permute-start = (bf16[128,2304]{1,0:T(8,128)(2,1)S(1)}, bf16[128,2304]{1,0:T(8,128)(2,1)S(1)}, u32[]{:S(2)}, u32[]{:S(2)}) collective-permute-start(bf16[128,2304]{1,0:T(8,128)(2,1)S(1)} %get-tuple-element.26.refs_0_), channel_id=1, source_target_pairs={{0,128},{64,192},{128,256},{192,320},{256,384},{320,448},{384,0},{... | collective-permute-start | bytes 1769480 | tf_op jit(solution)/shard_map/ppermute | solution.py:478
  32.4 2.1 %collective-permute-start.2 = (bf16[128,2304]{1,0:T(8,128)(2,1)S(1)}, bf16[128,2304]{1,0:T(8,128)(2,1)S(1)}, u32[]{:S(2)}, u32[]{:S(2)}) collective-permute-start(bf16[128,2304]{1,0:T(8,128)(2,1)S(1)} %get-tuple-element.27.refs_1_), channel_id=1, source_target_pairs={{0,128},{64,192},{128,256},{192,320},{256,384},{320,448},{384,0},{... | collective-permute-start | bytes 1769480 | tf_op jit(solution)/shard_map/ppermute | solution.py:478
  34.5 3.7 %collective-permute-start.1 = (bf16[128,2304]{1,0:T(8,128)(2,1)S(1)}, bf16[128,2304]{1,0:T(8,128)(2,1)}, u32[]{:S(2)}, u32[]{:S(2)}) collective-permute-start(bf16[128,2304]{1,0:T(8,128)(2,1)S(1)} %get-tuple-element.27.refs_1_), channel_id=1, source_target_pairs={{0,384},{64,448},{128,0},{192,64},{256,128},{320,192},{384,256},{4... | collective-permute-start | bytes 1769480 | tf_op jit(solution)/shard_map/ppermute | solution.py:478
  38.3 4.3 %collective-permute-done.3.refs_3_.refs_6_ = bf16[128,2304]{1,0:T(8,128)(2,1)S(1)} collective-permute-done((bf16[128,2304]{1,0:T(8,128)(2,1)S(1)}, bf16[128,2304]{1,0:T(8,128)(2,1)S(1)}, u32[]{:S(2)}, u32[]{:S(2)}) %collective-permute-start.3) | collective-permute-done | bytes 589856 | tf_op jit(solution)/shard_map/ppermute | solution.py:478
  44.2 11.9 %collective-permute-done.2.refs_2_.refs_5_ = bf16[128,2304]{1,0:T(8,128)(2,1)S(1)} collective-permute-done((bf16[128,2304]{1,0:T(8,128)(2,1)S(1)}, bf16[128,2304]{1,0:T(8,128)(2,1)S(1)}, u32[]{:S(2)}, u32[]{:S(2)}) %collective-permute-start.2) | collective-permute-done | bytes 589856 | tf_op jit(solution)/shard_map/ppermute | solution.py:478
  56.9 8.7 %all-to-all-done = bf16[64,8,1664]{2,1,0:T(8,128)(2,1)S(1)} async-done(((bf16[64,8,1664]{2,1,0:T(8,128)(2,1)}), bf16[64,8,1664]{2,1,0:T(8,128)(2,1)S(1)}, u32[]{:S(2)}, u32[]{:S(2)}) %all-to-all-start) | async-done | bytes 1703968 | tf_op jit(solution)/shard_map/all_to_all | solution.py:431
  65.7 2.1 %code_weights.1 = bf16[64,2048]{1,0:T(8,128)(2,1)S(1)} custom-call(bf16[512,1664]{1,0:T(8,128)(2,1)S(1)} %bitcast.39, s32[1]{0:T(128)} %bitcast.owner_ref, f32[1,512]{1,0:T(1,128)S(1)} %get-tuple-element.23.top_ref, f32[1,512]{1,0:T(1,128)S(1)} %get-tuple-element.24.rest_ref, s32[1,512]{1,0:T(1,128)S(1)} %bitcast.50, ...), custom_call_target="tpu_custom_call" | custom-call | tf_op jit(solution)/shard_map/code_weights/pallas_call | solution.py:489
  67.8 10.0 %all_to_all.20 = bf16[8,8,2048]{2,1,0:T(8,128)(2,1)S(1)} all-to-all(bf16[8,8,2048]{2,1,0:T(8,128)(2,1)S(1)} %bitcast.45), channel_id=1, replica_groups=mesh['dp'=8,'expert'=64] {'dp'}, dimensions={0} | all-to-all | bytes 524288 | tf_op jit(solution)/shard_map/all_to_all | solution.py:513
  77.9 2.5 %cotangent.1 = (bf16[512,1536]{1,0:T(8,128)(2,1)}, bf16[128,2048]{1,0:T(8,128)(2,1)}) custom-call(bf16[64,2048]{1,0:T(8,128)(2,1)S(1)} %bitcast.46, s32[1,8]{1,0:T(1,128)S(1)} %bitcast.52, s32[2,128]{1,0:T(2,128)S(1)} %get-tuple-element.28.q_ref), custom_call_target="tpu_custom_call" | custom-call | tf_op jit(solution)/shard_map/cotangent/pallas_call | solution.py:516
  80.4 7.5 %all-to-all-start.2 = ((bf16[64,8,1536]{2,1,0:T(8,128)(2,1)}), bf16[64,8,1536]{2,1,0:T(8,128)(2,1)}, u32[]{:S(2)}, u32[]{:S(2)}) async-start(bf16[64,8,1536]{2,1,0:T(8,128)(2,1)} %bitcast.54), calls=%async_computation.2 | async-start | bytes 3145728 | tf_op jit(solution)/shard_map/all_to_all | solution.py:431
  89.8 4.0 %collective-permute-start.6 = (bf16[128,2304]{1,0:T(8,128)(2,1)S(1)}, bf16[128,2304]{1,0:T(8,128)(2,1)}, u32[]{:S(2)}, u32[]{:S(2)}) collective-permute-start(bf16[128,2304]{1,0:T(8,128)(2,1)S(1)} %copy-done.12), channel_id=1, source_target_pairs={{0,128},{64,192},{128,256},{192,320},{256,384},{320,448},{384,0},{... | collective-permute-start | bytes 1769480 | tf_op jit(solution)/shard_map/ppermute | solution.py:478
  95.7 2.1 %collective-permute-start.8 = (bf16[128,2304]{1,0:T(8,128)(2,1)S(1)}, bf16[128,2304]{1,0:T(8,128)(2,1)}, u32[]{:S(2)}, u32[]{:S(2)}) collective-permute-start(bf16[128,2304]{1,0:T(8,128)(2,1)S(1)} %copy-done.12), channel_id=1, source_target_pairs={{0,64},{64,0},{128,192},{192,128},{256,320},{320,256},{384,448},{4... | collective-permute-start | bytes 1769480 | tf_op jit(solution)/shard_map/ppermute | solution.py:481
  97.8 2.2 %collective-permute-start.11 = (bf16[128,2304]{1,0:T(8,128)(2,1)}, bf16[128,2304]{1,0:T(8,128)(2,1)}, u32[]{:S(2)}, u32[]{:S(2)}) collective-permute-start(bf16[128,2304]{1,0:T(8,128)(2,1)} %collective-permute-done.1.refs_1_.refs_7_), channel_id=1, source_target_pairs={{0,64},{64,0},{128,192},{192,128},{256,320},{320,256},{384,448},{4... | collective-permute-start | bytes 1769480 | tf_op jit(solution)/shard_map/ppermute | solution.py:481
  100.1 2.1 %collective-permute-start.10 = (bf16[128,2304]{1,0:T(8,128)(2,1)S(1)}, bf16[128,2304]{1,0:T(8,128)(2,1)S(1)}, u32[]{:S(2)}, u32[]{:S(2)}) collective-permute-start(bf16[128,2304]{1,0:T(8,128)(2,1)S(1)} %copy-done.10), channel_id=1, source_target_pairs={{0,64},{64,0},{128,192},{192,128},{256,320},{320,256},{384,448},{4... | collective-permute-start | bytes 1769480 | tf_op jit(solution)/shard_map/ppermute | solution.py:481
  102.2 5.3 %collective-permute-done.6.refs_8_ = bf16[128,2304]{1,0:T(8,128)(2,1)} collective-permute-done((bf16[128,2304]{1,0:T(8,128)(2,1)S(1)}, bf16[128,2304]{1,0:T(8,128)(2,1)}, u32[]{:S(2)}, u32[]{:S(2)}) %collective-permute-start.6) | collective-permute-done | bytes 589856 | tf_op jit(solution)/shard_map/ppermute | solution.py:478
  109.4 3.2 %collective-permute-done.7.refs_9_ = bf16[128,2304]{1,0:T(8,128)(2,1)} collective-permute-done((bf16[128,2304]{1,0:T(8,128)(2,1)}, bf16[128,2304]{1,0:T(8,128)(2,1)}, u32[]{:S(2)}, u32[]{:S(2)}) %collective-permute-start.7) | collective-permute-done | bytes 589856 | tf_op jit(solution)/shard_map/ppermute | solution.py:478
  112.7 2.1 %collective-permute-start.13 = (bf16[128,2304]{1,0:T(8,128)(2,1)}, bf16[128,2304]{1,0:T(8,128)(2,1)}, u32[]{:S(2)}, u32[]{:S(2)}) collective-permute-start(bf16[128,2304]{1,0:T(8,128)(2,1)} %collective-permute-done.7.refs_9_), channel_id=1, source_target_pairs={{0,64},{64,0},{128,192},{192,128},{256,320},{320,256},{384,448},{4... | collective-permute-start | bytes 1769480 | tf_op jit(solution)/shard_map/ppermute | solution.py:481
  116.9 9.2 %expert_forward.1 = (bf16[2048,2304]{1,0:T(8,128)(2,1)}, f32[384,1536]{1,0:T(8,128)}) custom-call(s32[16]{0:T(128)S(1)} %stack.67.order_ref, bf16[512,1664]{1,0:T(8,128)(2,1)S(1)} %bitcast.40, bf16[128,2304]{1,0:T(8,128)(2,1)} %copy-done.1, bf16[128,2304]{1,0:T(8,128)(2,1)} %copy-done.2, bf16[128,2304]{1,0:T(8,128)(2,1)} %copy-done.8, ...), custom_call_target="tpu_custom_call" | custom-call | tf_op jit(solution)/shard_map/expert_forward/pallas_call | solution.py:547
  126.1 2.8 %all-to-all-done.2 = bf16[64,8,1536]{2,1,0:T(8,128)(2,1)} async-done(((bf16[64,8,1536]{2,1,0:T(8,128)(2,1)}), bf16[64,8,1536]{2,1,0:T(8,128)(2,1)}, u32[]{:S(2)}, u32[]{:S(2)}) %all-to-all-start.2) | async-done | bytes 1572896 | tf_op jit(solution)/shard_map/all_to_all | solution.py:431
  128.9 9.5 %expert_backward.1 = bf16[512,1536]{1,0:T(8,128)(2,1)S(1)} custom-call(bf16[512,1536]{1,0:T(8,128)(2,1)} %bitcast.15.block_hbm, bf16[2048,2304]{1,0:T(8,128)(2,1)} %get-tuple-element.36.weights_hbm, f32[384,1536]{1,0:T(8,128)} %get-tuple-element.37.factor_hbm), custom_call_target="tpu_custom_call" | custom-call | tf_op jit(solution)/shard_map/expert_backward/pallas_call | solution.py:561
  138.5 51.4 %all_to_all.21 = bf16[64,8,1536]{2,1,0:T(8,128)(2,1)S(1)} all-to-all(bf16[64,8,1536]{2,1,0:T(8,128)(2,1)S(1)} %bitcast.41), channel_id=1, replica_groups=mesh['dp'=8,'expert'=64] {'expert'}, dimensions={0} | all-to-all | bytes 3145728 | tf_op jit(solution)/shard_map/all_to_all | solution.py:431
  (53 shorter events, 15.9 us)
Async XLA Ops:
  4.7 29.8 %copy-start.2 = (bf16[128,2304]{1,0:T(8,128)(2,1)}, bf16[128,2304]{1,0:T(8,128)(2,1)S(1)}, u32[]{:S(2)}) copy-start(bf16[128,2304]{1,0:T(8,128)(2,1)S(1)} %get-tuple-element.27.refs_1_) | copy-start | bytes 1769476
  4.7 61.0 %copy-start.5 = (s32[512]{0:T(512)S(1)}, s32[512]{0:T(512)}, u32[]{:S(2)}) copy-start(s32[512]{0:T(512)} %param.13) | copy-start | bytes 6148
  4.7 61.0 %all-to-all-start = ((bf16[64,8,1664]{2,1,0:T(8,128)(2,1)}), bf16[64,8,1664]{2,1,0:T(8,128)(2,1)S(1)}, u32[]{:S(2)}, u32[]{:S(2)}) async-start(bf16[64,8,1664]{2,1,0:T(8,128)(2,1)} %bitcast.53), calls=%async_computation | async-start | bytes 3407872 | tf_op jit(solution)/shard_map/all_to_all | solution.py:431
  21.4 13.1 %collective-permute-start.4 = (bf16[128,2304]{1,0:T(8,128)(2,1)S(1)}, bf16[128,2304]{1,0:T(8,128)(2,1)S(1)}, u32[]{:S(2)}, u32[]{:S(2)}) collective-permute-start(bf16[128,2304]{1,0:T(8,128)(2,1)S(1)} %get-tuple-element.26.refs_0_), channel_id=1, source_target_pairs={{0,64},{64,0},{128,192},{192,128},{256,320},{320,256},{384,448},{4... | collective-permute-start | bytes 1769480 | tf_op jit(solution)/shard_map/ppermute | solution.py:481
  23.4 19.2 %collective-permute-start.3 = (bf16[128,2304]{1,0:T(8,128)(2,1)S(1)}, bf16[128,2304]{1,0:T(8,128)(2,1)S(1)}, u32[]{:S(2)}, u32[]{:S(2)}) collective-permute-start(bf16[128,2304]{1,0:T(8,128)(2,1)S(1)} %get-tuple-element.26.refs_0_), channel_id=1, source_target_pairs={{0,384},{64,448},{128,0},{192,64},{256,128},{320,192},{384,256},{4... | collective-permute-start | bytes 1769480 | tf_op jit(solution)/shard_map/ppermute | solution.py:478
  26.1 18.1 %collective-permute-start = (bf16[128,2304]{1,0:T(8,128)(2,1)S(1)}, bf16[128,2304]{1,0:T(8,128)(2,1)S(1)}, u32[]{:S(2)}, u32[]{:S(2)}) collective-permute-start(bf16[128,2304]{1,0:T(8,128)(2,1)S(1)} %get-tuple-element.26.refs_0_), channel_id=1, source_target_pairs={{0,128},{64,192},{128,256},{192,320},{256,384},{320,448},{384,0},{... | collective-permute-start | bytes 1769480 | tf_op jit(solution)/shard_map/ppermute | solution.py:478
  30.4 13.7 %collective-permute-start.5 = (bf16[128,2304]{1,0:T(8,128)(2,1)S(1)}, bf16[128,2304]{1,0:T(8,128)(2,1)S(1)}, u32[]{:S(2)}, u32[]{:S(2)}) collective-permute-start(bf16[128,2304]{1,0:T(8,128)(2,1)S(1)} %get-tuple-element.27.refs_1_), channel_id=1, source_target_pairs={{0,64},{64,0},{128,192},{192,128},{256,320},{320,256},{384,448},{4... | collective-permute-start | bytes 1769480 | tf_op jit(solution)/shard_map/ppermute | solution.py:481
  32.4 23.7 %collective-permute-start.2 = (bf16[128,2304]{1,0:T(8,128)(2,1)S(1)}, bf16[128,2304]{1,0:T(8,128)(2,1)S(1)}, u32[]{:S(2)}, u32[]{:S(2)}) collective-permute-start(bf16[128,2304]{1,0:T(8,128)(2,1)S(1)} %get-tuple-element.27.refs_1_), channel_id=1, source_target_pairs={{0,128},{64,192},{128,256},{192,320},{256,384},{320,448},{384,0},{... | collective-permute-start | bytes 1769480 | tf_op jit(solution)/shard_map/ppermute | solution.py:478
  34.5 31.2 %copy-start.8 = (bf16[128,2304]{1,0:T(8,128)(2,1)}, bf16[128,2304]{1,0:T(8,128)(2,1)S(1)}, u32[]{:S(2)}) copy-start(bf16[128,2304]{1,0:T(8,128)(2,1)S(1)} %collective-permute-done.4.refs_4_.refs_2_) | copy-start | bytes 1769476
  34.5 22.4 %collective-permute-start.1 = (bf16[128,2304]{1,0:T(8,128)(2,1)S(1)}, bf16[128,2304]{1,0:T(8,128)(2,1)}, u32[]{:S(2)}, u32[]{:S(2)}) collective-permute-start(bf16[128,2304]{1,0:T(8,128)(2,1)S(1)} %get-tuple-element.27.refs_1_), channel_id=1, source_target_pairs={{0,384},{64,448},{128,0},{192,64},{256,128},{320,192},{384,256},{4... | collective-permute-start | bytes 1769480 | tf_op jit(solution)/shard_map/ppermute | solution.py:478
  77.9 22.2 %copy-start.10 = (bf16[128,2304]{1,0:T(8,128)(2,1)S(1)}, bf16[128,2304]{1,0:T(8,128)(2,1)}, u32[]{:S(2)}) copy-start(bf16[128,2304]{1,0:T(8,128)(2,1)} %copy-done.9) | copy-start | bytes 1769476
  80.4 48.6 %all-to-all-start.2 = ((bf16[64,8,1536]{2,1,0:T(8,128)(2,1)}), bf16[64,8,1536]{2,1,0:T(8,128)(2,1)}, u32[]{:S(2)}, u32[]{:S(2)}) async-start(bf16[64,8,1536]{2,1,0:T(8,128)(2,1)} %bitcast.54), calls=%async_computation.2 | async-start | bytes 3145728 | tf_op jit(solution)/shard_map/all_to_all | solution.py:431
  87.9 12.2 %collective-permute-start.9 = (bf16[128,2304]{1,0:T(8,128)(2,1)S(1)}, bf16[128,2304]{1,0:T(8,128)(2,1)S(1)}, u32[]{:S(2)}, u32[]{:S(2)}) collective-permute-start(bf16[128,2304]{1,0:T(8,128)(2,1)S(1)} %copy-done.15), channel_id=1, source_target_pairs={{0,64},{64,0},{128,192},{192,128},{256,320},{320,256},{384,448},{4... | collective-permute-start | bytes 1769480 | tf_op jit(solution)/shard_map/ppermute | solution.py:481
  89.8 17.7 %collective-permute-start.6 = (bf16[128,2304]{1,0:T(8,128)(2,1)S(1)}, bf16[128,2304]{1,0:T(8,128)(2,1)}, u32[]{:S(2)}, u32[]{:S(2)}) collective-permute-start(bf16[128,2304]{1,0:T(8,128)(2,1)S(1)} %copy-done.12), channel_id=1, source_target_pairs={{0,128},{64,192},{128,256},{192,320},{256,384},{320,448},{384,0},{... | collective-permute-start | bytes 1769480 | tf_op jit(solution)/shard_map/ppermute | solution.py:478
  93.8 18.9 %collective-permute-start.7 = (bf16[128,2304]{1,0:T(8,128)(2,1)}, bf16[128,2304]{1,0:T(8,128)(2,1)}, u32[]{:S(2)}, u32[]{:S(2)}) collective-permute-start(bf16[128,2304]{1,0:T(8,128)(2,1)} %collective-permute-done.1.refs_1_.refs_7_), channel_id=1, source_target_pairs={{0,384},{64,448},{128,0},{192,64},{256,128},{320,192},{384,256},{4... | collective-permute-start | bytes 1769480 | tf_op jit(solution)/shard_map/ppermute | solution.py:478
  95.7 19.2 %collective-permute-start.8 = (bf16[128,2304]{1,0:T(8,128)(2,1)S(1)}, bf16[128,2304]{1,0:T(8,128)(2,1)}, u32[]{:S(2)}, u32[]{:S(2)}) collective-permute-start(bf16[128,2304]{1,0:T(8,128)(2,1)S(1)} %copy-done.12), channel_id=1, source_target_pairs={{0,64},{64,0},{128,192},{192,128},{256,320},{320,256},{384,448},{4... | collective-permute-start | bytes 1769480 | tf_op jit(solution)/shard_map/ppermute | solution.py:481
  97.8 17.1 %collective-permute-start.11 = (bf16[128,2304]{1,0:T(8,128)(2,1)}, bf16[128,2304]{1,0:T(8,128)(2,1)}, u32[]{:S(2)}, u32[]{:S(2)}) collective-permute-start(bf16[128,2304]{1,0:T(8,128)(2,1)} %collective-permute-done.1.refs_1_.refs_7_), channel_id=1, source_target_pairs={{0,64},{64,0},{128,192},{192,128},{256,320},{320,256},{384,448},{4... | collective-permute-start | bytes 1769480 | tf_op jit(solution)/shard_map/ppermute | solution.py:481
  100.1 14.8 %collective-permute-start.10 = (bf16[128,2304]{1,0:T(8,128)(2,1)S(1)}, bf16[128,2304]{1,0:T(8,128)(2,1)S(1)}, u32[]{:S(2)}, u32[]{:S(2)}) collective-permute-start(bf16[128,2304]{1,0:T(8,128)(2,1)S(1)} %copy-done.10), channel_id=1, source_target_pairs={{0,64},{64,0},{128,192},{192,128},{256,320},{320,256},{384,448},{4... | collective-permute-start | bytes 1769480 | tf_op jit(solution)/shard_map/ppermute | solution.py:481
  107.5 7.4 %collective-permute-start.12 = (bf16[128,2304]{1,0:T(8,128)(2,1)}, bf16[128,2304]{1,0:T(8,128)(2,1)}, u32[]{:S(2)}, u32[]{:S(2)}) collective-permute-start(bf16[128,2304]{1,0:T(8,128)(2,1)} %collective-permute-done.6.refs_8_), channel_id=1, source_target_pairs={{0,64},{64,0},{128,192},{192,128},{256,320},{320,256},{384,448},{4... | collective-permute-start | bytes 1769480 | tf_op jit(solution)/shard_map/ppermute | solution.py:481
  112.7 4.2 %collective-permute-start.13 = (bf16[128,2304]{1,0:T(8,128)(2,1)}, bf16[128,2304]{1,0:T(8,128)(2,1)}, u32[]{:S(2)}, u32[]{:S(2)}) collective-permute-start(bf16[128,2304]{1,0:T(8,128)(2,1)} %collective-permute-done.7.refs_9_), channel_id=1, source_target_pairs={{0,64},{64,0},{128,192},{192,128},{256,320},{320,256},{384,448},{4... | collective-permute-start | bytes 1769480 | tf_op jit(solution)/shard_map/ppermute | solution.py:481
  138.5 51.5 %copy-start = (bf16[1,128,2048]{2,1,0:T(8,128)(2,1)S(1)}, bf16[1,128,2048]{2,1,0:T(8,128)(2,1)}, u32[]{:S(2)}) copy-start(bf16[1,128,2048]{2,1,0:T(8,128)(2,1)} %param.15) | copy-start | bytes 1572868
  138.5 51.5 %copy-start.3 = (bf16[128,2048]{1,0:T(8,128)(2,1)S(1)}, bf16[128,2048]{1,0:T(8,128)(2,1)}, u32[]{:S(2)}) copy-start(bf16[128,2048]{1,0:T(8,128)(2,1)} %get-tuple-element.38.token_ref) | copy-start | bytes 1572868
  138.5 51.4 %copy-start.4 = (bf16[2048]{0:T(1024)(128)(2,1)S(1)}, bf16[2048]{0:T(1024)(128)(2,1)}, u32[]{:S(2)}) copy-start(bf16[2048]{0:T(1024)(128)(2,1)} %param.16) | copy-start | bytes 12292
  138.5 51.4 %copy-start.6 = (s32[1,128,2]{1,2,0:T(2,128)S(1)}, s32[1,128,2]{1,2,0:T(2,128)}, u32[]{:S(2)}) copy-start(s32[1,128,2]{1,2,0:T(2,128)} %param.18) | copy-start | bytes 3076
  (10 other events, 103.1 us)

commit v6 on v5

--- a/solution.py
+++ b/solution.py
@@ -295,13 +295,18 @@
             ).astype(BF)
 
 
+def place_rows(shards, order_ref, target_ref, columns, sems, first):
+    copies = []
+    for n, shard in enumerate(shards):
+        rows = pl.ds(pl.multiple_of(order_ref[n], LANES), shard.shape[0])
+        copies.append(pltpu.make_async_copy(shard.at[:, columns], target_ref.at[rows], sems.at[first + n]))
+    return copies
+
+
 def forward_kernel(order_ref, block_ref, *refs):
     *shards, weights_hbm, factor_hbm, weights_ref, factor_ref, rows_ref, sems = refs
     hidden = factor_ref.shape[1] // 2
-    copies = []
-    for n, shard in enumerate(shards):
-        rows = pl.ds(pl.multiple_of(order_ref[n], LANES), shard.shape[0])
-        copies.append(pltpu.make_async_copy(shard, weights_ref.at[rows], sems.at[n]))
+    copies = place_rows(shards, order_ref, weights_ref, slice(0, 2 * hidden), sems, 0)
     for copy in copies:
         copy.start()
     unpack_blocks(block_ref, rows_ref)
@@ -313,7 +318,7 @@
     ]
     keep[0].start()
     gate_pre = dot(rows_ref[...], weights_ref[:, :hidden])
-    up_pre = dot(rows_ref[...], weights_ref[:, hidden : 2 * hidden])
+    up_pre = dot(rows_ref[...], weights_ref[:, hidden:])
     s = jax.nn.sigmoid(gate_pre)
     factor_ref[:, :hidden] = up_pre * s * (1.0 + gate_pre * (1.0 - s))
     factor_ref[:, hidden:] = gate_pre * s
@@ -322,36 +327,29 @@
         copy.wait()
 
 
-def backward_kernel(
-    block_hbm, weights_hbm, factor_hbm, out_ref, block_ref, weights_ref, factor_ref, rows_ref, hidden_ref, sems
-):
+def backward_kernel(order_ref, block_hbm, weights_hbm, factor_hbm, *refs):
+    *shards, out_ref, block_ref, weights_ref, down_ref, factor_ref, rows_ref, hidden_ref, sems = refs
     hidden = factor_ref.shape[1] // 2
-    down, rest = slice(2 * hidden, 3 * hidden), slice(0, 2 * hidden)
-    copies = [
-        pltpu.make_async_copy(source, target, sems.at[n])
-        for n, (source, target) in enumerate(
-            (
-                (block_hbm, block_ref),
-                (weights_hbm.at[:, down], weights_ref.at[:, down]),
-                (factor_hbm, factor_ref),
-                (weights_hbm.at[:, rest], weights_ref.at[:, rest]),
-            )
-        )
-    ]
-    copies[0].start()
-    copies[1].start()
-    copies[0].wait()
-    copies[2].start()
-    copies[3].start()
+    block = pltpu.make_async_copy(block_hbm, block_ref, sems.at[0])
+    factor = pltpu.make_async_copy(factor_hbm, factor_ref, sems.at[1])
+    weights = pltpu.make_async_copy(weights_hbm, weights_ref, sems.at[2])
+    down = place_rows(shards, order_ref, down_ref, slice(2 * hidden, 3 * hidden), sems, 3)
+    block.start()
+    for copy in down:
+        copy.start()
+    block.wait()
+    factor.start()
+    weights.start()
     unpack_blocks(block_ref, rows_ref)
-    copies[1].wait()
-    back = dot(rows_ref[...], weights_ref[:, down])
-    copies[2].wait()
+    for copy in down:
+        copy.wait()
+    back = dot(rows_ref[...], down_ref[...])
+    factor.wait()
     hidden_ref[:, :hidden] = (back * factor_ref[:, :hidden]).astype(BF)
     hidden_ref[:, hidden:] = (back * factor_ref[:, hidden:]).astype(BF)
-    copies[3].wait()
+    weights.wait()
     for k in range(SECTIONS + 1):
-        rows_ref[:, section(k)] = dot_last(hidden_ref[...], weights_ref[section(k), rest]).astype(BF)
+        rows_ref[:, section(k)] = dot_last(hidden_ref[...], weights_ref[section(k), :]).astype(BF)
     pack_blocks(rows_ref, out_ref)
 
 
@@ -484,7 +482,9 @@
     upper_left, lower_right = ahead(upper, left), ahead(lower, right)
     lower_left, upper_right = ahead(lower, left), ahead(upper, right)
     partner_upper, partner_lower = partner(upper), partner(lower)
+    partner_upper_left, partner_upper_right = partner(upper_left), partner(upper_right)
     moved = [upper_left, lower_right, lower_left, upper_right, partner_upper, partner_lower]
+    moved += [partner_upper_left, partner_upper_right]
     blocks = exchange(blocks)
     parts = pl.pallas_call(
         weights_kernel,
@@ -531,10 +531,14 @@
     )(parts, lengths, q)
     cot_blocks = exchange(cot_blocks)
     moved = lax.optimization_barrier((*moved, parts))[:-1]
-    upper_left, lower_right, lower_left, upper_right, partner_upper, partner_lower = moved
-    shards = [upper_left, lower_left, upper_right, lower_right, ahead(upper_left, left), ahead(lower_right, right)]
-    shards += [partner(shard) for shard in shards]
-    shards = [hbm(shard) for shard in (upper, lower, partner_upper, partner_lower, *shards)]
+    upper_left, lower_right, lower_left, upper_right, partner_upper, partner_lower = moved[:6]
+    partner_upper_left, partner_upper_right = moved[6:]
+    upper_across, lower_across = ahead(upper_left, left), ahead(lower_right, right)
+    shards = [upper, lower, partner_upper, partner_lower]
+    shards += [upper_left, lower_left, upper_right, lower_right, upper_across, lower_across]
+    shards += [partner_upper_left, partner(lower_left), partner_upper_right, partner(lower_right)]
+    shards += [partner(upper_across), partner(lower_across)]
+    shards = [hbm(shard) for shard in shards]
     places = [(d, 0, start) for d in (me, me ^ 1) for start in (0, half)]
     places += [
         (d, step, start) for d in (me, me ^ 1) for step in (size - 2, 2, 4) for start in (0, half)
@@ -546,11 +550,11 @@
     rows = owners * SLOTS
     weights, factor = pl.pallas_call(
         forward_kernel,
-        out_shape=(pltpu.HBM((width, 3 * hidden), BF), pltpu.HBM((rows, 2 * hidden), F32)),
+        out_shape=(pltpu.HBM((width, 2 * hidden), BF), pltpu.HBM((rows, 2 * hidden), F32)),
         in_specs=[IN_SMEM, IN_VMEM] + [IN_HBM] * len(shards),
         out_specs=(IN_HBM, IN_HBM),
         scratch_shapes=[
-            pltpu.VMEM((width, 3 * hidden), BF),
+            pltpu.VMEM((width, 2 * hidden), BF),
             pltpu.VMEM((rows, 2 * hidden), F32),
             pltpu.VMEM((rows, width), BF),
             pltpu.SemaphoreType.DMA((len(shards) + 2,)),
@@ -561,19 +565,20 @@
     result = pl.pallas_call(
         backward_kernel,
         out_shape=jax.ShapeDtypeStruct((total, BLOCK_WIDTH), BF),
-        in_specs=[IN_HBM] * 3,
+        in_specs=[IN_SMEM] + [IN_HBM] * (3 + len(shards)),
         out_specs=IN_VMEM,
         scratch_shapes=[
             pltpu.VMEM((total, BLOCK_WIDTH), BF),
-            pltpu.VMEM((width, 3 * hidden), BF),
+            pltpu.VMEM((width, 2 * hidden), BF),
+            pltpu.VMEM((width, hidden), BF),
             pltpu.VMEM((rows, 2 * hidden), F32),
             pltpu.VMEM((rows, width), BF),
             pltpu.VMEM((rows, 2 * hidden), BF),
-            pltpu.SemaphoreType.DMA((4,)),
+            pltpu.SemaphoreType.DMA((len(shards) + 3,)),
         ],
         compiler_params=params(32),
         name="expert_backward",
-    )(hbm(cot_blocks), hbm(weights), hbm(factor))
+    )(order, hbm(cot_blocks), hbm(weights), hbm(factor), *shards)
 
     token_grad = pl.pallas_call(
         finish_kernel,

time: 193 us -> 189 us (0.979)
  blocking collectives: 61.5 us -> 56.8 us
    all_to_all x1, blocking collectives: 51.4 us -> 46.7 us  [exchange(): lax.all_to_all(value.reshape(owners, BLOCK, shape[1]), 'expert', 0, 0, ti...]
    all_to_all x2, waiting for transfers between devices: 11.6 us -> 14.9 us  [exchange(): lax.all_to_all(value.reshape(owners, BLOCK, shape[1]), 'expert', 0, 0, ti...]
    ppermute x6, waiting for transfers between devices: 26.3 us -> 23.1 us  [ahead(): lax.ppermute(value, 'dp', [(d, (d + step) % size) for d in range(size)])]
  transfers between devices with their start and end apart: 16 -> 16, of which waited for: 8 -> 8; matrix products, arithmetic and copies ran while one was open for 0% -> 0% of each run, Pallas kernels for 5% -> 4%
where the time goes in v6:
time: 189 us; the launch traced here: 188 us
  starting transfers between devices  59 us (31%)
  blocking collectives  56.8 us (30%)
  waiting for transfers between devices  40.1 us (21%)
  Pallas kernels  29.3 us (16%)
  local copies, waits for them, and re-layouts  2.14 us (1%)
    all_to_all x1, blocking collectives, exchange(): lax.all_to_all(value.reshape(owners, BLOCK, shape[1]), 'expert', 0, 0, ti...  46.7 us
    all_to_all x2, starting transfers between devices, exchange(): lax.all_to_all(value.reshape(owners, BLOCK, shape[1]), 'expert', 0, 0, ti...  24.2 us
    ppermute x6, waiting for transfers between devices, ahead(): lax.ppermute(value, 'dp', [(d, (d + step) % size) for d in range(size)])  23.1 us
    ppermute x6, starting transfers between devices, ahead(): lax.ppermute(value, 'dp', [(d, (d + step) % size) for d in range(size)])  18.8 us
    ppermute x8, starting transfers between devices, partner(): return lax.ppermute(value, 'dp', [(d, d ^ 1) for d in range(size)])  16 us
    all_to_all x2, waiting for transfers between devices, exchange(): lax.all_to_all(value.reshape(owners, BLOCK, shape[1]), 'expert', 0, 0, ti...  14.9 us
    pallas_call x1, Pallas kernels, per_device(): pl.pallas_call(backward_kernel, out_shape=jax.ShapeDtypeStruct((total, BL...  10.2 us
    all_to_all x1, blocking collectives, per_device(): lax.all_to_all(parts.reshape(columns // files, files, width), 'dp', 0, 0,...  10 us
  transfers between devices with their start and end apart: 16, of which 8 were waited for; matrix products, arithmetic and copies ran while one was open for 0% of the time, Pallas kernels for 4%

profile of v6, /device:TPU:6, one launch (start us, length us, event | category | flops | bytes accessed | tf_op | source)
XLA Modules:
  0.0 187.6 jit_solution(11088867904852132701)
XLA Ops:
  0.0 4.7 %dispatch.1 = (bf16[512,1664]{1,0:T(8,128)(2,1)}, f32[64,512]{1,0:T(8,128)}, s32[2,128]{1,0:T(2,128)S(1)}, f32[1,512]{1,0:T(1,128)S(1)}, f32[1,512]{1,0:T(1,128)...) custom-call(s32[1]{0:T(128)} %bitcast.16.owner_ref, s32[2,128]{1,0:T(2,128)} %bitcast.58, ...), custom_call_target="tpu_custom_call" | custom-call | tf_op jit(solution)/shard_map/dispatch/pallas_call | solution.py:433
  4.7 16.7 %all-to-all-start = ((bf16[64,8,1664]{2,1,0:T(8,128)(2,1)}), bf16[64,8,1664]{2,1,0:T(8,128)(2,1)S(1)}, u32[]{:S(2)}, u32[]{:S(2)}) async-start(bf16[64,8,1664]{2,1,0:T(8,128)(2,1)} %bitcast.53), calls=%async_computation | async-start | bytes 3407872 | tf_op jit(solution)/shard_map/all_to_all | solution.py:429
  21.4 2.4 %collective-permute-start = (bf16[128,2304]{1,0:T(8,128)(2,1)S(1)}, bf16[128,2304]{1,0:T(8,128)(2,1)S(1)}, u32[]{:S(2)}, u32[]{:S(2)}) collective-permute-start(bf16[128,2304]{1,0:T(8,128)(2,1)S(1)} %get-tuple-element.28.refs_0_), channel_id=1, source_target_pairs={{0,128},{64,192},{128,256},{192,320},{256,384},{320,448},{384,0},{... | collective-permute-start | bytes 1769480 | tf_op jit(solution)/shard_map/ppermute | solution.py:476
  23.8 3.5 %collective-permute-start.3 = (bf16[128,2304]{1,0:T(8,128)(2,1)S(1)}, bf16[128,2304]{1,0:T(8,128)(2,1)S(1)}, u32[]{:S(2)}, u32[]{:S(2)}) collective-permute-start(bf16[128,2304]{1,0:T(8,128)(2,1)S(1)} %get-tuple-element.28.refs_0_), channel_id=1, source_target_pairs={{0,384},{64,448},{128,0},{192,64},{256,128},{320,192},{384,256},{4... | collective-permute-start | bytes 1769480 | tf_op jit(solution)/shard_map/ppermute | solution.py:476
  27.3 2.7 %collective-permute-start.1 = (bf16[128,2304]{1,0:T(8,128)(2,1)S(1)}, bf16[128,2304]{1,0:T(8,128)(2,1)S(1)}, u32[]{:S(2)}, u32[]{:S(2)}) collective-permute-start(bf16[128,2304]{1,0:T(8,128)(2,1)S(1)} %get-tuple-element.29.refs_1_), channel_id=1, source_target_pairs={{0,384},{64,448},{128,0},{192,64},{256,128},{320,192},{384,256},{4... | collective-permute-start | bytes 1769480 | tf_op jit(solution)/shard_map/ppermute | solution.py:476
  30.0 4.3 %collective-permute-start.2 = (bf16[128,2304]{1,0:T(8,128)(2,1)S(1)}, bf16[128,2304]{1,0:T(8,128)(2,1)S(1)}, u32[]{:S(2)}, u32[]{:S(2)}) collective-permute-start(bf16[128,2304]{1,0:T(8,128)(2,1)S(1)} %get-tuple-element.29.refs_1_), channel_id=1, source_target_pairs={{0,128},{64,192},{128,256},{192,320},{256,384},{320,448},{384,0},{... | collective-permute-start | bytes 1769480 | tf_op jit(solution)/shard_map/ppermute | solution.py:476
  36.3 3.3 %collective-permute-done.refs_0_.refs_4_ = bf16[128,2304]{1,0:T(8,128)(2,1)S(1)} collective-permute-done((bf16[128,2304]{1,0:T(8,128)(2,1)S(1)}, bf16[128,2304]{1,0:T(8,128)(2,1)S(1)}, u32[]{:S(2)}, u32[]{:S(2)}) %collective-permute-start) | collective-permute-done | bytes 589856 | tf_op jit(solution)/shard_map/ppermute | solution.py:476
  45.1 9.0 %collective-permute-done.1.refs_1_.refs_7_ = bf16[128,2304]{1,0:T(8,128)(2,1)S(1)} collective-permute-done((bf16[128,2304]{1,0:T(8,128)(2,1)S(1)}, bf16[128,2304]{1,0:T(8,128)(2,1)S(1)}, u32[]{:S(2)}, u32[]{:S(2)}) %collective-permute-start.1) | collective-permute-done | bytes 589856 | tf_op jit(solution)/shard_map/ppermute | solution.py:476
  58.1 7.6 %all-to-all-done = bf16[64,8,1664]{2,1,0:T(8,128)(2,1)S(1)} async-done(((bf16[64,8,1664]{2,1,0:T(8,128)(2,1)}), bf16[64,8,1664]{2,1,0:T(8,128)(2,1)S(1)}, u32[]{:S(2)}, u32[]{:S(2)}) %all-to-all-start) | async-done | bytes 1703968 | tf_op jit(solution)/shard_map/all_to_all | solution.py:429
  65.7 2.1 %code_weights.1 = bf16[64,2048]{1,0:T(8,128)(2,1)S(1)} custom-call(bf16[512,1664]{1,0:T(8,128)(2,1)S(1)} %bitcast.39, s32[1]{0:T(128)} %bitcast.16.owner_ref, f32[1,512]{1,0:T(1,128)S(1)} %get-tuple-element.25.top_ref, f32[1,512]{1,0:T(1,128)S(1)} %get-tuple-element.26.rest_ref, s32[1,512]{1,0:T(1,128)S(1)} %bitcast.50, ...), custom_call_target="tpu_custom_call" | custom-call | tf_op jit(solution)/shard_map/code_weights/pallas_call | solution.py:489
  67.8 10.0 %all_to_all.20 = bf16[8,8,2048]{2,1,0:T(8,128)(2,1)S(1)} all-to-all(bf16[8,8,2048]{2,1,0:T(8,128)(2,1)S(1)} %bitcast.45), channel_id=1, replica_groups=mesh['dp'=8,'expert'=64] {'dp'}, dimensions={0} | all-to-all | bytes 524288 | tf_op jit(solution)/shard_map/all_to_all | solution.py:513
  77.9 2.5 %cotangent.1 = (bf16[512,1536]{1,0:T(8,128)(2,1)}, bf16[128,2048]{1,0:T(8,128)(2,1)}) custom-call(bf16[64,2048]{1,0:T(8,128)(2,1)S(1)} %bitcast.46, s32[1,8]{1,0:T(1,128)S(1)} %bitcast.52, s32[2,128]{1,0:T(2,128)S(1)} %get-tuple-element.30.q_ref), custom_call_target="tpu_custom_call" | custom-call | tf_op jit(solution)/shard_map/cotangent/pallas_call | solution.py:516
  80.4 7.5 %all-to-all-start.2 = ((bf16[64,8,1536]{2,1,0:T(8,128)(2,1)}), bf16[64,8,1536]{2,1,0:T(8,128)(2,1)}, u32[]{:S(2)}, u32[]{:S(2)}) async-start(bf16[64,8,1536]{2,1,0:T(8,128)(2,1)} %bitcast.54), calls=%async_computation.2 | async-start | bytes 3145728 | tf_op jit(solution)/shard_map/all_to_all | solution.py:429
  87.9 4.0 %collective-permute-start.8 = (bf16[128,2304]{1,0:T(8,128)(2,1)S(1)}, bf16[128,2304]{1,0:T(8,128)(2,1)}, u32[]{:S(2)}, u32[]{:S(2)}) collective-permute-start(bf16[128,2304]{1,0:T(8,128)(2,1)S(1)} %copy-done.9), channel_id=1, source_target_pairs={{0,128},{64,192},{128,256},{192,320},{256,384},{320,448},{384,0},{... | collective-permute-start | bytes 1769480 | tf_op jit(solution)/shard_map/ppermute | solution.py:476
  91.8 1.9 %collective-permute-start.9 = (bf16[128,2304]{1,0:T(8,128)(2,1)S(1)}, bf16[128,2304]{1,0:T(8,128)(2,1)}, u32[]{:S(2)}, u32[]{:S(2)}) collective-permute-start(bf16[128,2304]{1,0:T(8,128)(2,1)S(1)} %copy-done.12), channel_id=1, source_target_pairs={{0,384},{64,448},{128,0},{192,64},{256,128},{320,192},{384,256},{4... | collective-permute-start | bytes 1769480 | tf_op jit(solution)/shard_map/ppermute | solution.py:476
  95.7 2.4 %collective-permute-start.10 = (bf16[128,2304]{1,0:T(8,128)(2,1)S(1)}, bf16[128,2304]{1,0:T(8,128)(2,1)}, u32[]{:S(2)}, u32[]{:S(2)}) collective-permute-start(bf16[128,2304]{1,0:T(8,128)(2,1)S(1)} %copy-done.14), channel_id=1, source_target_pairs={{0,64},{64,0},{128,192},{192,128},{256,320},{320,256},{384,448},{4... | collective-permute-start | bytes 1769480 | tf_op jit(solution)/shard_map/ppermute | solution.py:479
  98.1 6.1 %collective-permute-done.8.refs_8_ = bf16[128,2304]{1,0:T(8,128)(2,1)} collective-permute-done((bf16[128,2304]{1,0:T(8,128)(2,1)S(1)}, bf16[128,2304]{1,0:T(8,128)(2,1)}, u32[]{:S(2)}, u32[]{:S(2)}) %collective-permute-start.8) | collective-permute-done | bytes 589856 | tf_op jit(solution)/shard_map/ppermute | solution.py:476
  106.2 3.0 %collective-permute-done.9.refs_9_ = bf16[128,2304]{1,0:T(8,128)(2,1)} collective-permute-done((bf16[128,2304]{1,0:T(8,128)(2,1)S(1)}, bf16[128,2304]{1,0:T(8,128)(2,1)}, u32[]{:S(2)}, u32[]{:S(2)}) %collective-permute-start.9) | collective-permute-done | bytes 589856 | tf_op jit(solution)/shard_map/ppermute | solution.py:476
  109.2 2.1 %collective-permute-start.13 = (bf16[128,2304]{1,0:T(8,128)(2,1)}, bf16[128,2304]{1,0:T(8,128)(2,1)}, u32[]{:S(2)}, u32[]{:S(2)}) collective-permute-start(bf16[128,2304]{1,0:T(8,128)(2,1)} %collective-permute-done.9.refs_9_), channel_id=1, source_target_pairs={{0,64},{64,0},{128,192},{192,128},{256,320},{320,256},{384,448},{4... | collective-permute-start | bytes 1769480 | tf_op jit(solution)/shard_map/ppermute | solution.py:479
  111.5 2.0 %collective-permute-done.13.refs_15_ = bf16[128,2304]{1,0:T(8,128)(2,1)} collective-permute-done((bf16[128,2304]{1,0:T(8,128)(2,1)}, bf16[128,2304]{1,0:T(8,128)(2,1)}, u32[]{:S(2)}, u32[]{:S(2)}) %collective-permute-start.13) | collective-permute-done | bytes 589856 | tf_op jit(solution)/shard_map/ppermute | solution.py:479
  113.4 8.1 %expert_forward.1 = (bf16[2048,1536]{1,0:T(8,128)(2,1)}, f32[384,1536]{1,0:T(8,128)}) custom-call(s32[16]{0:T(128)S(1)} %stack.67.order_ref, bf16[512,1664]{1,0:T(8,128)(2,1)S(1)} %bitcast.40, bf16[128,2304]{1,0:T(8,128)(2,1)} %copy-done, bf16[128,2304]{1,0:T(8,128)(2,1)} %copy-done.1, bf16[128,2304]{1,0:T(8,128)(2,1)} %copy-done.15, ...), custom_call_target="tpu_custom_call" | custom-call | tf_op jit(solution)/shard_map/expert_forward/pallas_call | solution.py:551
  121.6 7.4 %all-to-all-done.2 = bf16[64,8,1536]{2,1,0:T(8,128)(2,1)} async-done(((bf16[64,8,1536]{2,1,0:T(8,128)(2,1)}), bf16[64,8,1536]{2,1,0:T(8,128)(2,1)}, u32[]{:S(2)}, u32[]{:S(2)}) %all-to-all-start.2) | async-done | bytes 1572896 | tf_op jit(solution)/shard_map/all_to_all | solution.py:429
  128.9 10.2 %expert_backward.1 = bf16[512,1536]{1,0:T(8,128)(2,1)S(1)} custom-call(s32[16]{0:T(128)S(1)} %stack.67.order_ref, bf16[512,1536]{1,0:T(8,128)(2,1)} %bitcast.31.block_hbm, bf16[2048,1536]{1,0:T(8,128)(2,1)} %get-tuple-element.40.weights_hbm, f32[384,1536]{1,0:T(8,128)} %get-tuple-element.41.factor_hbm, bf16[128,2304]{1,0:T(8,128)(2,1)} %copy-done, ...), custom_call_target="tpu_custom_call" | custom-call | tf_op jit(solution)/shard_map/expert_backward/pallas_call | solution.py:565
  139.2 46.7 %all_to_all.21 = bf16[64,8,1536]{2,1,0:T(8,128)(2,1)S(1)} all-to-all(bf16[64,8,1536]{2,1,0:T(8,128)(2,1)S(1)} %bitcast.41), channel_id=1, replica_groups=mesh['dp'=8,'expert'=64] {'expert'}, dimensions={0} | all-to-all | bytes 3145728 | tf_op jit(solution)/shard_map/all_to_all | solution.py:429
  (55 shorter events, 17.1 us)
Async XLA Ops:
  4.7 29.7 %copy-start = (bf16[128,2304]{1,0:T(8,128)(2,1)}, bf16[128,2304]{1,0:T(8,128)(2,1)S(1)}, u32[]{:S(2)}) copy-start(bf16[128,2304]{1,0:T(8,128)(2,1)S(1)} %get-tuple-element.28.refs_0_) | copy-start | bytes 1769476
  4.7 34.9 %copy-start.1 = (bf16[128,2304]{1,0:T(8,128)(2,1)}, bf16[128,2304]{1,0:T(8,128)(2,1)S(1)}, u32[]{:S(2)}) copy-start(bf16[128,2304]{1,0:T(8,128)(2,1)S(1)} %get-tuple-element.29.refs_1_) | copy-start | bytes 1769476
  4.7 61.0 %copy-start.5 = (s32[512]{0:T(512)S(1)}, s32[512]{0:T(512)}, u32[]{:S(2)}) copy-start(s32[512]{0:T(512)} %param.13) | copy-start | bytes 6148
  4.7 61.0 %all-to-all-start = ((bf16[64,8,1664]{2,1,0:T(8,128)(2,1)}), bf16[64,8,1664]{2,1,0:T(8,128)(2,1)S(1)}, u32[]{:S(2)}, u32[]{:S(2)}) async-start(bf16[64,8,1664]{2,1,0:T(8,128)(2,1)} %bitcast.53), calls=%async_computation | async-start | bytes 3407872 | tf_op jit(solution)/shard_map/all_to_all | solution.py:429
  21.4 18.1 %collective-permute-start = (bf16[128,2304]{1,0:T(8,128)(2,1)S(1)}, bf16[128,2304]{1,0:T(8,128)(2,1)S(1)}, u32[]{:S(2)}, u32[]{:S(2)}) collective-permute-start(bf16[128,2304]{1,0:T(8,128)(2,1)S(1)} %get-tuple-element.28.refs_0_), channel_id=1, source_target_pairs={{0,128},{64,192},{128,256},{192,320},{256,384},{320,448},{384,0},{... | collective-permute-start | bytes 1769480 | tf_op jit(solution)/shard_map/ppermute | solution.py:476
  23.8 19.4 %collective-permute-start.3 = (bf16[128,2304]{1,0:T(8,128)(2,1)S(1)}, bf16[128,2304]{1,0:T(8,128)(2,1)S(1)}, u32[]{:S(2)}, u32[]{:S(2)}) collective-permute-start(bf16[128,2304]{1,0:T(8,128)(2,1)S(1)} %get-tuple-element.28.refs_0_), channel_id=1, source_target_pairs={{0,384},{64,448},{128,0},{192,64},{256,128},{320,192},{384,256},{4... | collective-permute-start | bytes 1769480 | tf_op jit(solution)/shard_map/ppermute | solution.py:476
  27.3 26.8 %collective-permute-start.1 = (bf16[128,2304]{1,0:T(8,128)(2,1)S(1)}, bf16[128,2304]{1,0:T(8,128)(2,1)S(1)}, u32[]{:S(2)}, u32[]{:S(2)}) collective-permute-start(bf16[128,2304]{1,0:T(8,128)(2,1)S(1)} %get-tuple-element.29.refs_1_), channel_id=1, source_target_pairs={{0,384},{64,448},{128,0},{192,64},{256,128},{320,192},{384,256},{4... | collective-permute-start | bytes 1769480 | tf_op jit(solution)/shard_map/ppermute | solution.py:476
  30.0 26.0 %collective-permute-start.2 = (bf16[128,2304]{1,0:T(8,128)(2,1)S(1)}, bf16[128,2304]{1,0:T(8,128)(2,1)S(1)}, u32[]{:S(2)}, u32[]{:S(2)}) collective-permute-start(bf16[128,2304]{1,0:T(8,128)(2,1)S(1)} %get-tuple-element.29.refs_1_), channel_id=1, source_target_pairs={{0,128},{64,192},{128,256},{192,320},{256,384},{320,448},{384,0},{... | collective-permute-start | bytes 1769480 | tf_op jit(solution)/shard_map/ppermute | solution.py:476
  34.4 21.7 %collective-permute-start.4 = (bf16[128,2304]{1,0:T(8,128)(2,1)S(1)}, bf16[128,2304]{1,0:T(8,128)(2,1)S(1)}, u32[]{:S(2)}, u32[]{:S(2)}) collective-permute-start(bf16[128,2304]{1,0:T(8,128)(2,1)S(1)} %get-tuple-element.28.refs_0_), channel_id=1, source_target_pairs={{0,64},{64,0},{128,192},{192,128},{256,320},{320,256},{384,448},{4... | collective-permute-start | bytes 1769480 | tf_op jit(solution)/shard_map/ppermute | solution.py:479
  39.6 26.1 %copy-start.8 = (bf16[128,2304]{1,0:T(8,128)(2,1)}, bf16[128,2304]{1,0:T(8,128)(2,1)S(1)}, u32[]{:S(2)}) copy-start(bf16[128,2304]{1,0:T(8,128)(2,1)S(1)} %collective-permute-done.refs_0_.refs_4_) | copy-start | bytes 1769476
  39.6 16.5 %collective-permute-start.5 = (bf16[128,2304]{1,0:T(8,128)(2,1)S(1)}, bf16[128,2304]{1,0:T(8,128)(2,1)S(1)}, u32[]{:S(2)}, u32[]{:S(2)}) collective-permute-start(bf16[128,2304]{1,0:T(8,128)(2,1)S(1)} %get-tuple-element.29.refs_1_), channel_id=1, source_target_pairs={{0,64},{64,0},{128,192},{192,128},{256,320},{320,256},{384,448},{4... | collective-permute-start | bytes 1769480 | tf_op jit(solution)/shard_map/ppermute | solution.py:479
  43.2 12.9 %collective-permute-start.6 = (bf16[128,2304]{1,0:T(8,128)(2,1)S(1)}, bf16[128,2304]{1,0:T(8,128)(2,1)S(1)}, u32[]{:S(2)}, u32[]{:S(2)}) collective-permute-start(bf16[128,2304]{1,0:T(8,128)(2,1)S(1)} %collective-permute-done.refs_0_.refs_4_), channel_id=1, source_target_pairs={{0,64},{64,0},{128,192},{192,128},{256,320},{320,256},{384,448},{4... | collective-permute-start | bytes 1769480 | tf_op jit(solution)/shard_map/ppermute | solution.py:479
  54.1 4.0 %collective-permute-start.7 = (bf16[128,2304]{1,0:T(8,128)(2,1)S(1)}, bf16[128,2304]{1,0:T(8,128)(2,1)}, u32[]{:S(2)}, u32[]{:S(2)}) collective-permute-start(bf16[128,2304]{1,0:T(8,128)(2,1)S(1)} %collective-permute-done.3.refs_3_.refs_6_), channel_id=1, source_target_pairs={{0,64},{64,0},{128,192},{192,128},{256,320},{320,256},{384,448},{4... | collective-permute-start | bytes 1769480 | tf_op jit(solution)/shard_map/ppermute | solution.py:479
  80.4 48.6 %all-to-all-start.2 = ((bf16[64,8,1536]{2,1,0:T(8,128)(2,1)}), bf16[64,8,1536]{2,1,0:T(8,128)(2,1)}, u32[]{:S(2)}, u32[]{:S(2)}) async-start(bf16[64,8,1536]{2,1,0:T(8,128)(2,1)} %bitcast.54), calls=%async_computation.2 | async-start | bytes 3145728 | tf_op jit(solution)/shard_map/all_to_all | solution.py:429
  87.9 16.4 %collective-permute-start.8 = (bf16[128,2304]{1,0:T(8,128)(2,1)S(1)}, bf16[128,2304]{1,0:T(8,128)(2,1)}, u32[]{:S(2)}, u32[]{:S(2)}) collective-permute-start(bf16[128,2304]{1,0:T(8,128)(2,1)S(1)} %copy-done.9), channel_id=1, source_target_pairs={{0,128},{64,192},{128,256},{192,320},{256,384},{320,448},{384,0},{... | collective-permute-start | bytes 1769480 | tf_op jit(solution)/shard_map/ppermute | solution.py:476
  91.8 17.3 %collective-permute-start.9 = (bf16[128,2304]{1,0:T(8,128)(2,1)S(1)}, bf16[128,2304]{1,0:T(8,128)(2,1)}, u32[]{:S(2)}, u32[]{:S(2)}) collective-permute-start(bf16[128,2304]{1,0:T(8,128)(2,1)S(1)} %copy-done.12), channel_id=1, source_target_pairs={{0,384},{64,448},{128,0},{192,64},{256,128},{320,192},{384,256},{4... | collective-permute-start | bytes 1769480 | tf_op jit(solution)/shard_map/ppermute | solution.py:476
  93.8 17.6 %collective-permute-start.11 = (bf16[128,2304]{1,0:T(8,128)(2,1)S(1)}, bf16[128,2304]{1,0:T(8,128)(2,1)}, u32[]{:S(2)}, u32[]{:S(2)}) collective-permute-start(bf16[128,2304]{1,0:T(8,128)(2,1)S(1)} %copy-done.12), channel_id=1, source_target_pairs={{0,64},{64,0},{128,192},{192,128},{256,320},{320,256},{384,448},{4... | collective-permute-start | bytes 1769480 | tf_op jit(solution)/shard_map/ppermute | solution.py:479
  95.7 15.7 %collective-permute-start.10 = (bf16[128,2304]{1,0:T(8,128)(2,1)S(1)}, bf16[128,2304]{1,0:T(8,128)(2,1)}, u32[]{:S(2)}, u32[]{:S(2)}) collective-permute-start(bf16[128,2304]{1,0:T(8,128)(2,1)S(1)} %copy-done.14), channel_id=1, source_target_pairs={{0,64},{64,0},{128,192},{192,128},{256,320},{320,256},{384,448},{4... | collective-permute-start | bytes 1769480 | tf_op jit(solution)/shard_map/ppermute | solution.py:479
  104.3 7.2 %collective-permute-start.12 = (bf16[128,2304]{1,0:T(8,128)(2,1)}, bf16[128,2304]{1,0:T(8,128)(2,1)S(1)}, u32[]{:S(2)}, u32[]{:S(2)}) collective-permute-start(bf16[128,2304]{1,0:T(8,128)(2,1)} %collective-permute-done.8.refs_8_), channel_id=1, source_target_pairs={{0,64},{64,0},{128,192},{192,128},{256,320},{320,256},{384,448},{4... | collective-permute-start | bytes 1769480 | tf_op jit(solution)/shard_map/ppermute | solution.py:479
  109.2 4.2 %collective-permute-start.13 = (bf16[128,2304]{1,0:T(8,128)(2,1)}, bf16[128,2304]{1,0:T(8,128)(2,1)}, u32[]{:S(2)}, u32[]{:S(2)}) collective-permute-start(bf16[128,2304]{1,0:T(8,128)(2,1)} %collective-permute-done.9.refs_9_), channel_id=1, source_target_pairs={{0,64},{64,0},{128,192},{192,128},{256,320},{320,256},{384,448},{4... | collective-permute-start | bytes 1769480 | tf_op jit(solution)/shard_map/ppermute | solution.py:479
  139.1 46.8 %copy-start.2 = (bf16[1,128,2048]{2,1,0:T(8,128)(2,1)S(1)}, bf16[1,128,2048]{2,1,0:T(8,128)(2,1)}, u32[]{:S(2)}) copy-start(bf16[1,128,2048]{2,1,0:T(8,128)(2,1)} %param.15) | copy-start | bytes 1572868
  139.1 46.8 %copy-start.3 = (bf16[128,2048]{1,0:T(8,128)(2,1)S(1)}, bf16[128,2048]{1,0:T(8,128)(2,1)}, u32[]{:S(2)}) copy-start(bf16[128,2048]{1,0:T(8,128)(2,1)} %get-tuple-element.42.token_ref) | copy-start | bytes 1572868
  139.1 46.8 %copy-start.4 = (bf16[2048]{0:T(1024)(128)(2,1)S(1)}, bf16[2048]{0:T(1024)(128)(2,1)}, u32[]{:S(2)}) copy-start(bf16[2048]{0:T(1024)(128)(2,1)} %param.16) | copy-start | bytes 12292
  139.2 46.8 %copy-start.6 = (s32[1,128,2]{1,2,0:T(2,128)S(1)}, s32[1,128,2]{1,2,0:T(2,128)}, u32[]{:S(2)}) copy-start(s32[1,128,2]{1,2,0:T(2,128)} %param.18) | copy-start | bytes 3076
  (11 other events, 74.6 us)

commit v7 on v6

--- a/solution.py
+++ b/solution.py
@@ -304,45 +304,70 @@
 
 
 def forward_kernel(order_ref, block_ref, *refs):
-    *shards, weights_hbm, factor_hbm, weights_ref, factor_ref, rows_ref, sems = refs
-    hidden = factor_ref.shape[1] // 2
+    *shards, weights_hbm, down_hbm, factor_hbm, weights_ref, down_ref, factor_ref, rows_ref, sems = refs
+    hidden, count = factor_ref.shape[1] // 2, len(shards)
     copies = place_rows(shards, order_ref, weights_ref, slice(0, 2 * hidden), sems, 0)
+    down = place_rows(shards, order_ref, down_ref, slice(2 * hidden, 3 * hidden), sems, count)
     for copy in copies:
         copy.start()
     unpack_blocks(block_ref, rows_ref)
+    for copy in down:
+        copy.start()
     for copy in copies:
         copy.wait()
     keep = [
-        pltpu.make_async_copy(weights_ref, weights_hbm, sems.at[len(shards)]),
-        pltpu.make_async_copy(factor_ref, factor_hbm, sems.at[len(shards) + 1]),
+        pltpu.make_async_copy(source, target, sems.at[2 * count + n])
+        for n, (source, target) in enumerate(
+            ((weights_ref, weights_hbm), (down_ref, down_hbm), (factor_ref, factor_hbm))
+        )
     ]
     keep[0].start()
     gate_pre = dot(rows_ref[...], weights_ref[:, :hidden])
+    for copy in down:
+        copy.wait()
+    keep[1].start()
     up_pre = dot(rows_ref[...], weights_ref[:, hidden:])
     s = jax.nn.sigmoid(gate_pre)
     factor_ref[:, :hidden] = up_pre * s * (1.0 + gate_pre * (1.0 - s))
     factor_ref[:, hidden:] = gate_pre * s
-    keep[1].start()
+    keep[2].start()
     for copy in keep:
         copy.wait()
 
 
-def backward_kernel(order_ref, block_hbm, weights_hbm, factor_hbm, *refs):
-    *shards, out_ref, block_ref, weights_ref, down_ref, factor_ref, rows_ref, hidden_ref, sems = refs
+def backward_kernel(
+    block_hbm,
+    weights_hbm,
+    down_hbm,
+    factor_hbm,
+    out_ref,
+    block_ref,
+    weights_ref,
+    down_ref,
+    factor_ref,
+    rows_ref,
+    hidden_ref,
+    sems,
+):
     hidden = factor_ref.shape[1] // 2
-    block = pltpu.make_async_copy(block_hbm, block_ref, sems.at[0])
-    factor = pltpu.make_async_copy(factor_hbm, factor_ref, sems.at[1])
-    weights = pltpu.make_async_copy(weights_hbm, weights_ref, sems.at[2])
-    down = place_rows(shards, order_ref, down_ref, slice(2 * hidden, 3 * hidden), sems, 3)
+    block, down, factor, weights = [
+        pltpu.make_async_copy(source, target, sems.at[n])
+        for n, (source, target) in enumerate(
+            (
+                (block_hbm, block_ref),
+                (down_hbm, down_ref),
+                (factor_hbm, factor_ref),
+                (weights_hbm, weights_ref),
+            )
+        )
+    ]
     block.start()
-    for copy in down:
-        copy.start()
+    down.start()
     block.wait()
     factor.start()
     weights.start()
     unpack_blocks(block_ref, rows_ref)
-    for copy in down:
-        copy.wait()
+    down.wait()
     back = dot(rows_ref[...], down_ref[...])
     factor.wait()
     hidden_ref[:, :hidden] = (back * factor_ref[:, :hidden]).astype(BF)
@@ -548,16 +573,21 @@
     ).astype(jnp.int32)
 
     rows = owners * SLOTS
-    weights, factor = pl.pallas_call(
+    weights, down, factor = pl.pallas_call(
         forward_kernel,
-        out_shape=(pltpu.HBM((width, 2 * hidden), BF), pltpu.HBM((rows, 2 * hidden), F32)),
+        out_shape=(
+            pltpu.HBM((width, 2 * hidden), BF),
+            pltpu.HBM((width, hidden), BF),
+            pltpu.HBM((rows, 2 * hidden), F32),
+        ),
         in_specs=[IN_SMEM, IN_VMEM] + [IN_HBM] * len(shards),
-        out_specs=(IN_HBM, IN_HBM),
+        out_specs=(IN_HBM,) * 3,
         scratch_shapes=[
             pltpu.VMEM((width, 2 * hidden), BF),
+            pltpu.VMEM((width, hidden), BF),
             pltpu.VMEM((rows, 2 * hidden), F32),
             pltpu.VMEM((rows, width), BF),
-            pltpu.SemaphoreType.DMA((len(shards) + 2,)),
+            pltpu.SemaphoreType.DMA((2 * len(shards) + 3,)),
         ],
         compiler_params=params(32),
         name="expert_forward",
@@ -565,7 +595,7 @@
     result = pl.pallas_call(
         backward_kernel,
         out_shape=jax.ShapeDtypeStruct((total, BLOCK_WIDTH), BF),
-        in_specs=[IN_SMEM] + [IN_HBM] * (3 + len(shards)),
+        in_specs=[IN_HBM] * 4,
         out_specs=IN_VMEM,
         scratch_shapes=[
             pltpu.VMEM((total, BLOCK_WIDTH), BF),
@@ -574,11 +604,11 @@
             pltpu.VMEM((rows, 2 * hidden), F32),
             pltpu.VMEM((rows, width), BF),
             pltpu.VMEM((rows, 2 * hidden), BF),
-            pltpu.SemaphoreType.DMA((len(shards) + 3,)),
+            pltpu.SemaphoreType.DMA((4,)),
         ],
         compiler_params=params(32),
         name="expert_backward",
-    )(order, hbm(cot_blocks), hbm(weights), hbm(factor), *shards)
+    )(hbm(cot_blocks), hbm(weights), hbm(down), hbm(factor))
 
     token_grad = pl.pallas_call(
         finish_kernel,

time: 189 us -> 189 us (level)
  transfers between devices with their start and end apart: 16 -> 16, of which waited for: 8 -> 7; matrix products, arithmetic and copies ran while one was open for 0% -> 0% of each run, Pallas kernels for 4% -> 5%
where the time goes in v7:
time: 189 us; the launch traced here: 188 us
  starting transfers between devices  59.5 us (31%)
  blocking collectives  57.5 us (30%)
  waiting for transfers between devices  38.7 us (20%)
  Pallas kernels  29.6 us (16%)
  local copies, waits for them, and re-layouts  1.97 us (1%)
    all_to_all x1, blocking collectives, exchange(): lax.all_to_all(value.reshape(owners, BLOCK, shape[1]), 'expert', 0, 0, ti...  47.5 us
    all_to_all x2, starting transfers between devices, exchange(): lax.all_to_all(value.reshape(owners, BLOCK, shape[1]), 'expert', 0, 0, ti...  24.2 us
    ppermute x6, waiting for transfers between devices, ahead(): lax.ppermute(value, 'dp', [(d, (d + step) % size) for d in range(size)])  22.6 us
    ppermute x6, starting transfers between devices, ahead(): lax.ppermute(value, 'dp', [(d, (d + step) % size) for d in range(size)])  18.8 us
    ppermute x8, starting transfers between devices, partner(): return lax.ppermute(value, 'dp', [(d, d ^ 1) for d in range(size)])  16.5 us
    all_to_all x2, waiting for transfers between devices, exchange(): lax.all_to_all(value.reshape(owners, BLOCK, shape[1]), 'expert', 0, 0, ti...  14.1 us
    all_to_all x1, blocking collectives, per_device(): lax.all_to_all(parts.reshape(columns // files, files, width), 'dp', 0, 0,...  10 us
    pallas_call x1, Pallas kernels, per_device(): pl.pallas_call(backward_kernel, out_shape=jax.ShapeDtypeStruct((total, BL...  9.5 us
  transfers between devices with their start and end apart: 16, of which 7 were waited for; matrix products, arithmetic and copies ran while one was open for 0% of the time, Pallas kernels for 5%

profile of v7, /device:TPU:6, one launch (start us, length us, event | category | flops | bytes accessed | tf_op | source)
XLA Modules:
  0.0 187.7 jit_solution(4095463307853080683)
XLA Ops:
  0.0 4.7 %dispatch.1 = (bf16[512,1664]{1,0:T(8,128)(2,1)}, f32[64,512]{1,0:T(8,128)}, s32[2,128]{1,0:T(2,128)S(1)}, f32[1,512]{1,0:T(1,128)S(1)}, f32[1,512]{1,0:T(1,128)...) custom-call(s32[1]{0:T(128)} %bitcast.owner_ref, s32[2,128]{1,0:T(2,128)} %bitcast.58, ...), custom_call_target="tpu_custom_call" | custom-call | tf_op jit(solution)/shard_map/dispatch/pallas_call | solution.py:458
  4.7 16.7 %all-to-all-start = ((bf16[64,8,1664]{2,1,0:T(8,128)(2,1)}), bf16[64,8,1664]{2,1,0:T(8,128)(2,1)S(1)}, u32[]{:S(2)}, u32[]{:S(2)}) async-start(bf16[64,8,1664]{2,1,0:T(8,128)(2,1)} %bitcast.53), calls=%async_computation | async-start | bytes 3407872 | tf_op jit(solution)/shard_map/all_to_all | solution.py:454
  23.4 2.7 %collective-permute-start.3 = (bf16[128,2304]{1,0:T(8,128)(2,1)S(1)}, bf16[128,2304]{1,0:T(8,128)(2,1)S(1)}, u32[]{:S(2)}, u32[]{:S(2)}) collective-permute-start(bf16[128,2304]{1,0:T(8,128)(2,1)S(1)} %get-tuple-element.29.refs_0_), channel_id=1, source_target_pairs={{0,384},{64,448},{128,0},{192,64},{256,128},{320,192},{384,256},{4... | collective-permute-start | bytes 1769480 | tf_op jit(solution)/shard_map/ppermute | solution.py:501
  26.1 4.3 %collective-permute-start = (bf16[128,2304]{1,0:T(8,128)(2,1)S(1)}, bf16[128,2304]{1,0:T(8,128)(2,1)S(1)}, u32[]{:S(2)}, u32[]{:S(2)}) collective-permute-start(bf16[128,2304]{1,0:T(8,128)(2,1)S(1)} %get-tuple-element.29.refs_0_), channel_id=1, source_target_pairs={{0,128},{64,192},{128,256},{192,320},{256,384},{320,448},{384,0},{... | collective-permute-start | bytes 1769480 | tf_op jit(solution)/shard_map/ppermute | solution.py:501
  32.4 2.1 %collective-permute-start.2 = (bf16[128,2304]{1,0:T(8,128)(2,1)S(1)}, bf16[128,2304]{1,0:T(8,128)(2,1)S(1)}, u32[]{:S(2)}, u32[]{:S(2)}) collective-permute-start(bf16[128,2304]{1,0:T(8,128)(2,1)S(1)} %get-tuple-element.30.refs_1_), channel_id=1, source_target_pairs={{0,128},{64,192},{128,256},{192,320},{256,384},{320,448},{384,0},{... | collective-permute-start | bytes 1769480 | tf_op jit(solution)/shard_map/ppermute | solution.py:501
  34.5 3.7 %collective-permute-start.1 = (bf16[128,2304]{1,0:T(8,128)(2,1)S(1)}, bf16[128,2304]{1,0:T(8,128)(2,1)S(1)}, u32[]{:S(2)}, u32[]{:S(2)}) collective-permute-start(bf16[128,2304]{1,0:T(8,128)(2,1)S(1)} %get-tuple-element.30.refs_1_), channel_id=1, source_target_pairs={{0,384},{64,448},{128,0},{192,64},{256,128},{320,192},{384,256},{4... | collective-permute-start | bytes 1769480 | tf_op jit(solution)/shard_map/ppermute | solution.py:501
  38.3 4.3 %collective-permute-done.3.refs_3_.refs_6_ = bf16[128,2304]{1,0:T(8,128)(2,1)S(1)} collective-permute-done((bf16[128,2304]{1,0:T(8,128)(2,1)S(1)}, bf16[128,2304]{1,0:T(8,128)(2,1)S(1)}, u32[]{:S(2)}, u32[]{:S(2)}) %collective-permute-start.3) | collective-permute-done | bytes 589856 | tf_op jit(solution)/shard_map/ppermute | solution.py:501
  44.5 2.4 %collective-permute-start.6 = (bf16[128,2304]{1,0:T(8,128)(2,1)S(1)}, bf16[128,2304]{1,0:T(8,128)(2,1)S(1)}, u32[]{:S(2)}, u32[]{:S(2)}) collective-permute-start(bf16[128,2304]{1,0:T(8,128)(2,1)S(1)} %collective-permute-done.refs_0_.refs_4_), channel_id=1, source_target_pairs={{0,64},{64,0},{128,192},{192,128},{256,320},{320,256},{384,448},{4... | collective-permute-start | bytes 1769480 | tf_op jit(solution)/shard_map/ppermute | solution.py:504
  47.0 9.1 %collective-permute-done.2.refs_2_.refs_5_ = bf16[128,2304]{1,0:T(8,128)(2,1)S(1)} collective-permute-done((bf16[128,2304]{1,0:T(8,128)(2,1)S(1)}, bf16[128,2304]{1,0:T(8,128)(2,1)S(1)}, u32[]{:S(2)}, u32[]{:S(2)}) %collective-permute-start.2) | collective-permute-done | bytes 589856 | tf_op jit(solution)/shard_map/ppermute | solution.py:501
  58.0 7.7 %all-to-all-done = bf16[64,8,1664]{2,1,0:T(8,128)(2,1)S(1)} async-done(((bf16[64,8,1664]{2,1,0:T(8,128)(2,1)}), bf16[64,8,1664]{2,1,0:T(8,128)(2,1)S(1)}, u32[]{:S(2)}, u32[]{:S(2)}) %all-to-all-start) | async-done | bytes 1703968 | tf_op jit(solution)/shard_map/all_to_all | solution.py:454
  65.7 2.1 %code_weights.1 = bf16[64,2048]{1,0:T(8,128)(2,1)S(1)} custom-call(bf16[512,1664]{1,0:T(8,128)(2,1)S(1)} %bitcast.39, s32[1]{0:T(128)} %bitcast.owner_ref, f32[1,512]{1,0:T(1,128)S(1)} %get-tuple-element.26.top_ref, f32[1,512]{1,0:T(1,128)S(1)} %get-tuple-element.27.rest_ref, s32[1,512]{1,0:T(1,128)S(1)} %bitcast.50, ...), custom_call_target="tpu_custom_call" | custom-call | tf_op jit(solution)/shard_map/code_weights/pallas_call | solution.py:514
  67.8 10.0 %all_to_all.20 = bf16[8,8,2048]{2,1,0:T(8,128)(2,1)S(1)} all-to-all(bf16[8,8,2048]{2,1,0:T(8,128)(2,1)S(1)} %bitcast.45), channel_id=1, replica_groups=mesh['dp'=8,'expert'=64] {'dp'}, dimensions={0} | all-to-all | bytes 524288 | tf_op jit(solution)/shard_map/all_to_all | solution.py:538
  77.9 2.5 %cotangent.1 = (bf16[512,1536]{1,0:T(8,128)(2,1)}, bf16[128,2048]{1,0:T(8,128)(2,1)}) custom-call(bf16[64,2048]{1,0:T(8,128)(2,1)S(1)} %bitcast.46, s32[1,8]{1,0:T(1,128)S(1)} %bitcast.52, s32[2,128]{1,0:T(2,128)S(1)} %get-tuple-element.31.q_ref), custom_call_target="tpu_custom_call" | custom-call | tf_op jit(solution)/shard_map/cotangent/pallas_call | solution.py:541
  80.4 7.5 %all-to-all-start.2 = ((bf16[64,8,1536]{2,1,0:T(8,128)(2,1)}), bf16[64,8,1536]{2,1,0:T(8,128)(2,1)}, u32[]{:S(2)}, u32[]{:S(2)}) async-start(bf16[64,8,1536]{2,1,0:T(8,128)(2,1)} %bitcast.54), calls=%async_computation.2 | async-start | bytes 3145728 | tf_op jit(solution)/shard_map/all_to_all | solution.py:454
  87.9 4.0 %collective-permute-start.8 = (bf16[128,2304]{1,0:T(8,128)(2,1)S(1)}, bf16[128,2304]{1,0:T(8,128)(2,1)}, u32[]{:S(2)}, u32[]{:S(2)}) collective-permute-start(bf16[128,2304]{1,0:T(8,128)(2,1)S(1)} %copy-done.11), channel_id=1, source_target_pairs={{0,128},{64,192},{128,256},{192,320},{256,384},{320,448},{384,0},{... | collective-permute-start | bytes 1769480 | tf_op jit(solution)/shard_map/ppermute | solution.py:501
  95.7 2.4 %collective-permute-start.10 = (bf16[128,2304]{1,0:T(8,128)(2,1)S(1)}, bf16[128,2304]{1,0:T(8,128)(2,1)}, u32[]{:S(2)}, u32[]{:S(2)}) collective-permute-start(bf16[128,2304]{1,0:T(8,128)(2,1)S(1)} %copy-done.14), channel_id=1, source_target_pairs={{0,64},{64,0},{128,192},{192,128},{256,320},{320,256},{384,448},{4... | collective-permute-start | bytes 1769480 | tf_op jit(solution)/shard_map/ppermute | solution.py:504
  98.1 6.1 %collective-permute-done.8.refs_8_ = bf16[128,2304]{1,0:T(8,128)(2,1)} collective-permute-done((bf16[128,2304]{1,0:T(8,128)(2,1)S(1)}, bf16[128,2304]{1,0:T(8,128)(2,1)}, u32[]{:S(2)}, u32[]{:S(2)}) %collective-permute-start.8) | collective-permute-done | bytes 589856 | tf_op jit(solution)/shard_map/ppermute | solution.py:501
  106.2 3.0 %collective-permute-done.9.refs_9_ = bf16[128,2304]{1,0:T(8,128)(2,1)} collective-permute-done((bf16[128,2304]{1,0:T(8,128)(2,1)S(1)}, bf16[128,2304]{1,0:T(8,128)(2,1)}, u32[]{:S(2)}, u32[]{:S(2)}) %collective-permute-start.9) | collective-permute-done | bytes 589856 | tf_op jit(solution)/shard_map/ppermute | solution.py:501
  109.2 2.1 %collective-permute-start.13 = (bf16[128,2304]{1,0:T(8,128)(2,1)}, bf16[128,2304]{1,0:T(8,128)(2,1)}, u32[]{:S(2)}, u32[]{:S(2)}) collective-permute-start(bf16[128,2304]{1,0:T(8,128)(2,1)} %collective-permute-done.9.refs_9_), channel_id=1, source_target_pairs={{0,64},{64,0},{128,192},{192,128},{256,320},{320,256},{384,448},{4... | collective-permute-start | bytes 1769480 | tf_op jit(solution)/shard_map/ppermute | solution.py:504
  111.5 2.0 %collective-permute-done.13.refs_15_ = bf16[128,2304]{1,0:T(8,128)(2,1)} collective-permute-done((bf16[128,2304]{1,0:T(8,128)(2,1)}, bf16[128,2304]{1,0:T(8,128)(2,1)}, u32[]{:S(2)}, u32[]{:S(2)}) %collective-permute-start.13) | collective-permute-done | bytes 589856 | tf_op jit(solution)/shard_map/ppermute | solution.py:504
  113.5 9.1 %expert_forward.1 = (bf16[2048,1536]{1,0:T(8,128)(2,1)}, bf16[2048,768]{1,0:T(8,128)(2,1)}, f32[384,1536]{1,0:T(8,128)}) custom-call(s32[16]{0:T(128)S(1)} %stack.67.order_ref, bf16[512,1664]{1,0:T(8,128)(2,1)S(1)} %bitcast.40, bf16[128,2304]{1,0:T(8,128)(2,1)} %copy-done.1, bf16[128,2304]{1,0:T(8,128)(2,1)} %copy-done.2, bf16[128,2304]{1,0:T(8,128)(2,1)} %copy-done.8, ...), custom_call_target="tpu_custom_call" | custom-call | tf_op jit(solution)/shard_map/expert_forward/pallas_call | solution.py:576
  122.6 6.4 %all-to-all-done.2 = bf16[64,8,1536]{2,1,0:T(8,128)(2,1)} async-done(((bf16[64,8,1536]{2,1,0:T(8,128)(2,1)}), bf16[64,8,1536]{2,1,0:T(8,128)(2,1)}, u32[]{:S(2)}, u32[]{:S(2)}) %all-to-all-start.2) | async-done | bytes 1572896 | tf_op jit(solution)/shard_map/all_to_all | solution.py:454
  129.0 9.5 %expert_backward.1 = bf16[512,1536]{1,0:T(8,128)(2,1)S(1)} custom-call(bf16[512,1536]{1,0:T(8,128)(2,1)} %bitcast.15.block_hbm, bf16[2048,1536]{1,0:T(8,128)(2,1)} %get-tuple-element.41.weights_hbm, bf16[2048,768]{1,0:T(8,128)(2,1)} %get-tuple-element.42.down_hbm, f32[384,1536]{1,0:T(8,128)} %get-tuple-element.43.factor_hbm), custom_call_target="tpu_custom_call" | custom-call | tf_op jit(solution)/shard_map/expert_backward/pallas_call | solution.py:595
  138.5 47.5 %all_to_all.21 = bf16[64,8,1536]{2,1,0:T(8,128)(2,1)S(1)} all-to-all(bf16[64,8,1536]{2,1,0:T(8,128)(2,1)S(1)} %bitcast.41), channel_id=1, replica_groups=mesh['dp'=8,'expert'=64] {'expert'}, dimensions={0} | all-to-all | bytes 3145728 | tf_op jit(solution)/shard_map/all_to_all | solution.py:454
  (57 shorter events, 15.2 us)
Async XLA Ops:
  4.7 21.4 %copy-start.1 = (bf16[128,2304]{1,0:T(8,128)(2,1)}, bf16[128,2304]{1,0:T(8,128)(2,1)S(1)}, u32[]{:S(2)}) copy-start(bf16[128,2304]{1,0:T(8,128)(2,1)S(1)} %get-tuple-element.29.refs_0_) | copy-start | bytes 1769476
  4.7 29.8 %copy-start.2 = (bf16[128,2304]{1,0:T(8,128)(2,1)}, bf16[128,2304]{1,0:T(8,128)(2,1)S(1)}, u32[]{:S(2)}) copy-start(bf16[128,2304]{1,0:T(8,128)(2,1)S(1)} %get-tuple-element.30.refs_1_) | copy-start | bytes 1769476
  4.7 61.0 %copy-start.5 = (s32[512]{0:T(512)S(1)}, s32[512]{0:T(512)}, u32[]{:S(2)}) copy-start(s32[512]{0:T(512)} %param.13) | copy-start | bytes 6148
  4.7 61.0 %all-to-all-start = ((bf16[64,8,1664]{2,1,0:T(8,128)(2,1)}), bf16[64,8,1664]{2,1,0:T(8,128)(2,1)S(1)}, u32[]{:S(2)}, u32[]{:S(2)}) async-start(bf16[64,8,1664]{2,1,0:T(8,128)(2,1)} %bitcast.53), calls=%async_computation | async-start | bytes 3407872 | tf_op jit(solution)/shard_map/all_to_all | solution.py:454
  21.4 13.1 %collective-permute-start.4 = (bf16[128,2304]{1,0:T(8,128)(2,1)S(1)}, bf16[128,2304]{1,0:T(8,128)(2,1)S(1)}, u32[]{:S(2)}, u32[]{:S(2)}) collective-permute-start(bf16[128,2304]{1,0:T(8,128)(2,1)S(1)} %get-tuple-element.29.refs_0_), channel_id=1, source_target_pairs={{0,64},{64,0},{128,192},{192,128},{256,320},{320,256},{384,448},{4... | collective-permute-start | bytes 1769480 | tf_op jit(solution)/shard_map/ppermute | solution.py:504
  23.4 19.2 %collective-permute-start.3 = (bf16[128,2304]{1,0:T(8,128)(2,1)S(1)}, bf16[128,2304]{1,0:T(8,128)(2,1)S(1)}, u32[]{:S(2)}, u32[]{:S(2)}) collective-permute-start(bf16[128,2304]{1,0:T(8,128)(2,1)S(1)} %get-tuple-element.29.refs_0_), channel_id=1, source_target_pairs={{0,384},{64,448},{128,0},{192,64},{256,128},{320,192},{384,256},{4... | collective-permute-start | bytes 1769480 | tf_op jit(solution)/shard_map/ppermute | solution.py:501
  26.1 18.4 %collective-permute-start = (bf16[128,2304]{1,0:T(8,128)(2,1)S(1)}, bf16[128,2304]{1,0:T(8,128)(2,1)S(1)}, u32[]{:S(2)}, u32[]{:S(2)}) collective-permute-start(bf16[128,2304]{1,0:T(8,128)(2,1)S(1)} %get-tuple-element.29.refs_0_), channel_id=1, source_target_pairs={{0,128},{64,192},{128,256},{192,320},{256,384},{320,448},{384,0},{... | collective-permute-start | bytes 1769480 | tf_op jit(solution)/shard_map/ppermute | solution.py:501
  30.4 16.5 %collective-permute-start.5 = (bf16[128,2304]{1,0:T(8,128)(2,1)S(1)}, bf16[128,2304]{1,0:T(8,128)(2,1)S(1)}, u32[]{:S(2)}, u32[]{:S(2)}) collective-permute-start(bf16[128,2304]{1,0:T(8,128)(2,1)S(1)} %get-tuple-element.30.refs_1_), channel_id=1, source_target_pairs={{0,64},{64,0},{128,192},{192,128},{256,320},{320,256},{384,448},{4... | collective-permute-start | bytes 1769480 | tf_op jit(solution)/shard_map/ppermute | solution.py:504
  32.4 23.7 %collective-permute-start.2 = (bf16[128,2304]{1,0:T(8,128)(2,1)S(1)}, bf16[128,2304]{1,0:T(8,128)(2,1)S(1)}, u32[]{:S(2)}, u32[]{:S(2)}) collective-permute-start(bf16[128,2304]{1,0:T(8,128)(2,1)S(1)} %get-tuple-element.30.refs_1_), channel_id=1, source_target_pairs={{0,128},{64,192},{128,256},{192,320},{256,384},{320,448},{384,0},{... | collective-permute-start | bytes 1769480 | tf_op jit(solution)/shard_map/ppermute | solution.py:501
  34.5 31.2 %copy-start.8 = (bf16[128,2304]{1,0:T(8,128)(2,1)}, bf16[128,2304]{1,0:T(8,128)(2,1)S(1)}, u32[]{:S(2)}) copy-start(bf16[128,2304]{1,0:T(8,128)(2,1)S(1)} %collective-permute-done.4.refs_4_.refs_2_) | copy-start | bytes 1769476
  34.5 21.6 %collective-permute-start.1 = (bf16[128,2304]{1,0:T(8,128)(2,1)S(1)}, bf16[128,2304]{1,0:T(8,128)(2,1)S(1)}, u32[]{:S(2)}, u32[]{:S(2)}) collective-permute-start(bf16[128,2304]{1,0:T(8,128)(2,1)S(1)} %get-tuple-element.30.refs_1_), channel_id=1, source_target_pairs={{0,384},{64,448},{128,0},{192,64},{256,128},{320,192},{384,256},{4... | collective-permute-start | bytes 1769480 | tf_op jit(solution)/shard_map/ppermute | solution.py:501
  42.6 13.5 %collective-permute-start.7 = (bf16[128,2304]{1,0:T(8,128)(2,1)S(1)}, bf16[128,2304]{1,0:T(8,128)(2,1)S(1)}, u32[]{:S(2)}, u32[]{:S(2)}) collective-permute-start(bf16[128,2304]{1,0:T(8,128)(2,1)S(1)} %collective-permute-done.3.refs_3_.refs_6_), channel_id=1, source_target_pairs={{0,64},{64,0},{128,192},{192,128},{256,320},{320,256},{384,448},{4... | collective-permute-start | bytes 1769480 | tf_op jit(solution)/shard_map/ppermute | solution.py:504
  44.5 13.4 %collective-permute-start.6 = (bf16[128,2304]{1,0:T(8,128)(2,1)S(1)}, bf16[128,2304]{1,0:T(8,128)(2,1)S(1)}, u32[]{:S(2)}, u32[]{:S(2)}) collective-permute-start(bf16[128,2304]{1,0:T(8,128)(2,1)S(1)} %collective-permute-done.refs_0_.refs_4_), channel_id=1, source_target_pairs={{0,64},{64,0},{128,192},{192,128},{256,320},{320,256},{384,448},{4... | collective-permute-start | bytes 1769480 | tf_op jit(solution)/shard_map/ppermute | solution.py:504
  80.4 48.6 %all-to-all-start.2 = ((bf16[64,8,1536]{2,1,0:T(8,128)(2,1)}), bf16[64,8,1536]{2,1,0:T(8,128)(2,1)}, u32[]{:S(2)}, u32[]{:S(2)}) async-start(bf16[64,8,1536]{2,1,0:T(8,128)(2,1)} %bitcast.54), calls=%async_computation.2 | async-start | bytes 3145728 | tf_op jit(solution)/shard_map/all_to_all | solution.py:454
  87.9 16.4 %collective-permute-start.8 = (bf16[128,2304]{1,0:T(8,128)(2,1)S(1)}, bf16[128,2304]{1,0:T(8,128)(2,1)}, u32[]{:S(2)}, u32[]{:S(2)}) collective-permute-start(bf16[128,2304]{1,0:T(8,128)(2,1)S(1)} %copy-done.11), channel_id=1, source_target_pairs={{0,128},{64,192},{128,256},{192,320},{256,384},{320,448},{384,0},{... | collective-permute-start | bytes 1769480 | tf_op jit(solution)/shard_map/ppermute | solution.py:501
  91.9 17.4 %collective-permute-start.9 = (bf16[128,2304]{1,0:T(8,128)(2,1)S(1)}, bf16[128,2304]{1,0:T(8,128)(2,1)}, u32[]{:S(2)}, u32[]{:S(2)}) collective-permute-start(bf16[128,2304]{1,0:T(8,128)(2,1)S(1)} %copy-done.16), channel_id=1, source_target_pairs={{0,384},{64,448},{128,0},{192,64},{256,128},{320,192},{384,256},{4... | collective-permute-start | bytes 1769480 | tf_op jit(solution)/shard_map/ppermute | solution.py:501
  93.8 17.7 %collective-permute-start.11 = (bf16[128,2304]{1,0:T(8,128)(2,1)S(1)}, bf16[128,2304]{1,0:T(8,128)(2,1)}, u32[]{:S(2)}, u32[]{:S(2)}) collective-permute-start(bf16[128,2304]{1,0:T(8,128)(2,1)S(1)} %copy-done.16), channel_id=1, source_target_pairs={{0,64},{64,0},{128,192},{192,128},{256,320},{320,256},{384,448},{4... | collective-permute-start | bytes 1769480 | tf_op jit(solution)/shard_map/ppermute | solution.py:504
  95.7 15.7 %collective-permute-start.10 = (bf16[128,2304]{1,0:T(8,128)(2,1)S(1)}, bf16[128,2304]{1,0:T(8,128)(2,1)}, u32[]{:S(2)}, u32[]{:S(2)}) collective-permute-start(bf16[128,2304]{1,0:T(8,128)(2,1)S(1)} %copy-done.14), channel_id=1, source_target_pairs={{0,64},{64,0},{128,192},{192,128},{256,320},{320,256},{384,448},{4... | collective-permute-start | bytes 1769480 | tf_op jit(solution)/shard_map/ppermute | solution.py:504
  104.3 7.2 %collective-permute-start.12 = (bf16[128,2304]{1,0:T(8,128)(2,1)}, bf16[128,2304]{1,0:T(8,128)(2,1)S(1)}, u32[]{:S(2)}, u32[]{:S(2)}) collective-permute-start(bf16[128,2304]{1,0:T(8,128)(2,1)} %collective-permute-done.8.refs_8_), channel_id=1, source_target_pairs={{0,64},{64,0},{128,192},{192,128},{256,320},{320,256},{384,448},{4... | collective-permute-start | bytes 1769480 | tf_op jit(solution)/shard_map/ppermute | solution.py:504
  109.2 4.2 %collective-permute-start.13 = (bf16[128,2304]{1,0:T(8,128)(2,1)}, bf16[128,2304]{1,0:T(8,128)(2,1)}, u32[]{:S(2)}, u32[]{:S(2)}) collective-permute-start(bf16[128,2304]{1,0:T(8,128)(2,1)} %collective-permute-done.9.refs_9_), channel_id=1, source_target_pairs={{0,64},{64,0},{128,192},{192,128},{256,320},{320,256},{384,448},{4... | collective-permute-start | bytes 1769480 | tf_op jit(solution)/shard_map/ppermute | solution.py:504
  138.5 47.5 %copy-start = (bf16[1,128,2048]{2,1,0:T(8,128)(2,1)S(1)}, bf16[1,128,2048]{2,1,0:T(8,128)(2,1)}, u32[]{:S(2)}) copy-start(bf16[1,128,2048]{2,1,0:T(8,128)(2,1)} %param.15) | copy-start | bytes 1572868
  138.5 47.5 %copy-start.3 = (bf16[128,2048]{1,0:T(8,128)(2,1)S(1)}, bf16[128,2048]{1,0:T(8,128)(2,1)}, u32[]{:S(2)}) copy-start(bf16[128,2048]{1,0:T(8,128)(2,1)} %get-tuple-element.44.token_ref) | copy-start | bytes 1572868
  138.5 47.5 %copy-start.4 = (bf16[2048]{0:T(1024)(128)(2,1)S(1)}, bf16[2048]{0:T(1024)(128)(2,1)}, u32[]{:S(2)}) copy-start(bf16[2048]{0:T(1024)(128)(2,1)} %param.16) | copy-start | bytes 12292
  138.5 47.5 %copy-start.6 = (s32[1,128,2]{1,2,0:T(2,128)S(1)}, s32[1,128,2]{1,2,0:T(2,128)}, u32[]{:S(2)}) copy-start(s32[1,128,2]{1,2,0:T(2,128)} %param.18) | copy-start | bytes 3076
  (12 other events, 100.6 us)
